TPU v7x, 512 devices: a whole 4x4x16 slice. The times are simulated.
512 devices in a mesh: row: 16 (over x_lo, y, core), col: 32 (over x_hi, z).
Axes of the slice: x: 4 (x_hi: 2, x_lo: 2; x = x_hi * 2 + x_lo), y: 4, z: 16, core: 2. Of those that a mesh axis runs over, the one named last changes fastest.
Arguments:
- trailing: bfloat16 [16384, 16384], P('row', 'col'), may hold values from -6 to 6
- left_outer: bfloat16 [1536, 16384], P('col', 'row'), may hold values from -0.625 to 0.625
- left_inner: bfloat16 [1536, 16384], P('col', 'row'), may hold values from -0.1875 to 0.1875
- upper_outer: bfloat16 [1536, 16384], P('row', 'col'), may hold values from -6 to 6
- upper_inner: bfloat16 [1536, 16384], P('row', 'col'), may hold values from -0.15625 to 0.15625
- left_ranks: int32 [16, 16], replicated, may hold values from 16 to 96
- upper_ranks: int32 [16, 16], replicated, may hold values from 16 to 96
Outputs:
- updated: bfloat16 [16384, 16384], P('row', 'col')
- next_panel: bfloat16 [16384, 1024], P(('row', 'col'))
All inputs are finite; a program needn't handle non-finite values.
Results may differ from a plain program's by a relative error of at most 0.0042.
Values may be sent and summed in bfloat16 or wider, within the bound.
No kernel may reach another device: no remote copies, remote signals or barrier semaphores. Data moves between devices by JAX's collectives and lax.ppermute only.
A program may use at most 64 MiB of HBM per device.

v0:
```python
import jax
import jax.numpy as jnp
from jax import lax
from jax.sharding import PartitionSpec as P

R = 96


def partner_2(block, axis, stride):
    count = lax.axis_size(axis)
    route = []
    for low in range(count):
        high = low | 1 << stride
        if high != low and high < count:
            route += [(low, high), (high, low)]
    return lax.ppermute(block, axis, route)


def passed_along(value, axis, steps):
    count = lax.axis_size(axis)
    pairs = [(source, (source + steps) % count) for source in range(count)]
    return lax.ppermute(value, axis, pairs)


def from_root(block, axis, source):
    block = jnp.where(lax.axis_index(axis) == source, block, jnp.zeros_like(block))
    return lax.psum(block, axis)


def body(trailing, left_outer, left_inner, upper_outer, upper_inner, left_ranks, upper_ranks):
    half_rank = R // 2
    row_at = lax.axis_index("row")
    col_at = lax.axis_index("col")
    column_count = lax.axis_size("col")
    tile_count = lax.axis_size("row")
    own_tile = col_at // 2
    partner = partner_2(upper_outer, "col", 0)
    even_side = col_at % 2 == 0
    lower_half = jnp.where(even_side, upper_outer, partner)
    top_half_block = jnp.where(even_side, partner, upper_outer)
    top_rows = jnp.concatenate([lower_half, top_half_block], axis=1)
    all_rows, every_column = (
        lax.all_gather(top_rows, "row", axis=0, tiled=True),
        lax.all_gather(upper_inner, "row", axis=0, tiled=True),
    )
    rank_index = jnp.arange(R, dtype=jnp.int32)
    col_ranks = lax.dynamic_index_in_dim(upper_ranks, own_tile, 1, keepdims=False)
    upper_live = rank_index[None, :] < col_ranks[:, None]
    row_ranks = lax.dynamic_index_in_dim(left_ranks, row_at, 0, keepdims=False)

    def contribute(buffer, outer_rows, interior_rows, first_row):
        row_count = outer_rows.shape[0]
        panel_at = first_row // R
        offset = first_row % R
        rank_here = lax.dynamic_index_in_dim(row_ranks, panel_at, 0, keepdims=False)
        upper_tile = lax.dynamic_slice_in_dim(all_rows, panel_at * R, R, 0)
        central_block = lax.dot_general(
            interior_rows, upper_tile, (((1,), (1,)), ((), ())), preferred_element_type=jnp.float32
        )
        live_rows = offset + jnp.arange(row_count, dtype=jnp.int32) < rank_here
        active_columns = lax.dynamic_index_in_dim(upper_live, panel_at, 0, keepdims=False)
        central_block = jnp.where(
            live_rows[:, None] & active_columns[None, :], central_block, 0.0
        ).astype(jnp.bfloat16)
        partial_value = lax.dot_general(
            outer_rows, central_block, (((0,), (0,)), ((), ())), preferred_element_type=jnp.float32
        )
        rank_slot = lax.dynamic_slice_in_dim(buffer, panel_at * R, R, 1)
        return lax.dynamic_update_slice_in_dim(buffer, rank_slot + partial_value, panel_at * R, 1)

    stacked = jnp.stack([left_outer, left_inner])
    buffer = jnp.zeros((trailing.shape[0], tile_count * R), jnp.float32)

    def advance(shift_step, carried_state):
        carried, block_parts = carried_state
        held_piece = (col_at - shift_step) % column_count
        carried = contribute(carried, block_parts[0], block_parts[1], held_piece * half_rank)
        block_parts = passed_along(block_parts, "col", 1)
        return (carried, block_parts)

    buffer, block_parts = lax.fori_loop(0, column_count - 1, advance, (buffer, stacked))
    held_piece = (col_at - (column_count - 1)) % column_count
    buffer = contribute(buffer, block_parts[0], block_parts[1], held_piece * half_rank)
    outer_sum = buffer.astype(jnp.bfloat16)
    product = jnp.dot(outer_sum, every_column, preferred_element_type=jnp.float32)
    updated = (trailing.astype(jnp.float32) - product).astype(jnp.bfloat16)
    received = []
    for which_half in range(2):
        received.append(from_root(updated, "col", which_half))
    whole_panel = jnp.concatenate(received, axis=1)
    share_rows = whole_panel.shape[0] // column_count
    next_panel = lax.dynamic_slice_in_dim(whole_panel, col_at * share_rows, share_rows, 0)
    return (updated, next_panel)


def solution(mesh):
    in_specs = (
        P("row", "col"),
        P("col", "row"),
        P("col", "row"),
        P("row", "col"),
        P("row", "col"),
        P(),
        P(),
    )
    out_specs = (P("row", "col"), P(("row", "col"), None))
    return jax.shard_map(body, mesh=mesh, in_specs=in_specs, out_specs=out_specs, check_vma=False)
```

profile of v0, /device:TPU:16, one launch (start us, length us, event | category | flops | bytes accessed | tf_op | source)
XLA Modules:
  0.0 740.8 jit_solution(10234027065098967471)
XLA Ops:
  20.5 42.1 %all-gather.3.cloned.1.call-done = bf16[1536,1024]{1,0:T(8,128)(2,1)} async-done(((bf16[96,1024]{1,0:T(8,128)(2,1)}), bf16[1536,1024]{1,0:T(8,128)(2,1)}) %all-gather.3.cloned.1.call-update) | async-done | bytes 3145744 | tf_op jit(solution)/shard_map/all_gather | solution.py:43
  66.0 360.5 %while.18 = (s32[]{:T(128)}, f32[1024,1536]{0,1:T(8,128)}, bf16[2,48,1024]{2,1,0:T(8,128)(2,1)S(1)}, s32[]{:T(128)}, s32[16]{0:T(128)S(1)}, /*index=5*/pred[16,9...) while((s32[]{:T(128)}, f32[1024,1536]{0,1:T(8,128)}, ...), condition=%wide.region_1.2_spmd, body=%wide.region_0.1_spmd.sunk | while | flops 18986624 | bytes 2361245 | solution.py:81
  73.3 6.2 collective-permute-done
  85.2 6.5 collective-permute-done
  97.2 5.6 collective-permute-done
  119.6 5.6 collective-permute-done
  130.8 5.6 collective-permute-done
  142.0 5.6 collective-permute-done
  153.2 5.6 collective-permute-done
  164.4 6.7 collective-permute-done
  176.7 7.6 %collective-permute-done = bf16[2,48,1024]{2,1,0:T(8,128)(2,1)S(1)} collective-permute-done((bf16[2,48,1024]{2,1,0:T(8,128)(2,1)S(1)}, bf16[2,48,1024]{2,1,0:T(8,128)(2,1)S(1)}, u32[]{:S(2)}, u32[]{:S(2)}) %collective-permute-start) | collective-permute-done | bytes 196640 | tf_op jit(solution)/shard_map/while/body/eval_jaxpr/ppermute | solution.py:22
  189.9 6.7 collective-permute-done
  202.2 5.9 collective-permute-done
  213.7 5.6 collective-permute-done
  224.9 5.6 collective-permute-done
  247.2 5.6 collective-permute-done
  258.4 5.6 collective-permute-done
  269.6 6.1 collective-permute-done
  281.3 7.3 collective-permute-done
  294.2 6.9 collective-permute-done
  306.8 6.1 collective-permute-done
  318.5 5.6 collective-permute-done
  329.7 5.6 collective-permute-done
  340.9 5.6 collective-permute-done
  352.1 5.6 collective-permute-done
  374.5 5.8 collective-permute-done
  385.9 7.0 collective-permute-done
  398.5 5.6 collective-permute-done
  409.7 5.6 collective-permute-done
  420.9 5.6 collective-permute-done
  428.9 6.9 broadcast_select_fusion
  435.8 297.1 %all-reduce.3.cloned.1.call-done = (bf16[1024,512]{1,0:T(8,128)(2,1)}, bf16[1024,512]{1,0:T(8,128)(2,1)}) async-done(((bf16[1024,512]{1,0:T(8,128)(2,1)}, bf16[1024,512]{1,0:T(8,128)(2,1)}), (bf16[1024,512]{1,0:T(8,128)(2,1)}, bf16[1024,512]{1,0:T(8,128)(2,1)})) %all-reduce.3.cloned.1.call-update) | async-done | bytes 2097168 | tf_op jit(solution)/shard_map/psum | solution.py:27
  (214 shorter events, 210.3 us)
Async XLA Ops:
  7.2 55.4 %all-gather.3.cloned.1.call-start = ((), (), s32[]{:S(2)}) async-start(), calls=%async_computation | async-start | bytes 3342336 | tf_op jit(solution)/shard_map/all_gather | solution.py:43
  15.7 413.2 %all-gather.5.cloned.1.call-start = ((), (), s32[]{:S(2)}) async-start(), calls=%async_computation.1 | async-start | bytes 1671168 | tf_op jit(solution)/shard_map/all_gather | solution.py:44
  16.4 716.5 %all-reduce.3.cloned.1.call-start = ((), (), s32[]{:S(2)}) async-start(), calls=%async_computation.2 | async-start | bytes 4194304 | tf_op jit(solution)/shard_map/psum | solution.py:27
  66.1 13.5 %collective-permute-start = (bf16[2,48,1024]{2,1,0:T(8,128)(2,1)S(1)}, bf16[2,48,1024]{2,1,0:T(8,128)(2,1)S(1)}, u32[]{:S(2)}, u32[]{:S(2)}) collective-permute-start(bf16[2,48,1024]{2,1,0:T(8,128)(2,1)S(1)} %copy.15), channel_id=1, source_target_pairs={{0,1},{1,2},{2,3},{3,4},{4,5},{5,6},{6,7},{7,8},{8,9},{9,10},{10,1... | collective-permute-start | bytes 589832 | tf_op jit(solution)/shard_map/while/body/eval_jaxpr/ppermute | solution.py:22
  79.6 12.0 %collective-permute-start = (bf16[2,48,1024]{2,1,0:T(8,128)(2,1)S(1)}, bf16[2,48,1024]{2,1,0:T(8,128)(2,1)S(1)}, u32[]{:S(2)}, u32[]{:S(2)}) collective-permute-start(bf16[2,48,1024]{2,1,0:T(8,128)(2,1)S(1)} %copy.15), channel_id=1, source_target_pairs={{0,1},{1,2},{2,3},{3,4},{4,5},{5,6},{6,7},{7,8},{8,9},{9,10},{10,1... | collective-permute-start | bytes 589832 | tf_op jit(solution)/shard_map/while/body/eval_jaxpr/ppermute | solution.py:22
  91.6 11.2 %collective-permute-start = (bf16[2,48,1024]{2,1,0:T(8,128)(2,1)S(1)}, bf16[2,48,1024]{2,1,0:T(8,128)(2,1)S(1)}, u32[]{:S(2)}, u32[]{:S(2)}) collective-permute-start(bf16[2,48,1024]{2,1,0:T(8,128)(2,1)S(1)} %copy.15), channel_id=1, source_target_pairs={{0,1},{1,2},{2,3},{3,4},{4,5},{5,6},{6,7},{7,8},{8,9},{9,10},{10,1... | collective-permute-start | bytes 589832 | tf_op jit(solution)/shard_map/while/body/eval_jaxpr/ppermute | solution.py:22
  102.8 11.2 %collective-permute-start = (bf16[2,48,1024]{2,1,0:T(8,128)(2,1)S(1)}, bf16[2,48,1024]{2,1,0:T(8,128)(2,1)S(1)}, u32[]{:S(2)}, u32[]{:S(2)}) collective-permute-start(bf16[2,48,1024]{2,1,0:T(8,128)(2,1)S(1)} %copy.15), channel_id=1, source_target_pairs={{0,1},{1,2},{2,3},{3,4},{4,5},{5,6},{6,7},{7,8},{8,9},{9,10},{10,1... | collective-permute-start | bytes 589832 | tf_op jit(solution)/shard_map/while/body/eval_jaxpr/ppermute | solution.py:22
  114.0 11.2 %collective-permute-start = (bf16[2,48,1024]{2,1,0:T(8,128)(2,1)S(1)}, bf16[2,48,1024]{2,1,0:T(8,128)(2,1)S(1)}, u32[]{:S(2)}, u32[]{:S(2)}) collective-permute-start(bf16[2,48,1024]{2,1,0:T(8,128)(2,1)S(1)} %copy.15), channel_id=1, source_target_pairs={{0,1},{1,2},{2,3},{3,4},{4,5},{5,6},{6,7},{7,8},{8,9},{9,10},{10,1... | collective-permute-start | bytes 589832 | tf_op jit(solution)/shard_map/while/body/eval_jaxpr/ppermute | solution.py:22
  125.2 11.2 %collective-permute-start = (bf16[2,48,1024]{2,1,0:T(8,128)(2,1)S(1)}, bf16[2,48,1024]{2,1,0:T(8,128)(2,1)S(1)}, u32[]{:S(2)}, u32[]{:S(2)}) collective-permute-start(bf16[2,48,1024]{2,1,0:T(8,128)(2,1)S(1)} %copy.15), channel_id=1, source_target_pairs={{0,1},{1,2},{2,3},{3,4},{4,5},{5,6},{6,7},{7,8},{8,9},{9,10},{10,1... | collective-permute-start | bytes 589832 | tf_op jit(solution)/shard_map/while/body/eval_jaxpr/ppermute | solution.py:22
  136.4 11.2 %collective-permute-start = (bf16[2,48,1024]{2,1,0:T(8,128)(2,1)S(1)}, bf16[2,48,1024]{2,1,0:T(8,128)(2,1)S(1)}, u32[]{:S(2)}, u32[]{:S(2)}) collective-permute-start(bf16[2,48,1024]{2,1,0:T(8,128)(2,1)S(1)} %copy.15), channel_id=1, source_target_pairs={{0,1},{1,2},{2,3},{3,4},{4,5},{5,6},{6,7},{7,8},{8,9},{9,10},{10,1... | collective-permute-start | bytes 589832 | tf_op jit(solution)/shard_map/while/body/eval_jaxpr/ppermute | solution.py:22
  147.6 11.2 %collective-permute-start = (bf16[2,48,1024]{2,1,0:T(8,128)(2,1)S(1)}, bf16[2,48,1024]{2,1,0:T(8,128)(2,1)S(1)}, u32[]{:S(2)}, u32[]{:S(2)}) collective-permute-start(bf16[2,48,1024]{2,1,0:T(8,128)(2,1)S(1)} %copy.15), channel_id=1, source_target_pairs={{0,1},{1,2},{2,3},{3,4},{4,5},{5,6},{6,7},{7,8},{8,9},{9,10},{10,1... | collective-permute-start | bytes 589832 | tf_op jit(solution)/shard_map/while/body/eval_jaxpr/ppermute | solution.py:22
  158.8 12.3 %collective-permute-start = (bf16[2,48,1024]{2,1,0:T(8,128)(2,1)S(1)}, bf16[2,48,1024]{2,1,0:T(8,128)(2,1)S(1)}, u32[]{:S(2)}, u32[]{:S(2)}) collective-permute-start(bf16[2,48,1024]{2,1,0:T(8,128)(2,1)S(1)} %copy.15), channel_id=1, source_target_pairs={{0,1},{1,2},{2,3},{3,4},{4,5},{5,6},{6,7},{7,8},{8,9},{9,10},{10,1... | collective-permute-start | bytes 589832 | tf_op jit(solution)/shard_map/while/body/eval_jaxpr/ppermute | solution.py:22
  171.1 13.2 %collective-permute-start = (bf16[2,48,1024]{2,1,0:T(8,128)(2,1)S(1)}, bf16[2,48,1024]{2,1,0:T(8,128)(2,1)S(1)}, u32[]{:S(2)}, u32[]{:S(2)}) collective-permute-start(bf16[2,48,1024]{2,1,0:T(8,128)(2,1)S(1)} %copy.15), channel_id=1, source_target_pairs={{0,1},{1,2},{2,3},{3,4},{4,5},{5,6},{6,7},{7,8},{8,9},{9,10},{10,1... | collective-permute-start | bytes 589832 | tf_op jit(solution)/shard_map/while/body/eval_jaxpr/ppermute | solution.py:22
  184.3 12.3 %collective-permute-start = (bf16[2,48,1024]{2,1,0:T(8,128)(2,1)S(1)}, bf16[2,48,1024]{2,1,0:T(8,128)(2,1)S(1)}, u32[]{:S(2)}, u32[]{:S(2)}) collective-permute-start(bf16[2,48,1024]{2,1,0:T(8,128)(2,1)S(1)} %copy.15), channel_id=1, source_target_pairs={{0,1},{1,2},{2,3},{3,4},{4,5},{5,6},{6,7},{7,8},{8,9},{9,10},{10,1... | collective-permute-start | bytes 589832 | tf_op jit(solution)/shard_map/while/body/eval_jaxpr/ppermute | solution.py:22
  196.6 11.5 %collective-permute-start = (bf16[2,48,1024]{2,1,0:T(8,128)(2,1)S(1)}, bf16[2,48,1024]{2,1,0:T(8,128)(2,1)S(1)}, u32[]{:S(2)}, u32[]{:S(2)}) collective-permute-start(bf16[2,48,1024]{2,1,0:T(8,128)(2,1)S(1)} %copy.15), channel_id=1, source_target_pairs={{0,1},{1,2},{2,3},{3,4},{4,5},{5,6},{6,7},{7,8},{8,9},{9,10},{10,1... | collective-permute-start | bytes 589832 | tf_op jit(solution)/shard_map/while/body/eval_jaxpr/ppermute | solution.py:22
  208.1 11.2 %collective-permute-start = (bf16[2,48,1024]{2,1,0:T(8,128)(2,1)S(1)}, bf16[2,48,1024]{2,1,0:T(8,128)(2,1)S(1)}, u32[]{:S(2)}, u32[]{:S(2)}) collective-permute-start(bf16[2,48,1024]{2,1,0:T(8,128)(2,1)S(1)} %copy.15), channel_id=1, source_target_pairs={{0,1},{1,2},{2,3},{3,4},{4,5},{5,6},{6,7},{7,8},{8,9},{9,10},{10,1... | collective-permute-start | bytes 589832 | tf_op jit(solution)/shard_map/while/body/eval_jaxpr/ppermute | solution.py:22
  219.3 11.2 %collective-permute-start = (bf16[2,48,1024]{2,1,0:T(8,128)(2,1)S(1)}, bf16[2,48,1024]{2,1,0:T(8,128)(2,1)S(1)}, u32[]{:S(2)}, u32[]{:S(2)}) collective-permute-start(bf16[2,48,1024]{2,1,0:T(8,128)(2,1)S(1)} %copy.15), channel_id=1, source_target_pairs={{0,1},{1,2},{2,3},{3,4},{4,5},{5,6},{6,7},{7,8},{8,9},{9,10},{10,1... | collective-permute-start | bytes 589832 | tf_op jit(solution)/shard_map/while/body/eval_jaxpr/ppermute | solution.py:22
  230.5 11.2 %collective-permute-start = (bf16[2,48,1024]{2,1,0:T(8,128)(2,1)S(1)}, bf16[2,48,1024]{2,1,0:T(8,128)(2,1)S(1)}, u32[]{:S(2)}, u32[]{:S(2)}) collective-permute-start(bf16[2,48,1024]{2,1,0:T(8,128)(2,1)S(1)} %copy.15), channel_id=1, source_target_pairs={{0,1},{1,2},{2,3},{3,4},{4,5},{5,6},{6,7},{7,8},{8,9},{9,10},{10,1... | collective-permute-start | bytes 589832 | tf_op jit(solution)/shard_map/while/body/eval_jaxpr/ppermute | solution.py:22
  241.6 11.2 %collective-permute-start = (bf16[2,48,1024]{2,1,0:T(8,128)(2,1)S(1)}, bf16[2,48,1024]{2,1,0:T(8,128)(2,1)S(1)}, u32[]{:S(2)}, u32[]{:S(2)}) collective-permute-start(bf16[2,48,1024]{2,1,0:T(8,128)(2,1)S(1)} %copy.15), channel_id=1, source_target_pairs={{0,1},{1,2},{2,3},{3,4},{4,5},{5,6},{6,7},{7,8},{8,9},{9,10},{10,1... | collective-permute-start | bytes 589832 | tf_op jit(solution)/shard_map/while/body/eval_jaxpr/ppermute | solution.py:22
  252.8 11.2 %collective-permute-start = (bf16[2,48,1024]{2,1,0:T(8,128)(2,1)S(1)}, bf16[2,48,1024]{2,1,0:T(8,128)(2,1)S(1)}, u32[]{:S(2)}, u32[]{:S(2)}) collective-permute-start(bf16[2,48,1024]{2,1,0:T(8,128)(2,1)S(1)} %copy.15), channel_id=1, source_target_pairs={{0,1},{1,2},{2,3},{3,4},{4,5},{5,6},{6,7},{7,8},{8,9},{9,10},{10,1... | collective-permute-start | bytes 589832 | tf_op jit(solution)/shard_map/while/body/eval_jaxpr/ppermute | solution.py:22
  264.0 11.7 %collective-permute-start = (bf16[2,48,1024]{2,1,0:T(8,128)(2,1)S(1)}, bf16[2,48,1024]{2,1,0:T(8,128)(2,1)S(1)}, u32[]{:S(2)}, u32[]{:S(2)}) collective-permute-start(bf16[2,48,1024]{2,1,0:T(8,128)(2,1)S(1)} %copy.15), channel_id=1, source_target_pairs={{0,1},{1,2},{2,3},{3,4},{4,5},{5,6},{6,7},{7,8},{8,9},{9,10},{10,1... | collective-permute-start | bytes 589832 | tf_op jit(solution)/shard_map/while/body/eval_jaxpr/ppermute | solution.py:22
  275.7 12.9 %collective-permute-start = (bf16[2,48,1024]{2,1,0:T(8,128)(2,1)S(1)}, bf16[2,48,1024]{2,1,0:T(8,128)(2,1)S(1)}, u32[]{:S(2)}, u32[]{:S(2)}) collective-permute-start(bf16[2,48,1024]{2,1,0:T(8,128)(2,1)S(1)} %copy.15), channel_id=1, source_target_pairs={{0,1},{1,2},{2,3},{3,4},{4,5},{5,6},{6,7},{7,8},{8,9},{9,10},{10,1... | collective-permute-start | bytes 589832 | tf_op jit(solution)/shard_map/while/body/eval_jaxpr/ppermute | solution.py:22
  288.6 12.5 %collective-permute-start = (bf16[2,48,1024]{2,1,0:T(8,128)(2,1)S(1)}, bf16[2,48,1024]{2,1,0:T(8,128)(2,1)S(1)}, u32[]{:S(2)}, u32[]{:S(2)}) collective-permute-start(bf16[2,48,1024]{2,1,0:T(8,128)(2,1)S(1)} %copy.15), channel_id=1, source_target_pairs={{0,1},{1,2},{2,3},{3,4},{4,5},{5,6},{6,7},{7,8},{8,9},{9,10},{10,1... | collective-permute-start | bytes 589832 | tf_op jit(solution)/shard_map/while/body/eval_jaxpr/ppermute | solution.py:22
  301.2 11.7 %collective-permute-start = (bf16[2,48,1024]{2,1,0:T(8,128)(2,1)S(1)}, bf16[2,48,1024]{2,1,0:T(8,128)(2,1)S(1)}, u32[]{:S(2)}, u32[]{:S(2)}) collective-permute-start(bf16[2,48,1024]{2,1,0:T(8,128)(2,1)S(1)} %copy.15), channel_id=1, source_target_pairs={{0,1},{1,2},{2,3},{3,4},{4,5},{5,6},{6,7},{7,8},{8,9},{9,10},{10,1... | collective-permute-start | bytes 589832 | tf_op jit(solution)/shard_map/while/body/eval_jaxpr/ppermute | solution.py:22
  312.9 11.2 %collective-permute-start = (bf16[2,48,1024]{2,1,0:T(8,128)(2,1)S(1)}, bf16[2,48,1024]{2,1,0:T(8,128)(2,1)S(1)}, u32[]{:S(2)}, u32[]{:S(2)}) collective-permute-start(bf16[2,48,1024]{2,1,0:T(8,128)(2,1)S(1)} %copy.15), channel_id=1, source_target_pairs={{0,1},{1,2},{2,3},{3,4},{4,5},{5,6},{6,7},{7,8},{8,9},{9,10},{10,1... | collective-permute-start | bytes 589832 | tf_op jit(solution)/shard_map/while/body/eval_jaxpr/ppermute | solution.py:22
  324.1 11.2 %collective-permute-start = (bf16[2,48,1024]{2,1,0:T(8,128)(2,1)S(1)}, bf16[2,48,1024]{2,1,0:T(8,128)(2,1)S(1)}, u32[]{:S(2)}, u32[]{:S(2)}) collective-permute-start(bf16[2,48,1024]{2,1,0:T(8,128)(2,1)S(1)} %copy.15), channel_id=1, source_target_pairs={{0,1},{1,2},{2,3},{3,4},{4,5},{5,6},{6,7},{7,8},{8,9},{9,10},{10,1... | collective-permute-start | bytes 589832 | tf_op jit(solution)/shard_map/while/body/eval_jaxpr/ppermute | solution.py:22
  346.5 11.2 %collective-permute-start = (bf16[2,48,1024]{2,1,0:T(8,128)(2,1)S(1)}, bf16[2,48,1024]{2,1,0:T(8,128)(2,1)S(1)}, u32[]{:S(2)}, u32[]{:S(2)}) collective-permute-start(bf16[2,48,1024]{2,1,0:T(8,128)(2,1)S(1)} %copy.15), channel_id=1, source_target_pairs={{0,1},{1,2},{2,3},{3,4},{4,5},{5,6},{6,7},{7,8},{8,9},{9,10},{10,1... | collective-permute-start | bytes 589832 | tf_op jit(solution)/shard_map/while/body/eval_jaxpr/ppermute | solution.py:22
  357.7 11.2 %collective-permute-start = (bf16[2,48,1024]{2,1,0:T(8,128)(2,1)S(1)}, bf16[2,48,1024]{2,1,0:T(8,128)(2,1)S(1)}, u32[]{:S(2)}, u32[]{:S(2)}) collective-permute-start(bf16[2,48,1024]{2,1,0:T(8,128)(2,1)S(1)} %copy.15), channel_id=1, source_target_pairs={{0,1},{1,2},{2,3},{3,4},{4,5},{5,6},{6,7},{7,8},{8,9},{9,10},{10,1... | collective-permute-start | bytes 589832 | tf_op jit(solution)/shard_map/while/body/eval_jaxpr/ppermute | solution.py:22
  368.9 11.4 %collective-permute-start = (bf16[2,48,1024]{2,1,0:T(8,128)(2,1)S(1)}, bf16[2,48,1024]{2,1,0:T(8,128)(2,1)S(1)}, u32[]{:S(2)}, u32[]{:S(2)}) collective-permute-start(bf16[2,48,1024]{2,1,0:T(8,128)(2,1)S(1)} %copy.15), channel_id=1, source_target_pairs={{0,1},{1,2},{2,3},{3,4},{4,5},{5,6},{6,7},{7,8},{8,9},{9,10},{10,1... | collective-permute-start | bytes 589832 | tf_op jit(solution)/shard_map/while/body/eval_jaxpr/ppermute | solution.py:22
  380.3 12.6 %collective-permute-start = (bf16[2,48,1024]{2,1,0:T(8,128)(2,1)S(1)}, bf16[2,48,1024]{2,1,0:T(8,128)(2,1)S(1)}, u32[]{:S(2)}, u32[]{:S(2)}) collective-permute-start(bf16[2,48,1024]{2,1,0:T(8,128)(2,1)S(1)} %copy.15), channel_id=1, source_target_pairs={{0,1},{1,2},{2,3},{3,4},{4,5},{5,6},{6,7},{7,8},{8,9},{9,10},{10,1... | collective-permute-start | bytes 589832 | tf_op jit(solution)/shard_map/while/body/eval_jaxpr/ppermute | solution.py:22
  404.1 11.2 %collective-permute-start = (bf16[2,48,1024]{2,1,0:T(8,128)(2,1)S(1)}, bf16[2,48,1024]{2,1,0:T(8,128)(2,1)S(1)}, u32[]{:S(2)}, u32[]{:S(2)}) collective-permute-start(bf16[2,48,1024]{2,1,0:T(8,128)(2,1)S(1)} %copy.15), channel_id=1, source_target_pairs={{0,1},{1,2},{2,3},{3,4},{4,5},{5,6},{6,7},{7,8},{8,9},{9,10},{10,1... | collective-permute-start | bytes 589832 | tf_op jit(solution)/shard_map/while/body/eval_jaxpr/ppermute | solution.py:22
  415.3 11.2 %collective-permute-start = (bf16[2,48,1024]{2,1,0:T(8,128)(2,1)S(1)}, bf16[2,48,1024]{2,1,0:T(8,128)(2,1)S(1)}, u32[]{:S(2)}, u32[]{:S(2)}) collective-permute-start(bf16[2,48,1024]{2,1,0:T(8,128)(2,1)S(1)} %copy.15), channel_id=1, source_target_pairs={{0,1},{1,2},{2,3},{3,4},{4,5},{5,6},{6,7},{7,8},{8,9},{9,10},{10,1... | collective-permute-start | bytes 589832 | tf_op jit(solution)/shard_map/while/body/eval_jaxpr/ppermute | solution.py:22
  (5 other events, 401.4 us)
Sparse Core Ops, SparseCore 0:
  15.8 46.7 all-gather.2
  64.7 45.6 all-gather.4
  435.9 296.9 all-reduce.2
where the time goes:
time: 743 us; the launch traced here: 741 us
  waiting for transfers between devices  528 us (71%)
  matrix products  82.2 us (11%)
  starting transfers between devices  65.2 us (9%)
  other arithmetic  24.9 us (3%)
  local copies, waits for them, and re-layouts  24.5 us (3%)
  between operations  13.9 us (2%)
    psum x1, waiting for transfers between devices, from_root(): return lax.psum(block, axis)  297 us
    ppermute x31, waiting for transfers between devices, passed_along(): return lax.ppermute(value, axis, pairs)  185 us
    dot_general x32, matrix products, contribute(): lax.dot_general(outer_rows, central_block, (((0,), (0,)), ((), ())), pref...  75.3 us
    ppermute x31, starting transfers between devices, passed_along(): return lax.ppermute(value, axis, pairs)  61.2 us
    all_gather x1, waiting for transfers between devices, body(): lax.all_gather(top_rows, 'row', axis=0, tiled=True)  42.1 us
    lt x32, other arithmetic, contribute(): live_rows = offset + jnp.arange(row_count, dtype=jnp.int32) < rank_here  20.8 us
    dynamic_slice x32, local copies, waits for them, and re-layouts, contribute(): rank_here = lax.dynamic_index_in_dim(row_ranks, panel_at, 0, keepdims=False)  19.5 us
  transfers between devices with their start and end apart: 35, of which 34 were waited for; matrix products, arithmetic and copies ran while one was open for 16% of the time, Pallas kernels for 0%

commit v1 on v0

v1 whole, which is shorter than its diff:
```python
import jax
import jax.numpy as jnp
from jax import lax
from jax.sharding import Mesh, PartitionSpec as P

R = 96
H = 48
NT = 16
COL = ("xhi", "z")
BF = jnp.bfloat16


def place(branches, default):
    for hit, value in branches:
        default = jnp.where(hit, value, default)
    return default


def spread(updated, col_at):
    sent = []
    for base in (24, 16, 8):
        sent.append(
            (col_at // 8 == base // 8, lax.ppermute(updated[base * 32 : base * 32 + 256], COL, [(0, base), (1, base + 1)]))
        )
    held = place(sent, updated[:256])
    sent = []
    for step in (6, 4, 2):
        pairs = [(b + h, b + step + h) for b in (0, 8, 16, 24) for h in (0, 1)]
        sent.append((col_at % 8 // 2 == step // 2, lax.ppermute(held[step * 32 : step * 32 + 64], COL, pairs)))
    held = place(sent, held[:64])
    odd = col_at % 2 == 1
    kept = jnp.where(odd, held[32:], held[:32])
    given = jnp.where(odd, held[:32], held[32:])
    got = lax.ppermute(given, "z", [(i, i ^ 1) for i in range(16)])
    return jnp.concatenate([jnp.where(odd, got, kept), jnp.where(odd, kept, got)], axis=1)


def body(trailing, left_outer, left_inner, upper_outer, upper_inner, left_ranks, upper_ranks):
    row_at = lax.axis_index("row")
    x_at, z_at = lax.axis_index("xhi"), lax.axis_index("z")
    col_at = x_at * 16 + z_at
    own_tile = col_at // 2

    mine = jnp.stack([left_outer, left_inner])
    other = lax.ppermute(mine, "xhi", [(0, 1), (1, 0)])
    first = x_at == 0
    pair = jnp.stack([jnp.where(first, mine, other), jnp.where(first, other, mine)], axis=1)
    columns = lax.all_gather(pair.reshape(4 * H, -1), "z", axis=0, tiled=True)
    columns = columns.reshape(NT, 2, 2, H, -1)

    partner = lax.ppermute(upper_outer, "z", [(i, i ^ 1) for i in range(16)])
    even = z_at % 2 == 0
    rows = jnp.concatenate(
        [jnp.where(even, upper_outer, partner), jnp.where(even, partner, upper_outer), upper_inner], axis=1
    )
    rows = jnp.broadcast_to(rows[None], (NT,) + rows.shape)
    rows = lax.all_to_all(rows, "row", 0, 0)
    width = trailing.shape[1]
    p_rows = rows[:, :, : 2 * width].reshape(2, 8, R, 2 * width)
    q_rows = rows[:, :, 2 * width :].reshape(2, 8, R, width)

    col_ranks = lax.dynamic_index_in_dim(upper_ranks, own_tile, 1, keepdims=False).reshape(2, 8)
    row_ranks = lax.dynamic_index_in_dim(left_ranks, row_at, 0, keepdims=False).reshape(2, 8)
    rank = jnp.arange(R, dtype=jnp.int32)
    live = (rank.reshape(2, H) < row_ranks[:, :, None, None])[..., None] & (rank < col_ranks[:, :, None])[:, :, None, None, :]

    inner = columns[:, 1].reshape(8, 2, 2, H, -1)
    core = jnp.einsum("zhxrq,xzuq->xzhru", inner, p_rows, preferred_element_type=jnp.float32)
    core = jnp.where(live, core, 0.0).astype(BF)
    weights = jnp.einsum("xzhru,xzup->zhxrp", core, q_rows, preferred_element_type=jnp.float32).astype(BF)
    product = lax.dot_general(
        columns[:, 0].reshape(NT * R, -1),
        weights.reshape(NT * R, width),
        (((0,), (0,)), ((), ())),
        preferred_element_type=jnp.float32,
    )
    updated = (trailing.astype(jnp.float32) - product).astype(BF)
    return updated, spread(updated, col_at)


def solution(mesh):
    fine = Mesh(mesh.devices.reshape(16, 2, 16), ("row", "xhi", "z"))
    grid = P("row", COL)
    turned = P(COL, "row")
    return jax.shard_map(
        body,
        mesh=fine,
        in_specs=(grid, turned, turned, grid, grid, P(), P()),
        out_specs=(grid, P(("row",) + COL, None)),
        check_vma=False,
    )
```

time: 743 us -> 183 us (0.25)
  the two profiles are of different devices: /device:TPU:16 before, /device:TPU:510 now
where the time goes in v1:
time: 183 us
  waiting for transfers between devices  118 us (64%)
  starting transfers between devices  18.5 us (10%)
  local copies, waits for them, and re-layouts  18.3 us (10%)
  between operations  14.3 us (8%)
  matrix products  7.98 us (4%)
  other arithmetic  5.45 us (3%)
    all_to_all x1, waiting for transfers between devices, body(): rows = lax.all_to_all(rows, 'row', 0, 0)  68.5 us
    ppermute x3, waiting for transfers between devices, spread(): lax.ppermute(held[step * 32:step * 32 + 64], COL, pairs)  35.3 us
    slice x1, local copies, waits for them, and re-layouts, body(): inner = columns[:, 1].reshape(8, 2, 2, H, -1)  6.84 us
    ppermute x1, waiting for transfers between devices, body(): other = lax.ppermute(mine, 'xhi', [(0, 1), (1, 0)])  6.71 us
    all_to_all x1, starting transfers between devices, body(): rows = lax.all_to_all(rows, 'row', 0, 0)  5.61 us
    dot_general x1, matrix products, body(): jnp.einsum('xzhru,xzup->zhxrp', core, q_rows, preferred_element_type=jnp....  4.94 us
    ppermute x1, waiting for transfers between devices, spread(): got = lax.ppermute(given, 'z', [(i, i ^ 1) for i in range(16)])  3.88 us
    ppermute x1, waiting for transfers between devices, body(): partner = lax.ppermute(upper_outer, 'z', [(i, i ^ 1) for i in range(16)])  3.79 us
  transfers between devices with their start and end apart: 11, of which 5 were waited for; matrix products, arithmetic and copies ran while one was open for 6% of the time, Pallas kernels for 0%

profile of v1, /device:TPU:510, one launch (start us, length us, event | category | flops | bytes accessed | tf_op | source)
XLA Modules:
  0.0 182.7 jit_solution(3454837583356629247)
XLA Ops:
  7.2 1.0 pad_maximum_fusion.2
  8.2 3.3 %collective-permute-start = (bf16[2,48,1024]{2,1,0:T(8,128)(2,1)S(1)}, bf16[2,48,1024]{2,1,0:T(8,128)(2,1)S(1)}, u32[]{:S(2)}, u32[]{:S(2)}) collective-permute-start(bf16[2,48,1024]{2,1,0:T(8,128)(2,1)S(1)} %pad_maximum_fusion.2), channel_id=1, source_target_pairs={{0,16},{16,0},{1,17},{17,1},{2,18},{18,2},{3,19},{19,3},{4,20},{20... | collective-permute-start | bytes 589832 | tf_op jit(solution)/shard_map/ppermute | solution.py:45
  11.5 6.7 %collective-permute-done = bf16[2,48,1024]{2,1,0:T(8,128)(2,1)S(1)} collective-permute-done((bf16[2,48,1024]{2,1,0:T(8,128)(2,1)S(1)}, bf16[2,48,1024]{2,1,0:T(8,128)(2,1)S(1)}, u32[]{:S(2)}, u32[]{:S(2)}) %collective-permute-start) | collective-permute-done | bytes 196640 | tf_op jit(solution)/shard_map/ppermute | solution.py:45
  18.2 1.0 select_bitcast_fusion.1
  19.2 0.8 pad_maximum_fusion
  20.0 2.9 %collective-permute-start.1 = (bf16[96,512]{1,0:T(8,128)(2,1)}, bf16[96,512]{1,0:T(8,128)(2,1)S(1)}, u32[]{:S(2)}, u32[]{:S(2)}) collective-permute-start(bf16[96,512]{1,0:T(8,128)(2,1)} %param.10), channel_id=1, source_target_pairs={{0,1},{1,0},{2,3},{3,2},{4,5},{5,4},{6,7},{7,6},{8,9},{9,8},{10,11... | collective-permute-start | bytes 294920 | tf_op jit(solution)/shard_map/ppermute | solution.py:51
  23.0 3.8 %collective-permute-done.1 = bf16[96,512]{1,0:T(8,128)(2,1)S(1)} collective-permute-done((bf16[96,512]{1,0:T(8,128)(2,1)}, bf16[96,512]{1,0:T(8,128)(2,1)S(1)}, u32[]{:S(2)}, u32[]{:S(2)}) %collective-permute-start.1) | collective-permute-done | bytes 98336 | tf_op jit(solution)/shard_map/ppermute | solution.py:51
  26.8 0.9 broadcast_select_fusion.1
  27.7 0.9 pad_maximum_fusion.1
  28.6 2.7 %broadcast_in_dim.5 = bf16[16,96,1536]{2,1,0:T(8,128)(2,1)} broadcast(bf16[96,1536]{1,0:T(8,128)(2,1)S(1)} %pad_maximum_fusion.1), dimensions={1,2} | broadcast | bytes 5013504 | tf_op jit(solution)/shard_map/broadcast_in_dim | solution.py:56
  31.3 5.6 %all-to-all-start = ((bf16[16,96,1536]{2,1,0:T(8,128)(2,1)}), bf16[16,96,1536]{2,1,0:T(8,128)(2,1)}, u32[]{:S(2)}, u32[]{:S(2)}) async-start(bf16[16,96,1536]{2,1,0:T(8,128)(2,1)} %broadcast_in_dim.5), calls=%async_computation | async-start | bytes 9437184 | tf_op jit(solution)/shard_map/all_to_all | solution.py:57
  36.9 0.2 dynamic-slice_reduce_fusion
  37.2 0.7 dynamic-slice_reduce_fusion.1
  38.2 0.1 broadcast_compare_fusion
  38.3 68.5 %all-to-all-done = bf16[16,96,1536]{2,1,0:T(8,128)(2,1)} async-done(((bf16[16,96,1536]{2,1,0:T(8,128)(2,1)}), bf16[16,96,1536]{2,1,0:T(8,128)(2,1)}, u32[]{:S(2)}, u32[]{:S(2)}) %all-to-all-start) | async-done | bytes 4718624 | tf_op jit(solution)/shard_map/all_to_all | solution.py:57
  106.7 2.7 %slice.59 = bf16[16,96,512]{2,1,0:T(8,128)(2,1)} slice(bf16[16,96,1536]{2,1,0:T(8,128)(2,1)} %all-to-all-done), slice={[0:16], [0:96], [1024:1536]} | slice | bytes 3145728 | tf_op jit(solution)/shard_map/slice | solution.py:60
  109.5 2.4 %slice.61 = bf16[16,96,1024]{2,1,0:T(8,128)(2,1)S(1)} slice(bf16[16,96,1536]{2,1,0:T(8,128)(2,1)} %all-to-all-done), slice={[0:16], [0:96], [0:1024]} | slice | bytes 6291456 | tf_op jit(solution)/shard_map/slice | solution.py:59
  111.9 6.8 %fusion.30 = (bf16[16,1,2,48,1024]{4,3,2,1,0:T(8,128)(2,1)}, bf16[16,1,2,48,1024]{4,3,2,1,0:T(8,128)(2,1)}) fusion(bf16[16,2,2,48,1024]{4,3,2,1,0:T(8,128)(2,1)} %bitcast.31), kind=kLoop, calls=%fused_computation.37 | loop fusion | bytes 12582912 | tf_op jit(solution)/shard_map/slice | solution.py:67
  118.7 4.9 %fusion.4 = bf16[8,2,2,48,512]{4,3,1,2,0:T(8,128)(2,1)} fusion(bf16[2,8,96,512,1]{3,2,1,0,4:T(8,128)(2,1)} %bitcast.35, bf16[2,8,96,1024,1]{3,2,1,0,4:T(8,128)(2,1)S(1)} %bitcast.32, pred[2,8,96]{2,0,1:T(4,128)(4,1)S(1)} %iota_compare_fusion, pred[2,8,2,48]{3,2,0,1:T(4,128)(4,1)S(1)} %broadcast_compare_fusion, bf16[8,2,2,48,1024]{4,3,2,1,0:T(8,128)(2,1)} %bitcast.34), kind=kOutput, calls=%fused_computation.6 | convolution fusion | flops 454213632 | bytes 9440256 | tf_op jit(solution)/shard_map/xzhru,xzup->zhxrp/dot_general | solution.py:70
  123.6 1.7 copy.15
  125.4 0.7 copy-done.1
  126.0 3.0 %subtract_convert_fusion = bf16[1024,512]{1,0:T(8,128)(2,1)S(1)} fusion(bf16[1024,512]{1,0:T(8,128)(2,1)} %param.7, bf16[1536,1024]{1,0:T(8,128)(2,1)S(1)} %bitcast.33, bf16[1536,512]{1,0:T(8,128)(2,1)S(1)} %bitcast.36), kind=kOutput, calls=%fused_computation.3 | convolution fusion | flops 1612185600 | bytes 6815744 | tf_op jit(solution)/shard_map/dot_general | solution.py:71
  129.1 0.7 collective-permute-start.2
  129.8 0.7 collective-permute-start.3
  130.5 0.7 collective-permute-start.4
  131.3 0.7 collective-permute-start.5
  132.0 0.7 collective-permute-start.6
  132.7 1.3 collective-permute-start.7
  134.0 35.3 %collective-permute-done.7 = bf16[64,512]{1,0:T(8,128)(2,1)S(1)} collective-permute-done((bf16[64,512]{1,0:T(8,128)(2,1)S(1)}, bf16[64,512]{1,0:T(8,128)(2,1)S(1)}, u32[]{:S(2)}, u32[]{:S(2)}) %collective-permute-start.7) | collective-permute-done | bytes 65568 | tf_op jit(solution)/shard_map/ppermute | solution.py:29
  169.4 1.9 %collective-permute-start.8 = (bf16[32,512]{1,0:T(8,128)(2,1)S(1)}, bf16[32,512]{1,0:T(8,128)(2,1)S(1)}, u32[]{:S(2)}, u32[]{:S(2)}) collective-permute-start(bf16[32,512]{1,0:T(8,128)(2,1)S(1)} %broadcast_select_fusion.5), channel_id=1, source_target_pairs={{0,1},{1,0},{2,3},{3,2},{4,5},{5,4},{6,7},{7,6},{8,9},{9,8},{10,11... | collective-permute-start | bytes 98312 | tf_op jit(solution)/shard_map/ppermute | solution.py:34
  171.3 3.9 %collective-permute-done.8 = bf16[32,512]{1,0:T(8,128)(2,1)S(1)} collective-permute-done((bf16[32,512]{1,0:T(8,128)(2,1)S(1)}, bf16[32,512]{1,0:T(8,128)(2,1)S(1)}, u32[]{:S(2)}, u32[]{:S(2)}) %collective-permute-start.8) | collective-permute-done | bytes 32800 | tf_op jit(solution)/shard_map/ppermute | solution.py:34
  175.2 0.6 pad_maximum_fusion.3
  (25 shorter events, 0.7 us)
Async XLA Ops:
  7.2 29.7 %copy-start = (s32[16,16]{1,0:T(8,128)S(1)}, s32[16,16]{1,0:T(8,128)}, u32[]{:S(2)}) copy-start(s32[16,16]{1,0:T(8,128)} %param.13) | copy-start | bytes 3076
  7.2 104.7 %all-gather.2.cloned.1.call-start = ((), (), s32[]{:S(2)}) async-start(), calls=%async_computation.1 | async-start | bytes 6684672 | tf_op jit(solution)/shard_map/all_gather | solution.py:48
  8.2 10.0 %collective-permute-start = (bf16[2,48,1024]{2,1,0:T(8,128)(2,1)S(1)}, bf16[2,48,1024]{2,1,0:T(8,128)(2,1)S(1)}, u32[]{:S(2)}, u32[]{:S(2)}) collective-permute-start(bf16[2,48,1024]{2,1,0:T(8,128)(2,1)S(1)} %pad_maximum_fusion.2), channel_id=1, source_target_pairs={{0,16},{16,0},{1,17},{17,1},{2,18},{18,2},{3,19},{19,3},{4,20},{20... | collective-permute-start | bytes 589832 | tf_op jit(solution)/shard_map/ppermute | solution.py:45
  20.0 6.7 %collective-permute-start.1 = (bf16[96,512]{1,0:T(8,128)(2,1)}, bf16[96,512]{1,0:T(8,128)(2,1)S(1)}, u32[]{:S(2)}, u32[]{:S(2)}) collective-permute-start(bf16[96,512]{1,0:T(8,128)(2,1)} %param.10), channel_id=1, source_target_pairs={{0,1},{1,0},{2,3},{3,2},{4,5},{5,4},{6,7},{7,6},{8,9},{9,8},{10,11... | collective-permute-start | bytes 294920 | tf_op jit(solution)/shard_map/ppermute | solution.py:51
  31.3 75.5 %all-to-all-start = ((bf16[16,96,1536]{2,1,0:T(8,128)(2,1)}), bf16[16,96,1536]{2,1,0:T(8,128)(2,1)}, u32[]{:S(2)}, u32[]{:S(2)}) async-start(bf16[16,96,1536]{2,1,0:T(8,128)(2,1)} %broadcast_in_dim.5), calls=%async_computation | async-start | bytes 9437184 | tf_op jit(solution)/shard_map/all_to_all | solution.py:57
  123.6 2.4 %copy-start.1 = (bf16[16,1,2,48,1024]{4,3,2,1,0:T(8,128)(2,1)S(1)}, bf16[16,1,2,48,1024]{4,3,2,1,0:T(8,128)(2,1)}, u32[]{:S(2)}) copy-start(bf16[16,1,2,48,1024]{4,3,2,1,0:T(8,128)(2,1)} %get-tuple-element.3) | copy-start | bytes 9437188
  129.1 46.8 %copy-start.2 = (bf16[1024,512]{1,0:T(8,128)(2,1)}, bf16[1024,512]{1,0:T(8,128)(2,1)S(1)}, u32[]{:S(2)}) copy-start(bf16[1024,512]{1,0:T(8,128)(2,1)S(1)} %subtract_convert_fusion) | copy-start | bytes 3145732
  129.1 2.1 %collective-permute-start.2 = (bf16[256,512]{1,0:T(8,128)(2,1)S(1)}, bf16[256,512]{1,0:T(8,128)(2,1)S(1)}, u32[]{:S(2)}, u32[]{:S(2)}) collective-permute-start(bf16[256,512]{1,0:T(8,128)(2,1)S(1)} %get-tuple-element.6), channel_id=1, source_target_pairs={{0,8},{1,9},{32,40},{33,41},{64,72},{65,73},{96,104},{97,105},{128... | collective-permute-start | bytes 786440 | tf_op jit(solution)/shard_map/ppermute | solution.py:23
  129.8 1.4 collective-permute-start.3
  130.5 0.7 collective-permute-start.4
  131.3 2.7 %collective-permute-start.5 = (bf16[64,512]{1,0:T(8,128)(2,1)S(1)}, bf16[64,512]{1,0:T(8,128)(2,1)S(1)}, u32[]{:S(2)}, u32[]{:S(2)}) collective-permute-start(bf16[64,512]{1,0:T(8,128)(2,1)S(1)} %get-tuple-element.11), channel_id=1, source_target_pairs={{0,2},{1,3},{8,10},{9,11},{16,18},{17,19},{24,26},{25,27},{32,34},... | collective-permute-start | bytes 196616 | tf_op jit(solution)/shard_map/ppermute | solution.py:29
  132.0 2.0 %collective-permute-start.6 = (bf16[64,512]{1,0:T(8,128)(2,1)S(1)}, bf16[64,512]{1,0:T(8,128)(2,1)S(1)}, u32[]{:S(2)}, u32[]{:S(2)}) collective-permute-start(bf16[64,512]{1,0:T(8,128)(2,1)S(1)} %get-tuple-element.10), channel_id=1, source_target_pairs={{0,4},{1,5},{8,12},{9,13},{16,20},{17,21},{24,28},{25,29},{32,36},... | collective-permute-start | bytes 196616 | tf_op jit(solution)/shard_map/ppermute | solution.py:29
  132.7 36.7 %collective-permute-start.7 = (bf16[64,512]{1,0:T(8,128)(2,1)S(1)}, bf16[64,512]{1,0:T(8,128)(2,1)S(1)}, u32[]{:S(2)}, u32[]{:S(2)}) collective-permute-start(bf16[64,512]{1,0:T(8,128)(2,1)S(1)} %get-tuple-element.9), channel_id=1, source_target_pairs={{0,6},{1,7},{8,14},{9,15},{16,22},{17,23},{24,30},{25,31},{32,38},... | collective-permute-start | bytes 196616 | tf_op jit(solution)/shard_map/ppermute | solution.py:29
  169.4 5.8 %collective-permute-start.8 = (bf16[32,512]{1,0:T(8,128)(2,1)S(1)}, bf16[32,512]{1,0:T(8,128)(2,1)S(1)}, u32[]{:S(2)}, u32[]{:S(2)}) collective-permute-start(bf16[32,512]{1,0:T(8,128)(2,1)S(1)} %broadcast_select_fusion.5), channel_id=1, source_target_pairs={{0,1},{1,0},{2,3},{3,2},{4,5},{5,4},{6,7},{7,6},{8,9},{9,8},{10,11... | collective-permute-start | bytes 98312 | tf_op jit(solution)/shard_map/ppermute | solution.py:34
Sparse Core Ops, SparseCore 0:
  20.1 83.1 all-gather.1

commit v2 on v1

v2 whole, which is shorter than its diff:
```python
import jax
import jax.numpy as jnp
from jax import lax
from jax.sharding import Mesh, PartitionSpec as P

NT = 16
COL = ("xhi", "z")
TURNED_COL = ("z", "xhi")
BF = jnp.bfloat16
SWAP_Z = [(i, i ^ 1) for i in range(16)]


def place(branches, default):
    for hit, value in branches:
        default = jnp.where(hit, value, default)
    return default


def spread(updated, col_at):
    share = updated.shape[0] // 32
    part = 4 * share
    sent = []
    for m in range(7, 0, -1):
        block = lax.ppermute(updated[m * part : (m + 1) * part], COL, [(0, 4 * m), (1, 4 * m + 1)])
        sent.append((col_at // 4 == m, block))
    held = place(sent, updated[:part])
    spot = col_at % 4
    got = []
    for d in (1, 2, 3):
        piece = lax.dynamic_slice_in_dim(held, (spot + d) % 4 * share, share, 0)
        pairs = [(b + h, b + (h + d) % 4) for b in range(0, 32, 4) for h in (0, 1)]
        got.append(lax.ppermute(piece, COL, pairs))
    own = lax.dynamic_slice_in_dim(held, spot * share, share, 0)
    left = place([(spot == d, got[d - 1]) for d in (1, 2, 3)], own)
    right = place([((spot - 1) % 4 == d, got[d - 1]) for d in (1, 2, 3)], own)
    return jnp.concatenate([left, right], axis=1)


def turn(block, flip):
    pairs = [
        (k * 32 + 2 * j + h, j * 32 + 2 * k + (h ^ flip)) for k in range(NT) for j in range(NT) for h in (0, 1)
    ]
    return lax.ppermute(block, ("row",) + COL, pairs)


def body(trailing, left_outer, left_inner, upper_outer, upper_inner, left_ranks, upper_ranks):
    row_at = lax.axis_index("row")
    x_at, z_at = lax.axis_index("xhi"), lax.axis_index("z")
    col_at = x_at * 16 + z_at
    pair_at = col_at // 2
    even = z_at % 2 == 0
    width = trailing.shape[1]
    rank_pad, half = upper_outer.shape[0], left_outer.shape[0]

    other = lax.ppermute(left_outer, "xhi", [(0, 1), (1, 0)])
    first = x_at == 0
    outer = jnp.concatenate([jnp.where(first, left_outer, other), jnp.where(first, other, left_outer)], axis=0)
    outer = lax.all_gather(outer, "z", axis=0, tiled=True)

    same, crossed = turn(upper_outer, 0), turn(upper_outer, 1)
    p_block = jnp.concatenate([jnp.where(even, same, crossed), jnp.where(even, crossed, same)], axis=1)
    p_all = lax.all_to_all(jnp.broadcast_to(p_block[None], (NT,) + p_block.shape), "row", 0, 0)
    q_all = lax.all_to_all(jnp.broadcast_to(upper_inner[None], (NT,) + upper_inner.shape), "row", 0, 0)

    core = jnp.einsum("tq,juq->jtu", left_inner, p_all, preferred_element_type=jnp.float32)
    rank = jnp.arange(rank_pad, dtype=jnp.int32)
    t_at = (col_at % 2) * half + jnp.arange(half, dtype=jnp.int32)
    t_live = t_at < lax.dynamic_slice(left_ranks, (row_at, pair_at), (1, 1))[0]
    u_live = rank[None, :] < lax.dynamic_index_in_dim(upper_ranks, pair_at, 0, keepdims=False)[:, None]
    core = jnp.where(t_live[None, :, None] & u_live[:, None, :], core, 0.0).astype(BF)
    core = core.reshape(2, 8, 1, half, rank_pad).transpose(1, 2, 0, 3, 4)
    core = jnp.broadcast_to(core, (8, 2, 2, half, rank_pad)).reshape(32, half, rank_pad)
    core = lax.all_to_all(core, TURNED_COL, 0, 0)

    weights = jnp.einsum(
        "zhxru,xzup->zhxrp",
        core.reshape(8, 2, 2, half, rank_pad),
        q_all.reshape(2, 8, rank_pad, width),
        preferred_element_type=jnp.float32,
    ).astype(BF)
    product = lax.dot_general(
        outer, weights.reshape(NT * rank_pad, width), (((0,), (0,)), ((), ())), preferred_element_type=jnp.float32
    )
    updated = (trailing.astype(jnp.float32) - product).astype(BF)
    return updated, spread(updated, col_at)


def solution(mesh):
    fine = Mesh(mesh.devices.reshape(16, 2, 16), ("row", "xhi", "z"))
    grid = P("row", COL)
    turned = P(COL, "row")
    return jax.shard_map(
        body,
        mesh=fine,
        in_specs=(grid, turned, turned, grid, grid, P(), P()),
        out_specs=(grid, P(("row",) + COL, None)),
        check_vma=False,
    )
```

time: 183 us -> 207 us (1.13)
  the two profiles are of different devices: /device:TPU:510 before, /device:TPU:56 now
where the time goes in v2:
time: 207 us; the launch traced here: 206 us
  blocking collectives  84.7 us (41%)
  waiting for transfers between devices  49.3 us (24%)
  starting transfers between devices  43.4 us (21%)
  between operations  14.5 us (7%)
  matrix products  7.22 us (3%)
  local copies, waits for them, and re-layouts  3.96 us (2%)
  other arithmetic  3.07 us (1%)
    all_to_all x1, blocking collectives, body(): lax.all_to_all(jnp.broadcast_to(p_block[None], (NT,) + p_block.shape), 'r...  43.1 us
    all_to_all x1, blocking collectives, body(): core = lax.all_to_all(core, TURNED_COL, 0, 0)  41.6 us
    all_to_all x1, waiting for transfers between devices, body(): lax.all_to_all(jnp.broadcast_to(upper_inner[None], (NT,) + upper_inner.sh...  18.1 us
    ppermute x2, waiting for transfers between devices, turn(): return lax.ppermute(block, ('row',) + COL, pairs)  17 us
    ppermute x2, starting transfers between devices, turn(): return lax.ppermute(block, ('row',) + COL, pairs)  13.9 us
    ppermute x7, starting transfers between devices, spread(): lax.ppermute(updated[m * part:(m + 1) * part], COL, [(0, 4 * m), (1, 4 *...  13.6 us
    ppermute x7, waiting for transfers between devices, spread(): lax.ppermute(updated[m * part:(m + 1) * part], COL, [(0, 4 * m), (1, 4 *...  10.3 us
    all_to_all x1, starting transfers between devices, body(): lax.all_to_all(jnp.broadcast_to(upper_inner[None], (NT,) + upper_inner.sh...  6.43 us
  transfers between devices with their start and end apart: 15, of which 7 were waited for; matrix products, arithmetic and copies ran while one was open for 5% of the time, Pallas kernels for 0%

profile of v2, /device:TPU:56, one launch (start us, length us, event | category | flops | bytes accessed | tf_op | source)
XLA Modules:
  0.0 206.1 jit_solution(15094508217720052962)
XLA Ops:
  7.2 4.9 %collective-permute-start = (bf16[48,1024]{1,0:T(8,128)(2,1)}, bf16[48,1024]{1,0:T(8,128)(2,1)S(1)}, u32[]{:S(2)}, u32[]{:S(2)}) collective-permute-start(bf16[48,1024]{1,0:T(8,128)(2,1)} %param.8), channel_id=1, source_target_pairs={{0,16},{16,0},{1,17},{17,1},{2,18},{18,2},{3,19},{19,3},{4,20},{20... | collective-permute-start | bytes 294920 | tf_op jit(solution)/shard_map/ppermute | solution.py:55
  12.2 11.5 %collective-permute-start.1 = (bf16[96,512]{1,0:T(8,128)(2,1)}, bf16[96,512]{1,0:T(8,128)(2,1)S(1)}, u32[]{:S(2)}, u32[]{:S(2)}) collective-permute-start(bf16[96,512]{1,0:T(8,128)(2,1)} %param.10), channel_id=1, source_target_pairs={{0,0},{1,1},{2,32},{3,33},{4,64},{5,65},{6,96},{7,97},{8,128},{9,1... | collective-permute-start | bytes 294920 | tf_op jit(solution)/shard_map/ppermute | solution.py:43
  23.7 2.4 %collective-permute-start.2 = (bf16[96,512]{1,0:T(8,128)(2,1)}, bf16[96,512]{1,0:T(8,128)(2,1)S(1)}, u32[]{:S(2)}, u32[]{:S(2)}) collective-permute-start(bf16[96,512]{1,0:T(8,128)(2,1)} %param.10), channel_id=1, source_target_pairs={{0,1},{1,0},{2,33},{3,32},{4,65},{5,64},{6,97},{7,96},{8,129},{9,1... | collective-permute-start | bytes 294920 | tf_op jit(solution)/shard_map/ppermute | solution.py:43
  26.1 0.9 broadcast_select_fusion.3
  27.0 0.7 pad_maximum_fusion
  27.7 15.6 %collective-permute-done.1 = bf16[96,512]{1,0:T(8,128)(2,1)S(1)} collective-permute-done((bf16[96,512]{1,0:T(8,128)(2,1)}, bf16[96,512]{1,0:T(8,128)(2,1)S(1)}, u32[]{:S(2)}, u32[]{:S(2)}) %collective-permute-start.1) | collective-permute-done | bytes 98336 | tf_op jit(solution)/shard_map/ppermute | solution.py:43
  43.3 1.4 collective-permute-done.2
  45.2 43.1 %all_to_all.15 = bf16[16,96,1024]{2,1,0:T(8,128)(2,1)S(1)} all-to-all(bf16[16,96,1024]{2,1,0:T(8,128)(2,1)S(1)} %broadcast_in_dim.11), channel_id=1, replica_groups=mesh['row'=16,'xhi'=2,'z'=16] {'row'}, dimensions={0} | all-to-all | bytes 6291456 | tf_op jit(solution)/shard_map/all_to_all | solution.py:62
  88.2 1.3 broadcast_in_dim.16
  89.6 6.4 %all-to-all-start.2 = ((bf16[16,96,512]{2,1,0:T(8,128)(2,1)}), bf16[16,96,512]{2,1,0:T(8,128)(2,1)}, u32[]{:S(2)}, u32[]{:S(2)}) async-start(bf16[16,96,512]{2,1,0:T(8,128)(2,1)} %broadcast_in_dim.16), calls=%async_computation.2 | async-start | bytes 3145728 | tf_op jit(solution)/shard_map/all_to_all | solution.py:63
  96.0 1.3 dynamic_slice.19
  97.3 0.7 fusion.14
  98.0 0.7 add_compare_fusion
  98.7 1.2 fusion.5
  100.0 18.1 %all-to-all-done.2 = bf16[16,96,512]{2,1,0:T(8,128)(2,1)} async-done(((bf16[16,96,512]{2,1,0:T(8,128)(2,1)}), bf16[16,96,512]{2,1,0:T(8,128)(2,1)}, u32[]{:S(2)}, u32[]{:S(2)}) %all-to-all-start.2) | async-done | bytes 1572896 | tf_op jit(solution)/shard_map/all_to_all | solution.py:63
  118.2 41.6 %all_to_all.16 = bf16[32,48,96]{2,1,0:T(8,128)(2,1)S(1)} all-to-all(bf16[32,48,96]{2,1,0:T(8,128)(2,1)S(1)} %bitcast.30), channel_id=1, replica_groups=mesh['row'=16,'xhi'=2,'z'=16] {'z','xhi'}, dimensions={0} | all-to-all | bytes 589824 | tf_op jit(solution)/shard_map/all_to_all | solution.py:73
  159.8 2.0 fusion.1
  161.9 4.0 %subtract_convert_fusion = bf16[1024,512]{1,0:T(8,128)(2,1)S(1)} fusion(bf16[1024,512]{1,0:T(8,128)(2,1)} %param.7, bf16[1536,1024]{1,0:T(8,128)(2,1)} %all-gather.2.cloned.1.call-done, bf16[1536,512]{1,0:T(8,128)(2,1)S(1)} %bitcast.28), kind=kOutput, calls=%fused_computation | convolution fusion | flops 1612185600 | bytes 6815744 | tf_op jit(solution)/shard_map/dot_general | solution.py:81
  166.0 5.4 %collective-permute-start.3 = (bf16[128,512]{1,0:T(8,128)(2,1)S(1)}, bf16[128,512]{1,0:T(8,128)(2,1)S(1)}, u32[]{:S(2)}, u32[]{:S(2)}) collective-permute-start(bf16[128,512]{1,0:T(8,128)(2,1)S(1)} %get-tuple-element.8), channel_id=1, source_target_pairs={{0,4},{1,5},{32,36},{33,37},{64,68},{65,69},{96,100},{97,101},{128... | collective-permute-start | bytes 393224 | tf_op jit(solution)/shard_map/ppermute | solution.py:24
  171.4 1.8 collective-permute-start.4
  173.2 1.3 collective-permute-start.5
  174.5 1.3 collective-permute-start.6
  175.8 1.3 collective-permute-start.7
  177.1 7.5 %collective-permute-done.3 = bf16[128,512]{1,0:T(8,128)(2,1)S(1)} collective-permute-done((bf16[128,512]{1,0:T(8,128)(2,1)S(1)}, bf16[128,512]{1,0:T(8,128)(2,1)S(1)}, u32[]{:S(2)}, u32[]{:S(2)}) %collective-permute-start.3) | collective-permute-done | bytes 131104 | tf_op jit(solution)/shard_map/ppermute | solution.py:24
  184.7 1.3 collective-permute-start.8
  186.0 1.3 collective-permute-start.9
  187.4 1.1 collective-permute-done.8
  188.5 1.7 collective-permute-done.9
  190.2 1.3 collective-permute-start.10
  191.5 1.3 collective-permute-start.11
  192.8 1.9 collective-permute-start.12
  194.8 3.8 %collective-permute-done.12 = bf16[32,512]{1,0:T(8,128)(2,1)S(1)} collective-permute-done((bf16[32,512]{1,0:T(8,128)(2,1)S(1)}, bf16[32,512]{1,0:T(8,128)(2,1)S(1)}, u32[]{:S(2)}, u32[]{:S(2)}) %collective-permute-start.12) | collective-permute-done | bytes 32800 | tf_op jit(solution)/shard_map/ppermute | solution.py:32
  (28 shorter events, 1.6 us)
Async XLA Ops:
  7.2 91.6 %copy-start = (bf16[48,1024]{1,0:T(8,128)(2,1)S(1)}, bf16[48,1024]{1,0:T(8,128)(2,1)}, u32[]{:S(2)}) copy-start(bf16[48,1024]{1,0:T(8,128)(2,1)} %param.9) | copy-start | bytes 294916
  7.2 154.7 %all-gather.2.cloned.1.call-start = ((), (), s32[]{:S(2)}) async-start(), calls=%async_computation.3 | async-start | bytes 3342336 | tf_op jit(solution)/shard_map/all_gather | solution.py:58
  7.2 18.8 %collective-permute-start = (bf16[48,1024]{1,0:T(8,128)(2,1)}, bf16[48,1024]{1,0:T(8,128)(2,1)S(1)}, u32[]{:S(2)}, u32[]{:S(2)}) collective-permute-start(bf16[48,1024]{1,0:T(8,128)(2,1)} %param.8), channel_id=1, source_target_pairs={{0,16},{16,0},{1,17},{17,1},{2,18},{18,2},{3,19},{19,3},{4,20},{20... | collective-permute-start | bytes 294920 | tf_op jit(solution)/shard_map/ppermute | solution.py:55
  12.2 31.1 %collective-permute-start.1 = (bf16[96,512]{1,0:T(8,128)(2,1)}, bf16[96,512]{1,0:T(8,128)(2,1)S(1)}, u32[]{:S(2)}, u32[]{:S(2)}) collective-permute-start(bf16[96,512]{1,0:T(8,128)(2,1)} %param.10), channel_id=1, source_target_pairs={{0,0},{1,1},{2,32},{3,33},{4,64},{5,65},{6,96},{7,97},{8,128},{9,1... | collective-permute-start | bytes 294920 | tf_op jit(solution)/shard_map/ppermute | solution.py:43
  23.7 21.1 %collective-permute-start.2 = (bf16[96,512]{1,0:T(8,128)(2,1)}, bf16[96,512]{1,0:T(8,128)(2,1)S(1)}, u32[]{:S(2)}, u32[]{:S(2)}) collective-permute-start(bf16[96,512]{1,0:T(8,128)(2,1)} %param.10), channel_id=1, source_target_pairs={{0,1},{1,0},{2,33},{3,32},{4,65},{5,64},{6,97},{7,96},{8,129},{9,1... | collective-permute-start | bytes 294920 | tf_op jit(solution)/shard_map/ppermute | solution.py:43
  45.2 43.1 %copy-start.2 = (bf16[96,512]{1,0:T(8,128)(2,1)S(1)}, bf16[96,512]{1,0:T(8,128)(2,1)}, u32[]{:S(2)}) copy-start(bf16[96,512]{1,0:T(8,128)(2,1)} %param.11) | copy-start | bytes 294916
  89.6 28.5 %all-to-all-start.2 = ((bf16[16,96,512]{2,1,0:T(8,128)(2,1)}), bf16[16,96,512]{2,1,0:T(8,128)(2,1)}, u32[]{:S(2)}, u32[]{:S(2)}) async-start(bf16[16,96,512]{2,1,0:T(8,128)(2,1)} %broadcast_in_dim.16), calls=%async_computation.2 | async-start | bytes 3145728 | tf_op jit(solution)/shard_map/all_to_all | solution.py:63
  165.9 33.3 %copy-start.1 = (bf16[1024,512]{1,0:T(8,128)(2,1)}, bf16[1024,512]{1,0:T(8,128)(2,1)S(1)}, u32[]{:S(2)}) copy-start(bf16[1024,512]{1,0:T(8,128)(2,1)S(1)} %subtract_convert_fusion) | copy-start | bytes 3145732
  166.0 18.6 %collective-permute-start.3 = (bf16[128,512]{1,0:T(8,128)(2,1)S(1)}, bf16[128,512]{1,0:T(8,128)(2,1)S(1)}, u32[]{:S(2)}, u32[]{:S(2)}) collective-permute-start(bf16[128,512]{1,0:T(8,128)(2,1)S(1)} %get-tuple-element.8), channel_id=1, source_target_pairs={{0,4},{1,5},{32,36},{33,37},{64,68},{65,69},{96,100},{97,101},{128... | collective-permute-start | bytes 393224 | tf_op jit(solution)/shard_map/ppermute | solution.py:24
  171.4 14.6 %collective-permute-start.4 = (bf16[128,512]{1,0:T(8,128)(2,1)S(1)}, bf16[128,512]{1,0:T(8,128)(2,1)S(1)}, u32[]{:S(2)}, u32[]{:S(2)}) collective-permute-start(bf16[128,512]{1,0:T(8,128)(2,1)S(1)} %get-tuple-element.7), channel_id=1, source_target_pairs={{0,8},{1,9},{32,40},{33,41},{64,72},{65,73},{96,104},{97,105},{128... | collective-permute-start | bytes 393224 | tf_op jit(solution)/shard_map/ppermute | solution.py:24
  173.2 14.2 %collective-permute-start.5 = (bf16[128,512]{1,0:T(8,128)(2,1)S(1)}, bf16[128,512]{1,0:T(8,128)(2,1)S(1)}, u32[]{:S(2)}, u32[]{:S(2)}) collective-permute-start(bf16[128,512]{1,0:T(8,128)(2,1)S(1)} %get-tuple-element.6), channel_id=1, source_target_pairs={{0,12},{1,13},{32,44},{33,45},{64,76},{65,77},{96,108},{97,109},{1... | collective-permute-start | bytes 393224 | tf_op jit(solution)/shard_map/ppermute | solution.py:24
  174.5 12.9 %collective-permute-start.6 = (bf16[128,512]{1,0:T(8,128)(2,1)S(1)}, bf16[128,512]{1,0:T(8,128)(2,1)S(1)}, u32[]{:S(2)}, u32[]{:S(2)}) collective-permute-start(bf16[128,512]{1,0:T(8,128)(2,1)S(1)} %get-tuple-element.5), channel_id=1, source_target_pairs={{0,16},{1,17},{32,48},{33,49},{64,80},{65,81},{96,112},{97,113},{1... | collective-permute-start | bytes 393224 | tf_op jit(solution)/shard_map/ppermute | solution.py:24
  175.8 11.6 %collective-permute-start.7 = (bf16[128,512]{1,0:T(8,128)(2,1)S(1)}, bf16[128,512]{1,0:T(8,128)(2,1)S(1)}, u32[]{:S(2)}, u32[]{:S(2)}) collective-permute-start(bf16[128,512]{1,0:T(8,128)(2,1)S(1)} %get-tuple-element.4), channel_id=1, source_target_pairs={{0,20},{1,21},{32,52},{33,53},{64,84},{65,85},{96,116},{97,117},{1... | collective-permute-start | bytes 393224 | tf_op jit(solution)/shard_map/ppermute | solution.py:24
  184.7 3.8 %collective-permute-start.8 = (bf16[128,512]{1,0:T(8,128)(2,1)S(1)}, bf16[128,512]{1,0:T(8,128)(2,1)S(1)}, u32[]{:S(2)}, u32[]{:S(2)}) collective-permute-start(bf16[128,512]{1,0:T(8,128)(2,1)S(1)} %get-tuple-element.3), channel_id=1, source_target_pairs={{0,24},{1,25},{32,56},{33,57},{64,88},{65,89},{96,120},{97,121},{1... | collective-permute-start | bytes 393224 | tf_op jit(solution)/shard_map/ppermute | solution.py:24
  186.0 4.2 %collective-permute-start.9 = (bf16[128,512]{1,0:T(8,128)(2,1)S(1)}, bf16[128,512]{1,0:T(8,128)(2,1)S(1)}, u32[]{:S(2)}, u32[]{:S(2)}) collective-permute-start(bf16[128,512]{1,0:T(8,128)(2,1)S(1)} %get-tuple-element.2), channel_id=1, source_target_pairs={{0,28},{1,29},{32,60},{33,61},{64,92},{65,93},{96,124},{97,125},{1... | collective-permute-start | bytes 393224 | tf_op jit(solution)/shard_map/ppermute | solution.py:24
  190.2 4.6 %collective-permute-start.10 = (bf16[32,512]{1,0:T(8,128)(2,1)S(1)}, bf16[32,512]{1,0:T(8,128)(2,1)S(1)}, u32[]{:S(2)}, u32[]{:S(2)}) collective-permute-start(bf16[32,512]{1,0:T(8,128)(2,1)S(1)} %get-tuple-element.17), channel_id=1, source_target_pairs={{0,3},{1,0},{4,7},{5,4},{8,11},{9,8},{12,15},{13,12},{16,19},{17,1... | collective-permute-start | bytes 98312 | tf_op jit(solution)/shard_map/ppermute | solution.py:32
  191.5 3.3 %collective-permute-start.11 = (bf16[32,512]{1,0:T(8,128)(2,1)S(1)}, bf16[32,512]{1,0:T(8,128)(2,1)S(1)}, u32[]{:S(2)}, u32[]{:S(2)}) collective-permute-start(bf16[32,512]{1,0:T(8,128)(2,1)S(1)} %get-tuple-element.16), channel_id=1, source_target_pairs={{0,2},{1,3},{4,6},{5,7},{8,10},{9,11},{12,14},{13,15},{16,18},{17,... | collective-permute-start | bytes 98312 | tf_op jit(solution)/shard_map/ppermute | solution.py:32
  192.8 5.8 %collective-permute-start.12 = (bf16[32,512]{1,0:T(8,128)(2,1)S(1)}, bf16[32,512]{1,0:T(8,128)(2,1)S(1)}, u32[]{:S(2)}, u32[]{:S(2)}) collective-permute-start(bf16[32,512]{1,0:T(8,128)(2,1)S(1)} %get-tuple-element.15), channel_id=1, source_target_pairs={{0,1},{1,2},{4,5},{5,6},{8,9},{9,10},{12,13},{13,14},{16,17},{17,1... | collective-permute-start | bytes 98312 | tf_op jit(solution)/shard_map/ppermute | solution.py:32
Sparse Core Ops, SparseCore 0:
  27.8 78.6 all-gather.1

commit v3 on v2

v3 whole, which is shorter than its diff:
```python
import jax
import jax.numpy as jnp
from jax import lax
from jax.experimental import pallas as pl
from jax.experimental.pallas import tpu as pltpu
from jax.sharding import Mesh, PartitionSpec as P

NT = 16
COL = ("xhi", "z")
BF = jnp.bfloat16
SWAP_Z = [(i, i ^ 1) for i in range(16)]
STEP = 2


def place(branches, default):
    for hit, value in branches:
        default = jnp.where(hit, value, default)
    return default


def spread(updated, col_at):
    share = updated.shape[0] // 32
    part = 4 * share
    sent = []
    for m in range(7, 0, -1):
        block = lax.ppermute(updated[m * part : (m + 1) * part], COL, [(0, 4 * m), (1, 4 * m + 1)])
        sent.append((col_at // 4 == m, block))
    held = place(sent, updated[:part])
    spot = col_at % 4
    got = []
    for d in (1, 2, 3):
        piece = lax.dynamic_slice_in_dim(held, (spot + d) % 4 * share, share, 0)
        pairs = [(b + h, b + (h + d) % 4) for b in range(0, 32, 4) for h in (0, 1)]
        got.append(lax.ppermute(piece, COL, pairs))
    own = lax.dynamic_slice_in_dim(held, spot * share, share, 0)
    left = place([(spot == d, got[d - 1]) for d in (1, 2, 3)], own)
    right = place([((spot - 1) % 4 == d, got[d - 1]) for d in (1, 2, 3)], own)
    return jnp.concatenate([left, right], axis=1)


def update_kernel(x_at_ref, left_ref, upper_ref, cols_ref, rows_ref, trailing_ref, out_ref, acc_ref):
    step = pl.program_id(0)
    rank_pad = rows_ref.shape[2]
    depth = cols_ref.shape[4]
    t = lax.broadcasted_iota(jnp.int32, (rank_pad, rank_pad), 0)
    u = lax.broadcasted_iota(jnp.int32, (rank_pad, rank_pad), 1)
    outers, weights = [], []
    for local in range(STEP):
        for slot in range(2):
            xhi = slot ^ x_at_ref[0]
            k = xhi * 8 + step * STEP + local
            inner = jnp.concatenate([cols_ref[2 * local, slot, 1], cols_ref[2 * local + 1, slot, 1]], axis=0)
            core = lax.dot_general(
                inner,
                rows_ref[xhi, local, :, :depth],
                (((1,), (1,)), ((), ())),
                preferred_element_type=jnp.float32,
            )
            core = jnp.where((t < left_ref[k]) & (u < upper_ref[k]), core, 0.0).astype(BF)
            weights.append(
                jnp.dot(core, rows_ref[xhi, local, :, depth:], preferred_element_type=jnp.float32).astype(BF)
            )
            outers += [cols_ref[2 * local, slot, 0], cols_ref[2 * local + 1, slot, 0]]
    product = lax.dot_general(
        jnp.concatenate(outers, axis=0),
        jnp.concatenate(weights, axis=0),
        (((0,), (0,)), ((), ())),
        preferred_element_type=jnp.float32,
    )

    @pl.when(step == 0)
    def _():
        acc_ref[...] = product

    @pl.when(step > 0)
    def _():
        acc_ref[...] += product

    @pl.when(step == pl.num_programs(0) - 1)
    def _():
        out_ref[...] = (trailing_ref[...].astype(jnp.float32) - acc_ref[...]).astype(BF)


def update(x_at, left, upper, cols, rows, trailing):
    height, width = trailing.shape
    rank_pad, depth = rows.shape[2], cols.shape[4]
    half = cols.shape[3]
    return pl.pallas_call(
        update_kernel,
        out_shape=jax.ShapeDtypeStruct(trailing.shape, BF),
        grid_spec=pltpu.PrefetchScalarGridSpec(
            num_scalar_prefetch=3,
            grid=(8 // STEP,),
            in_specs=[
                pl.BlockSpec((2 * STEP, 2, 2, half, depth), lambda i, *_: (i, 0, 0, 0, 0)),
                pl.BlockSpec((2, STEP, rank_pad, depth + width), lambda i, *_: (0, i, 0, 0)),
                pl.BlockSpec((height, width), lambda i, *_: (0, 0)),
            ],
            out_specs=pl.BlockSpec((height, width), lambda i, *_: (0, 0)),
            scratch_shapes=[pltpu.VMEM((height, width), jnp.float32)],
        ),
        compiler_params=pltpu.CompilerParams(dimension_semantics=("arbitrary",), vmem_limit_bytes=40 << 20),
    )(x_at, left, upper, cols, rows, trailing)


def body(trailing, left_outer, left_inner, upper_outer, upper_inner, left_ranks, upper_ranks):
    row_at = lax.axis_index("row")
    x_at, z_at = lax.axis_index("xhi"), lax.axis_index("z")
    col_at = x_at * 16 + z_at
    half = left_outer.shape[0]

    mine = jnp.concatenate([left_outer, left_inner], axis=0)
    other = lax.ppermute(mine, "xhi", [(0, 1), (1, 0)])
    cols = lax.all_gather(jnp.concatenate([mine, other], axis=0), "z", axis=0, tiled=True)
    cols = cols.reshape(NT, 2, 2, half, -1)

    partner = lax.ppermute(upper_outer, "z", SWAP_Z)
    even = z_at % 2 == 0
    rows = jnp.concatenate(
        [jnp.where(even, upper_outer, partner), jnp.where(even, partner, upper_outer), upper_inner], axis=1
    )
    rows = lax.all_to_all(jnp.broadcast_to(rows[None], (NT,) + rows.shape), "row", 0, 0)
    rows = rows.reshape((2, 8) + rows.shape[1:])

    left = lax.dynamic_index_in_dim(left_ranks, row_at, 0, keepdims=False)
    upper = lax.dynamic_index_in_dim(upper_ranks, col_at // 2, 1, keepdims=False)
    updated = update(x_at.reshape(1).astype(jnp.int32), left, upper, cols, rows, trailing)
    return updated, spread(updated, col_at)


def solution(mesh):
    fine = Mesh(mesh.devices.reshape(16, 2, 16), ("row", "xhi", "z"))
    grid = P("row", COL)
    turned = P(COL, "row")
    return jax.shard_map(
        body,
        mesh=fine,
        in_specs=(grid, turned, turned, grid, grid, P(), P()),
        out_specs=(grid, P(("row",) + COL, None)),
        check_vma=False,
    )
```

time: 207 us -> 173 us (0.84)
  the two profiles are of different devices: /device:TPU:56 before, /device:TPU:26 now
where the time goes in v3:
time: 173 us; the launch traced here: 172 us
  waiting for transfers between devices  93.2 us (54%)
  starting transfers between devices  40.6 us (23%)
  between operations  14.3 us (8%)
  Pallas kernels  10 us (6%)
  local copies, waits for them, and re-layouts  7.67 us (4%)
  other arithmetic  6.16 us (4%)
    all_to_all x1, waiting for transfers between devices, body(): lax.all_to_all(jnp.broadcast_to(rows[None], (NT,) + rows.shape), 'row', 0...  68.1 us
    ppermute x7, starting transfers between devices, spread(): lax.ppermute(updated[m * part:(m + 1) * part], COL, [(0, 4 * m), (1, 4 *...  19.1 us
    ppermute x7, waiting for transfers between devices, spread(): lax.ppermute(updated[m * part:(m + 1) * part], COL, [(0, 4 * m), (1, 4 *...  11.1 us
    pallas_call x1, Pallas kernels, update(): pl.pallas_call(update_kernel, out_shape=jax.ShapeDtypeStruct(trailing.sha...  10 us
    all_to_all x1, starting transfers between devices, body(): lax.all_to_all(jnp.broadcast_to(rows[None], (NT,) + rows.shape), 'row', 0...  9.12 us
    ppermute x1, waiting for transfers between devices, body(): other = lax.ppermute(mine, 'xhi', [(0, 1), (1, 0)])  6 us
    ppermute x3, starting transfers between devices, spread(): got.append(lax.ppermute(piece, COL, pairs))  4.5 us
    ppermute x1, starting transfers between devices, body(): other = lax.ppermute(mine, 'xhi', [(0, 1), (1, 0)])  4.03 us
  transfers between devices with their start and end apart: 14, of which 7 were waited for; matrix products, arithmetic and copies ran while one was open for 3% of the time, Pallas kernels for 0%

profile of v3, /device:TPU:26, one launch (start us, length us, event | category | flops | bytes accessed | tf_op | source)
XLA Modules:
  0.0 172.0 jit_solution(11042906450888783273)
XLA Ops:
  7.2 1.0 pad_maximum_fusion.2
  8.2 4.0 %collective-permute-start = (bf16[96,1024]{1,0:T(8,128)(2,1)S(1)}, bf16[96,1024]{1,0:T(8,128)(2,1)S(1)}, u32[]{:S(2)}, u32[]{:S(2)}) collective-permute-start(bf16[96,1024]{1,0:T(8,128)(2,1)S(1)} %pad_maximum_fusion.2), channel_id=1, source_target_pairs={{0,16},{16,0},{1,17},{17,1},{2,18},{18,2},{3,19},{19,3},{4,20},{20... | collective-permute-start | bytes 589832 | tf_op jit(solution)/shard_map/ppermute | solution.py:113
  12.2 6.0 %collective-permute-done = bf16[96,1024]{1,0:T(8,128)(2,1)S(1)} collective-permute-done((bf16[96,1024]{1,0:T(8,128)(2,1)S(1)}, bf16[96,1024]{1,0:T(8,128)(2,1)S(1)}, u32[]{:S(2)}, u32[]{:S(2)}) %collective-permute-start) | collective-permute-done | bytes 196640 | tf_op jit(solution)/shard_map/ppermute | solution.py:113
  18.2 1.7 %pad_maximum_fusion = bf16[192,1024]{1,0:T(8,128)(2,1)} fusion(bf16[96,1024]{1,0:T(8,128)(2,1)S(1)} %collective-permute-done, bf16[48,1024]{1,0:T(8,128)(2,1)} %param.9, bf16[48,1024]{1,0:T(8,128)(2,1)} %param.8), kind=kLoop, calls=%fused_computation | loop fusion | flops 1179648 | bytes 786432 | tf_op jit(solution)/shard_map/concatenate | solution.py:114
  20.0 3.8 %collective-permute-start.1 = (bf16[96,512]{1,0:T(8,128)(2,1)}, bf16[96,512]{1,0:T(8,128)(2,1)S(1)}, u32[]{:S(2)}, u32[]{:S(2)}) collective-permute-start(bf16[96,512]{1,0:T(8,128)(2,1)} %param.10), channel_id=1, source_target_pairs={{0,1},{1,0},{2,3},{3,2},{4,5},{5,4},{6,7},{7,6},{8,9},{9,8},{10,11... | collective-permute-start | bytes 294920 | tf_op jit(solution)/shard_map/ppermute | solution.py:117
  23.8 2.9 %collective-permute-done.1 = bf16[96,512]{1,0:T(8,128)(2,1)S(1)} collective-permute-done((bf16[96,512]{1,0:T(8,128)(2,1)}, bf16[96,512]{1,0:T(8,128)(2,1)S(1)}, u32[]{:S(2)}, u32[]{:S(2)}) %collective-permute-start.1) | collective-permute-done | bytes 98336 | tf_op jit(solution)/shard_map/ppermute | solution.py:117
  26.7 0.9 broadcast_select_fusion.1
  27.6 0.9 pad_maximum_fusion.1
  28.5 2.6 %broadcast_in_dim.2 = bf16[16,96,1536]{2,1,0:T(8,128)(2,1)} broadcast(bf16[96,1536]{1,0:T(8,128)(2,1)S(1)} %pad_maximum_fusion.1), dimensions={1,2} | broadcast | bytes 5013504 | tf_op jit(solution)/shard_map/broadcast_in_dim | solution.py:122
  31.2 9.1 %all-to-all-start = ((bf16[16,96,1536]{2,1,0:T(8,128)(2,1)}), bf16[16,96,1536]{2,1,0:T(8,128)(2,1)}, u32[]{:S(2)}, u32[]{:S(2)}) async-start(bf16[16,96,1536]{2,1,0:T(8,128)(2,1)} %broadcast_in_dim.2), calls=%async_computation | async-start | bytes 9437184 | tf_op jit(solution)/shard_map/all_to_all | solution.py:122
  40.3 0.2 dynamic-slice_reduce_fusion.upper_ref
  40.5 0.7 fusion.6.left_ref
  41.2 68.1 %all-to-all-done = bf16[16,96,1536]{2,1,0:T(8,128)(2,1)} async-done(((bf16[16,96,1536]{2,1,0:T(8,128)(2,1)}), bf16[16,96,1536]{2,1,0:T(8,128)(2,1)}, u32[]{:S(2)}, u32[]{:S(2)}) %all-to-all-start) | async-done | bytes 4718624 | tf_op jit(solution)/shard_map/all_to_all | solution.py:122
  109.3 1.3 all-gather.2.cloned.1.call-done
  110.6 2.8 %copy-done.1 = bf16[3072,1024]{1,0:T(8,128)(2,1)S(1)} copy-done((bf16[3072,1024]{1,0:T(8,128)(2,1)S(1)}, bf16[3072,1024]{1,0:T(8,128)(2,1)}, u32[]{:S(2)}) %copy-start.1) | copy-done | bytes 6291480
  113.4 10.0 %shard_map.86 = bf16[1024,512]{1,0:T(8,128)(2,1)} custom-call(s32[1]{0:T(128)} %bitcast.x_at_ref, s32[16]{0:T(128)S(1)} %fusion.6.left_ref, s32[16]{0:T(128)S(1)} %dynamic-slice_reduce_fusion.upper_ref, bf16[16,2,2,48,1024]{4,3,2,1,0:T(8,128)(2,1)S(1)} %bitcast.5, bf16[2,8,96,1536]{3,2,1,0:T(8,128)(2,1)} %bitcast.3.rows_ref, bf16[1024,512]{1,0:T(8,128)(2,1)S(1)} %copy-done.2), custom_call_target="tpu_custom_call" | custom-call | tf_op jit(solution)/shard_map/pallas_call | solution.py:88
  123.4 1.3 fusion.7
  124.7 5.3 %collective-permute-start.2 = (bf16[128,512]{1,0:T(8,128)(2,1)S(1)}, bf16[128,512]{1,0:T(8,128)(2,1)S(1)}, u32[]{:S(2)}, u32[]{:S(2)}) collective-permute-start(bf16[128,512]{1,0:T(8,128)(2,1)S(1)} %get-tuple-element.8), channel_id=1, source_target_pairs={{0,4},{1,5},{32,36},{33,37},{64,68},{65,69},{96,100},{97,101},{128... | collective-permute-start | bytes 393224 | tf_op jit(solution)/shard_map/ppermute | solution.py:26
  130.1 7.3 %collective-permute-start.3 = (bf16[128,512]{1,0:T(8,128)(2,1)S(1)}, bf16[128,512]{1,0:T(8,128)(2,1)S(1)}, u32[]{:S(2)}, u32[]{:S(2)}) collective-permute-start(bf16[128,512]{1,0:T(8,128)(2,1)S(1)} %get-tuple-element.7), channel_id=1, source_target_pairs={{0,8},{1,9},{32,40},{33,41},{64,72},{65,73},{96,104},{97,105},{128... | collective-permute-start | bytes 393224 | tf_op jit(solution)/shard_map/ppermute | solution.py:26
  137.4 1.3 collective-permute-start.4
  138.7 1.3 collective-permute-start.5
  140.0 1.3 collective-permute-start.6
  141.3 1.3 collective-permute-start.7
  142.6 1.3 collective-permute-start.8
  144.0 8.3 %collective-permute-done.4 = bf16[128,512]{1,0:T(8,128)(2,1)S(1)} collective-permute-done((bf16[128,512]{1,0:T(8,128)(2,1)S(1)}, bf16[128,512]{1,0:T(8,128)(2,1)S(1)}, u32[]{:S(2)}, u32[]{:S(2)}) %collective-permute-start.4) | collective-permute-done | bytes 131104 | tf_op jit(solution)/shard_map/ppermute | solution.py:26
  152.3 2.7 %collective-permute-done.8 = bf16[128,512]{1,0:T(8,128)(2,1)S(1)} collective-permute-done((bf16[128,512]{1,0:T(8,128)(2,1)S(1)}, bf16[128,512]{1,0:T(8,128)(2,1)S(1)}, u32[]{:S(2)}, u32[]{:S(2)}) %collective-permute-start.8) | collective-permute-done | bytes 131104 | tf_op jit(solution)/shard_map/ppermute | solution.py:26
  155.1 1.0 fusion.5
  156.1 1.3 collective-permute-start.10
  157.4 1.3 collective-permute-start.11
  158.7 1.9 %collective-permute-start.9 = (bf16[32,512]{1,0:T(8,128)(2,1)S(1)}, bf16[32,512]{1,0:T(8,128)(2,1)S(1)}, u32[]{:S(2)}, u32[]{:S(2)}) collective-permute-start(bf16[32,512]{1,0:T(8,128)(2,1)S(1)} %get-tuple-element.15), channel_id=1, source_target_pairs={{0,3},{1,0},{4,7},{5,4},{8,11},{9,8},{12,15},{13,12},{16,19},{17,1... | collective-permute-start | bytes 98312 | tf_op jit(solution)/shard_map/ppermute | solution.py:34
  160.6 3.8 %collective-permute-done.9 = bf16[32,512]{1,0:T(8,128)(2,1)S(1)} collective-permute-done((bf16[32,512]{1,0:T(8,128)(2,1)S(1)}, bf16[32,512]{1,0:T(8,128)(2,1)S(1)}, u32[]{:S(2)}, u32[]{:S(2)}) %collective-permute-start.9) | collective-permute-done | bytes 32800 | tf_op jit(solution)/shard_map/ppermute | solution.py:34
  164.5 0.6 pad_maximum_fusion.3
  (16 shorter events, 0.1 us)
Async XLA Ops:
  7.2 33.2 %copy-start = (s32[16,16]{1,0:T(8,128)S(1)}, s32[16,16]{1,0:T(8,128)}, u32[]{:S(2)}) copy-start(s32[16,16]{1,0:T(8,128)} %param.13) | copy-start | bytes 3076
  7.2 103.4 %all-gather.2.cloned.1.call-start = ((), (), s32[]{:S(2)}) async-start(), calls=%async_computation.1 | async-start | bytes 6684672 | tf_op jit(solution)/shard_map/all_gather | solution.py:114
  8.2 10.0 %collective-permute-start = (bf16[96,1024]{1,0:T(8,128)(2,1)S(1)}, bf16[96,1024]{1,0:T(8,128)(2,1)S(1)}, u32[]{:S(2)}, u32[]{:S(2)}) collective-permute-start(bf16[96,1024]{1,0:T(8,128)(2,1)S(1)} %pad_maximum_fusion.2), channel_id=1, source_target_pairs={{0,16},{16,0},{1,17},{17,1},{2,18},{18,2},{3,19},{19,3},{4,20},{20... | collective-permute-start | bytes 589832 | tf_op jit(solution)/shard_map/ppermute | solution.py:113
  20.0 6.7 %collective-permute-start.1 = (bf16[96,512]{1,0:T(8,128)(2,1)}, bf16[96,512]{1,0:T(8,128)(2,1)S(1)}, u32[]{:S(2)}, u32[]{:S(2)}) collective-permute-start(bf16[96,512]{1,0:T(8,128)(2,1)} %param.10), channel_id=1, source_target_pairs={{0,1},{1,0},{2,3},{3,2},{4,5},{5,4},{6,7},{7,6},{8,9},{9,8},{10,11... | collective-permute-start | bytes 294920 | tf_op jit(solution)/shard_map/ppermute | solution.py:117
  31.2 79.4 %copy-start.2 = (bf16[1024,512]{1,0:T(8,128)(2,1)S(1)}, bf16[1024,512]{1,0:T(8,128)(2,1)}, u32[]{:S(2)}) copy-start(bf16[1024,512]{1,0:T(8,128)(2,1)} %trailing_ref.1) | copy-start | bytes 3145732
  31.2 78.1 %all-to-all-start = ((bf16[16,96,1536]{2,1,0:T(8,128)(2,1)}), bf16[16,96,1536]{2,1,0:T(8,128)(2,1)}, u32[]{:S(2)}, u32[]{:S(2)}) async-start(bf16[16,96,1536]{2,1,0:T(8,128)(2,1)} %broadcast_in_dim.2), calls=%async_computation | async-start | bytes 9437184 | tf_op jit(solution)/shard_map/all_to_all | solution.py:122
  110.6 2.8 %copy-start.1 = (bf16[3072,1024]{1,0:T(8,128)(2,1)S(1)}, bf16[3072,1024]{1,0:T(8,128)(2,1)}, u32[]{:S(2)}) copy-start(bf16[3072,1024]{1,0:T(8,128)(2,1)} %all-gather.2.cloned.1.call-done) | copy-start | bytes 18874372
  124.7 16.5 %collective-permute-start.2 = (bf16[128,512]{1,0:T(8,128)(2,1)S(1)}, bf16[128,512]{1,0:T(8,128)(2,1)S(1)}, u32[]{:S(2)}, u32[]{:S(2)}) collective-permute-start(bf16[128,512]{1,0:T(8,128)(2,1)S(1)} %get-tuple-element.8), channel_id=1, source_target_pairs={{0,4},{1,5},{32,36},{33,37},{64,68},{65,69},{96,100},{97,101},{128... | collective-permute-start | bytes 393224 | tf_op jit(solution)/shard_map/ppermute | solution.py:26
  130.1 12.5 %collective-permute-start.3 = (bf16[128,512]{1,0:T(8,128)(2,1)S(1)}, bf16[128,512]{1,0:T(8,128)(2,1)S(1)}, u32[]{:S(2)}, u32[]{:S(2)}) collective-permute-start(bf16[128,512]{1,0:T(8,128)(2,1)S(1)} %get-tuple-element.7), channel_id=1, source_target_pairs={{0,8},{1,9},{32,40},{33,41},{64,72},{65,73},{96,104},{97,105},{128... | collective-permute-start | bytes 393224 | tf_op jit(solution)/shard_map/ppermute | solution.py:26
  137.4 14.9 %collective-permute-start.4 = (bf16[128,512]{1,0:T(8,128)(2,1)S(1)}, bf16[128,512]{1,0:T(8,128)(2,1)S(1)}, u32[]{:S(2)}, u32[]{:S(2)}) collective-permute-start(bf16[128,512]{1,0:T(8,128)(2,1)S(1)} %get-tuple-element.6), channel_id=1, source_target_pairs={{0,12},{1,13},{32,44},{33,45},{64,76},{65,77},{96,108},{97,109},{1... | collective-permute-start | bytes 393224 | tf_op jit(solution)/shard_map/ppermute | solution.py:26
  138.7 13.6 %collective-permute-start.5 = (bf16[128,512]{1,0:T(8,128)(2,1)S(1)}, bf16[128,512]{1,0:T(8,128)(2,1)S(1)}, u32[]{:S(2)}, u32[]{:S(2)}) collective-permute-start(bf16[128,512]{1,0:T(8,128)(2,1)S(1)} %get-tuple-element.5), channel_id=1, source_target_pairs={{0,16},{1,17},{32,48},{33,49},{64,80},{65,81},{96,112},{97,113},{1... | collective-permute-start | bytes 393224 | tf_op jit(solution)/shard_map/ppermute | solution.py:26
  140.0 12.3 %collective-permute-start.6 = (bf16[128,512]{1,0:T(8,128)(2,1)S(1)}, bf16[128,512]{1,0:T(8,128)(2,1)S(1)}, u32[]{:S(2)}, u32[]{:S(2)}) collective-permute-start(bf16[128,512]{1,0:T(8,128)(2,1)S(1)} %get-tuple-element.4), channel_id=1, source_target_pairs={{0,20},{1,21},{32,52},{33,53},{64,84},{65,85},{96,116},{97,117},{1... | collective-permute-start | bytes 393224 | tf_op jit(solution)/shard_map/ppermute | solution.py:26
  141.3 11.0 %collective-permute-start.7 = (bf16[128,512]{1,0:T(8,128)(2,1)S(1)}, bf16[128,512]{1,0:T(8,128)(2,1)S(1)}, u32[]{:S(2)}, u32[]{:S(2)}) collective-permute-start(bf16[128,512]{1,0:T(8,128)(2,1)S(1)} %get-tuple-element.3), channel_id=1, source_target_pairs={{0,24},{1,25},{32,56},{33,57},{64,88},{65,89},{96,120},{97,121},{1... | collective-permute-start | bytes 393224 | tf_op jit(solution)/shard_map/ppermute | solution.py:26
  142.6 12.5 %collective-permute-start.8 = (bf16[128,512]{1,0:T(8,128)(2,1)S(1)}, bf16[128,512]{1,0:T(8,128)(2,1)S(1)}, u32[]{:S(2)}, u32[]{:S(2)}) collective-permute-start(bf16[128,512]{1,0:T(8,128)(2,1)S(1)} %get-tuple-element.2), channel_id=1, source_target_pairs={{0,28},{1,29},{32,60},{33,61},{64,92},{65,93},{96,124},{97,125},{1... | collective-permute-start | bytes 393224 | tf_op jit(solution)/shard_map/ppermute | solution.py:26
  156.1 4.6 %collective-permute-start.10 = (bf16[32,512]{1,0:T(8,128)(2,1)S(1)}, bf16[32,512]{1,0:T(8,128)(2,1)S(1)}, u32[]{:S(2)}, u32[]{:S(2)}) collective-permute-start(bf16[32,512]{1,0:T(8,128)(2,1)S(1)} %get-tuple-element.14), channel_id=1, source_target_pairs={{0,2},{1,3},{4,6},{5,7},{8,10},{9,11},{12,14},{13,15},{16,18},{17,... | collective-permute-start | bytes 98312 | tf_op jit(solution)/shard_map/ppermute | solution.py:34
  157.4 3.3 %collective-permute-start.11 = (bf16[32,512]{1,0:T(8,128)(2,1)S(1)}, bf16[32,512]{1,0:T(8,128)(2,1)S(1)}, u32[]{:S(2)}, u32[]{:S(2)}) collective-permute-start(bf16[32,512]{1,0:T(8,128)(2,1)S(1)} %get-tuple-element.13), channel_id=1, source_target_pairs={{0,1},{1,2},{4,5},{5,6},{8,9},{9,10},{12,13},{13,14},{16,17},{17,1... | collective-permute-start | bytes 98312 | tf_op jit(solution)/shard_map/ppermute | solution.py:34
  158.7 5.8 %collective-permute-start.9 = (bf16[32,512]{1,0:T(8,128)(2,1)S(1)}, bf16[32,512]{1,0:T(8,128)(2,1)S(1)}, u32[]{:S(2)}, u32[]{:S(2)}) collective-permute-start(bf16[32,512]{1,0:T(8,128)(2,1)S(1)} %get-tuple-element.15), channel_id=1, source_target_pairs={{0,3},{1,0},{4,7},{5,4},{8,11},{9,8},{12,15},{13,12},{16,19},{17,1... | collective-permute-start | bytes 98312 | tf_op jit(solution)/shard_map/ppermute | solution.py:34
Sparse Core Ops, SparseCore 0:
  20.1 90.4 all-gather.1

commit v4 on v3

v4 whole, which is shorter than its diff:
```python
import jax
import jax.numpy as jnp
from jax import lax
from jax.experimental import pallas as pl
from jax.experimental.pallas import tpu as pltpu
from jax.sharding import Mesh, PartitionSpec as P

NT = 16
COL = ("xhi", "z")
BF = jnp.bfloat16
SWAP_Z = [(i, i ^ 1) for i in range(16)]
LIMIT = 28


def place(branches, default):
    for hit, value in branches:
        default = jnp.where(hit, value, default)
    return default


def spread(updated, parts, col_at):
    share = updated.shape[0] // 32
    part = 4 * share
    sent = []
    for m in range(7, 0, -1):
        block = lax.ppermute(parts[m - 1], COL, [(0, 4 * m), (1, 4 * m + 1)])
        sent.append((col_at // 4 == m, block))
    held = place(sent, updated[:part])
    spot = col_at % 4
    got = []
    for d in (1, 2, 3):
        piece = lax.dynamic_slice_in_dim(held, (spot + d) % 4 * share, share, 0)
        pairs = [(b + h, b + (h + d) % 4) for b in range(0, 32, 4) for h in (0, 1)]
        got.append(lax.ppermute(piece, COL, pairs))
    own = lax.dynamic_slice_in_dim(held, spot * share, share, 0)
    left = place([(spot == d, got[d - 1]) for d in (1, 2, 3)], own)
    right = place([((spot - 1) % 4 == d, got[d - 1]) for d in (1, 2, 3)], own)
    return jnp.concatenate([left, right], axis=1)


def update_kernel(
    x_at_ref, left_ref, upper_ref, cols_ref, p_ref, q_ref, trailing_ref, out_ref, *rest
):
    parts, (outer_ref, inner_ref, weights_ref, q_held, dense_ref, sems) = rest[:7], rest[7:]
    rank_pad = p_ref.shape[2]
    depth = cols_ref.shape[4]
    copies = []

    def fetch(source, target):
        copies.append(pltpu.make_async_copy(source, target, sems.at[len(copies)]))

    for zz in range(8):
        for h in range(2):
            fetch(cols_ref.at[2 * zz + h, :, 1], inner_ref.at[zz, :, h])
        fetch(q_ref.at[:, zz], q_held.at[:, zz])
    for zz in range(8):
        for h in range(2):
            fetch(cols_ref.at[2 * zz + h, :, 0], outer_ref.at[zz, :, h])
    fetch(trailing_ref, dense_ref)
    for copy in copies:
        copy.start()
    t = lax.broadcasted_iota(jnp.int32, (rank_pad, rank_pad), 0)
    u = lax.broadcasted_iota(jnp.int32, (rank_pad, rank_pad), 1)
    for zz in range(8):
        for copy in copies[3 * zz : 3 * zz + 3]:
            copy.wait()
        for slot in range(2):
            xhi = slot ^ x_at_ref[0]
            k = xhi * 8 + zz
            core = lax.dot_general(
                inner_ref[zz, slot].reshape(rank_pad, depth),
                p_ref[xhi, zz],
                (((1,), (1,)), ((), ())),
                preferred_element_type=jnp.float32,
            )
            core = jnp.where((t < left_ref[k]) & (u < upper_ref[k]), core, 0.0).astype(BF)
            at = (2 * zz + slot) * rank_pad
            weights_ref[at : at + rank_pad, :] = jnp.dot(
                core, q_held[xhi, zz], preferred_element_type=jnp.float32
            ).astype(BF)
    for copy in copies[24:]:
        copy.wait()
    outer = outer_ref[...].reshape(NT * rank_pad, depth)
    product = lax.dot_general(outer, weights_ref[...], (((0,), (0,)), ((), ())), preferred_element_type=jnp.float32)
    done = (dense_ref[...].astype(jnp.float32) - product).astype(BF)
    out_ref[...] = done
    part = done.shape[0] // 8
    for m in range(1, 8):
        parts[m - 1][...] = done[m * part : (m + 1) * part]


def update(x_at, left, upper, cols, p_rows, q_rows, trailing):
    height, width = trailing.shape
    rank_pad, depth, half = p_rows.shape[2], cols.shape[4], cols.shape[3]
    vmem, smem = pl.BlockSpec(memory_space=pltpu.VMEM), pl.BlockSpec(memory_space=pltpu.SMEM)
    hbm = pl.BlockSpec(memory_space=pltpu.HBM)
    held = pltpu.VMEM((8, 2, 2, half, depth), BF)
    return pl.pallas_call(
        update_kernel,
        out_shape=[jax.ShapeDtypeStruct((height, width), BF)] + [jax.ShapeDtypeStruct((height // 8, width), BF)] * 7,
        in_specs=[smem, smem, smem, hbm, vmem, hbm, hbm],
        out_specs=[vmem] * 8,
        scratch_shapes=[held, held, pltpu.VMEM((NT * rank_pad, width), BF), pltpu.VMEM(q_rows.shape, BF), pltpu.VMEM(trailing.shape, BF), pltpu.SemaphoreType.DMA((41,))],
        compiler_params=pltpu.CompilerParams(vmem_limit_bytes=LIMIT << 20),
    )(
        x_at,
        left,
        upper,
        pltpu.with_memory_space_constraint(cols, pltpu.HBM),
        p_rows,
        pltpu.with_memory_space_constraint(q_rows, pltpu.HBM),
        pltpu.with_memory_space_constraint(trailing, pltpu.HBM),
    )


def body(trailing, left_outer, left_inner, upper_outer, upper_inner, left_ranks, upper_ranks):
    row_at = lax.axis_index("row")
    x_at, z_at = lax.axis_index("xhi"), lax.axis_index("z")
    col_at = x_at * 16 + z_at
    half = left_outer.shape[0]

    mine = jnp.concatenate([left_outer, left_inner], axis=0)
    other = lax.ppermute(mine, "xhi", [(0, 1), (1, 0)])
    cols = lax.all_gather(jnp.concatenate([mine, other], axis=0), "z", axis=0, tiled=True)
    cols = cols.reshape(NT, 2, 2, half, -1)

    partner = lax.ppermute(upper_outer, "z", SWAP_Z)
    even = z_at % 2 == 0
    rows = jnp.concatenate(
        [jnp.where(even, upper_outer, partner), jnp.where(even, partner, upper_outer), upper_inner], axis=1
    )
    rows = lax.all_to_all(jnp.broadcast_to(rows[None], (NT,) + rows.shape), "row", 0, 0)
    rows = rows.reshape((2, 8) + rows.shape[1:])
    depth = cols.shape[-1]
    p_rows, q_rows = rows[..., :depth], rows[..., depth:]

    left = lax.dynamic_index_in_dim(left_ranks, row_at, 0, keepdims=False)
    upper = lax.dynamic_index_in_dim(upper_ranks, col_at // 2, 1, keepdims=False)
    updated, *parts = update(x_at.reshape(1).astype(jnp.int32), left, upper, cols, p_rows, q_rows, trailing)
    return updated, spread(updated, parts, col_at)


def solution(mesh):
    fine = Mesh(mesh.devices.reshape(16, 2, 16), ("row", "xhi", "z"))
    grid = P("row", COL)
    turned = P(COL, "row")
    return jax.shard_map(
        body,
        mesh=fine,
        in_specs=(grid, turned, turned, grid, grid, P(), P()),
        out_specs=(grid, P(("row",) + COL, None)),
        check_vma=False,
    )
```

time: 173 us -> 173 us (level)
    slice x1 -> x2, local copies, waits for them, and re-layouts: 1.33 us -> 4.92 us  [body(): p_rows, q_rows = (rows[..., :depth], rows[..., depth:])]
    unnamed x6 -> x2, local copies, waits for them, and re-layouts: 2.8 us -> 0.01 us
  transfers between devices with their start and end apart: 14 -> 14, of which waited for: 7 -> 6; matrix products, arithmetic and copies ran while one was open for 3% -> 6% of each run, Pallas kernels for 0% -> 0%
where the time goes in v4:
time: 173 us
  waiting for transfers between devices  91.9 us (53%)
  starting transfers between devices  41.7 us (24%)
  between operations  14.3 us (8%)
  Pallas kernels  9.95 us (6%)
  local copies, waits for them, and re-layouts  8.48 us (5%)
  other arithmetic  6.16 us (4%)
    all_to_all x1, waiting for transfers between devices, body(): lax.all_to_all(jnp.broadcast_to(rows[None], (NT,) + rows.shape), 'row', 0...  68.1 us
    ppermute x7, starting transfers between devices, spread(): block = lax.ppermute(parts[m - 1], COL, [(0, 4 * m), (1, 4 * m + 1)])  20.3 us
    ppermute x7, waiting for transfers between devices, spread(): block = lax.ppermute(parts[m - 1], COL, [(0, 4 * m), (1, 4 * m + 1)])  11.1 us
    pallas_call x1, Pallas kernels, update(): pl.pallas_call(update_kernel, out_shape=[jax.ShapeDtypeStruct((height, wi...  9.95 us
    all_to_all x1, starting transfers between devices, body(): lax.all_to_all(jnp.broadcast_to(rows[None], (NT,) + rows.shape), 'row', 0...  8.99 us
    ppermute x1, waiting for transfers between devices, body(): other = lax.ppermute(mine, 'xhi', [(0, 1), (1, 0)])  6 us
    slice x2, local copies, waits for them, and re-layouts, body(): p_rows, q_rows = (rows[..., :depth], rows[..., depth:])  4.92 us
    ppermute x3, starting transfers between devices, spread(): got.append(lax.ppermute(piece, COL, pairs))  4.5 us
  transfers between devices with their start and end apart: 14, of which 6 were waited for; matrix products, arithmetic and copies ran while one was open for 6% of the time, Pallas kernels for 0%

profile of v4, /device:TPU:26, one launch (start us, length us, event | category | flops | bytes accessed | tf_op | source)
XLA Modules:
  0.0 172.6 jit_solution(5577860487854260668)
XLA Ops:
  7.2 0.0 all-gather.2.cloned.1.call-start
  7.2 1.0 pad_maximum_fusion.2
  8.2 4.0 %collective-permute-start = (bf16[96,1024]{1,0:T(8,128)(2,1)S(1)}, bf16[96,1024]{1,0:T(8,128)(2,1)S(1)}, u32[]{:S(2)}, u32[]{:S(2)}) collective-permute-start(bf16[96,1024]{1,0:T(8,128)(2,1)S(1)} %pad_maximum_fusion.2), channel_id=1, source_target_pairs={{0,16},{16,0},{1,17},{17,1},{2,18},{18,2},{3,19},{19,3},{4,20},{20... | collective-permute-start | bytes 589832 | tf_op jit(solution)/shard_map/ppermute | solution.py:123
  12.2 6.0 %collective-permute-done = bf16[96,1024]{1,0:T(8,128)(2,1)S(1)} collective-permute-done((bf16[96,1024]{1,0:T(8,128)(2,1)S(1)}, bf16[96,1024]{1,0:T(8,128)(2,1)S(1)}, u32[]{:S(2)}, u32[]{:S(2)}) %collective-permute-start) | collective-permute-done | bytes 196640 | tf_op jit(solution)/shard_map/ppermute | solution.py:123
  18.2 1.7 %pad_maximum_fusion = bf16[192,1024]{1,0:T(8,128)(2,1)} fusion(bf16[96,1024]{1,0:T(8,128)(2,1)S(1)} %collective-permute-done, bf16[48,1024]{1,0:T(8,128)(2,1)} %param.9, bf16[48,1024]{1,0:T(8,128)(2,1)} %param.8), kind=kLoop, calls=%fused_computation | loop fusion | flops 1179648 | bytes 786432 | tf_op jit(solution)/shard_map/concatenate | solution.py:124
  20.0 3.8 %collective-permute-start.1 = (bf16[96,512]{1,0:T(8,128)(2,1)}, bf16[96,512]{1,0:T(8,128)(2,1)S(1)}, u32[]{:S(2)}, u32[]{:S(2)}) collective-permute-start(bf16[96,512]{1,0:T(8,128)(2,1)} %param.10), channel_id=1, source_target_pairs={{0,1},{1,0},{2,3},{3,2},{4,5},{5,4},{6,7},{7,6},{8,9},{9,8},{10,11... | collective-permute-start | bytes 294920 | tf_op jit(solution)/shard_map/ppermute | solution.py:127
  23.8 2.9 %collective-permute-done.1 = bf16[96,512]{1,0:T(8,128)(2,1)S(1)} collective-permute-done((bf16[96,512]{1,0:T(8,128)(2,1)}, bf16[96,512]{1,0:T(8,128)(2,1)S(1)}, u32[]{:S(2)}, u32[]{:S(2)}) %collective-permute-start.1) | collective-permute-done | bytes 98336 | tf_op jit(solution)/shard_map/ppermute | solution.py:127
  26.7 0.9 broadcast_select_fusion.1
  27.6 0.9 pad_maximum_fusion.1
  28.5 2.6 %broadcast_in_dim.2 = bf16[16,96,1536]{2,1,0:T(8,128)(2,1)} broadcast(bf16[96,1536]{1,0:T(8,128)(2,1)S(1)} %pad_maximum_fusion.1), dimensions={1,2} | broadcast | bytes 5013504 | tf_op jit(solution)/shard_map/broadcast_in_dim | solution.py:132
  31.2 9.0 %all-to-all-start = ((bf16[16,96,1536]{2,1,0:T(8,128)(2,1)}), bf16[16,96,1536]{2,1,0:T(8,128)(2,1)}, u32[]{:S(2)}, u32[]{:S(2)}) async-start(bf16[16,96,1536]{2,1,0:T(8,128)(2,1)} %broadcast_in_dim.2), calls=%async_computation | async-start | bytes 9437184 | tf_op jit(solution)/shard_map/all_to_all | solution.py:132
  40.2 0.2 dynamic-slice_reduce_fusion.upper_ref
  40.4 0.7 fusion.left_ref
  41.1 68.1 %all-to-all-done = bf16[16,96,1536]{2,1,0:T(8,128)(2,1)} async-done(((bf16[16,96,1536]{2,1,0:T(8,128)(2,1)}), bf16[16,96,1536]{2,1,0:T(8,128)(2,1)}, u32[]{:S(2)}, u32[]{:S(2)}) %all-to-all-start) | async-done | bytes 4718624 | tf_op jit(solution)/shard_map/all_to_all | solution.py:132
  109.2 2.2 %slice.12.p_ref = bf16[2,8,96,1024]{3,2,1,0:T(8,128)(2,1)S(1)} slice(bf16[2,8,96,1536]{3,2,1,0:T(8,128)(2,1)} %bitcast.3), slice={[0:2], [0:8], [0:96], [0:1024]} | slice | bytes 6291456 | tf_op jit(solution)/shard_map/slice | solution.py:135
  111.4 2.7 %slice.13.q_ref = bf16[2,8,96,512]{3,2,1,0:T(8,128)(2,1)} slice(bf16[2,8,96,1536]{3,2,1,0:T(8,128)(2,1)} %bitcast.3), slice={[0:2], [0:8], [0:96], [1024:1536]} | slice | bytes 3145728 | tf_op jit(solution)/shard_map/slice | solution.py:135
  114.1 10.0 %shard_map.86 = (bf16[1024,512]{1,0:T(8,128)(2,1)}, bf16[128,512]{1,0:T(8,128)(2,1)S(1)}, bf16[128,512]{1,0:T(8,128)(2,1)S(1)}, bf16[128,512]{1,0:T(8,128)(2,1)}...) custom-call(s32[1]{0:T(128)} %bitcast.x_at_ref, ...), custom_call_target="tpu_custom_call" | custom-call | tf_op jit(solution)/shard_map/pallas_call | solution.py:98
  124.1 6.6 %collective-permute-start.2 = (bf16[128,512]{1,0:T(8,128)(2,1)S(1)}, bf16[128,512]{1,0:T(8,128)(2,1)S(1)}, u32[]{:S(2)}, u32[]{:S(2)}) collective-permute-start(bf16[128,512]{1,0:T(8,128)(2,1)S(1)} %get-tuple-element.11), channel_id=1, source_target_pairs={{0,4},{1,5},{32,36},{33,37},{64,68},{65,69},{96,100},{97,101},{128... | collective-permute-start | bytes 393224 | tf_op jit(solution)/shard_map/ppermute | solution.py:26
  130.7 7.3 %collective-permute-start.3 = (bf16[128,512]{1,0:T(8,128)(2,1)S(1)}, bf16[128,512]{1,0:T(8,128)(2,1)S(1)}, u32[]{:S(2)}, u32[]{:S(2)}) collective-permute-start(bf16[128,512]{1,0:T(8,128)(2,1)S(1)} %get-tuple-element.12), channel_id=1, source_target_pairs={{0,8},{1,9},{32,40},{33,41},{64,72},{65,73},{96,104},{97,105},{128... | collective-permute-start | bytes 393224 | tf_op jit(solution)/shard_map/ppermute | solution.py:26
  138.0 1.3 collective-permute-start.4
  139.3 1.3 collective-permute-start.5
  140.6 1.3 collective-permute-start.6
  141.9 1.3 collective-permute-start.7
  143.2 1.3 collective-permute-start.8
  144.6 8.4 %collective-permute-done.4 = bf16[128,512]{1,0:T(8,128)(2,1)S(1)} collective-permute-done((bf16[128,512]{1,0:T(8,128)(2,1)}, bf16[128,512]{1,0:T(8,128)(2,1)S(1)}, u32[]{:S(2)}, u32[]{:S(2)}) %collective-permute-start.4) | collective-permute-done | bytes 131104 | tf_op jit(solution)/shard_map/ppermute | solution.py:26
  153.0 2.6 %collective-permute-done.8 = bf16[128,512]{1,0:T(8,128)(2,1)S(1)} collective-permute-done((bf16[128,512]{1,0:T(8,128)(2,1)S(1)}, bf16[128,512]{1,0:T(8,128)(2,1)S(1)}, u32[]{:S(2)}, u32[]{:S(2)}) %collective-permute-start.8) | collective-permute-done | bytes 131104 | tf_op jit(solution)/shard_map/ppermute | solution.py:26
  155.7 1.0 select_select_fusion
  156.7 1.3 collective-permute-start.10
  158.0 1.3 collective-permute-start.11
  159.3 1.9 %collective-permute-start.9 = (bf16[32,512]{1,0:T(8,128)(2,1)S(1)}, bf16[32,512]{1,0:T(8,128)(2,1)S(1)}, u32[]{:S(2)}, u32[]{:S(2)}) collective-permute-start(bf16[32,512]{1,0:T(8,128)(2,1)S(1)} %get-tuple-element.24), channel_id=1, source_target_pairs={{0,3},{1,0},{4,7},{5,4},{8,11},{9,8},{12,15},{13,12},{16,19},{17,1... | collective-permute-start | bytes 98312 | tf_op jit(solution)/shard_map/ppermute | solution.py:34
  161.3 3.8 %collective-permute-done.9 = bf16[32,512]{1,0:T(8,128)(2,1)S(1)} collective-permute-done((bf16[32,512]{1,0:T(8,128)(2,1)S(1)}, bf16[32,512]{1,0:T(8,128)(2,1)S(1)}, u32[]{:S(2)}, u32[]{:S(2)}) %collective-permute-start.9) | collective-permute-done | bytes 32800 | tf_op jit(solution)/shard_map/ppermute | solution.py:34
  165.1 0.6 pad_maximum_fusion.3
  (13 shorter events, 0.1 us)
Async XLA Ops:
  7.2 33.0 %copy-start = (s32[16,16]{1,0:T(8,128)S(1)}, s32[16,16]{1,0:T(8,128)}, u32[]{:S(2)}) copy-start(s32[16,16]{1,0:T(8,128)} %param.13) | copy-start | bytes 3076
  7.2 107.0 %all-gather.2.cloned.1.call-start = ((), (), s32[]{:S(2)}) async-start(), calls=%async_computation.1 | async-start | bytes 6684672 | tf_op jit(solution)/shard_map/all_gather | solution.py:124
  8.2 10.0 %collective-permute-start = (bf16[96,1024]{1,0:T(8,128)(2,1)S(1)}, bf16[96,1024]{1,0:T(8,128)(2,1)S(1)}, u32[]{:S(2)}, u32[]{:S(2)}) collective-permute-start(bf16[96,1024]{1,0:T(8,128)(2,1)S(1)} %pad_maximum_fusion.2), channel_id=1, source_target_pairs={{0,16},{16,0},{1,17},{17,1},{2,18},{18,2},{3,19},{19,3},{4,20},{20... | collective-permute-start | bytes 589832 | tf_op jit(solution)/shard_map/ppermute | solution.py:123
  20.0 6.7 %collective-permute-start.1 = (bf16[96,512]{1,0:T(8,128)(2,1)}, bf16[96,512]{1,0:T(8,128)(2,1)S(1)}, u32[]{:S(2)}, u32[]{:S(2)}) collective-permute-start(bf16[96,512]{1,0:T(8,128)(2,1)} %param.10), channel_id=1, source_target_pairs={{0,1},{1,0},{2,3},{3,2},{4,5},{5,4},{6,7},{7,6},{8,9},{9,8},{10,11... | collective-permute-start | bytes 294920 | tf_op jit(solution)/shard_map/ppermute | solution.py:127
  31.2 78.0 %all-to-all-start = ((bf16[16,96,1536]{2,1,0:T(8,128)(2,1)}), bf16[16,96,1536]{2,1,0:T(8,128)(2,1)}, u32[]{:S(2)}, u32[]{:S(2)}) async-start(bf16[16,96,1536]{2,1,0:T(8,128)(2,1)} %broadcast_in_dim.2), calls=%async_computation | async-start | bytes 9437184 | tf_op jit(solution)/shard_map/all_to_all | solution.py:132
  124.1 17.8 %collective-permute-start.2 = (bf16[128,512]{1,0:T(8,128)(2,1)S(1)}, bf16[128,512]{1,0:T(8,128)(2,1)S(1)}, u32[]{:S(2)}, u32[]{:S(2)}) collective-permute-start(bf16[128,512]{1,0:T(8,128)(2,1)S(1)} %get-tuple-element.11), channel_id=1, source_target_pairs={{0,4},{1,5},{32,36},{33,37},{64,68},{65,69},{96,100},{97,101},{128... | collective-permute-start | bytes 393224 | tf_op jit(solution)/shard_map/ppermute | solution.py:26
  130.7 12.5 %collective-permute-start.3 = (bf16[128,512]{1,0:T(8,128)(2,1)S(1)}, bf16[128,512]{1,0:T(8,128)(2,1)S(1)}, u32[]{:S(2)}, u32[]{:S(2)}) collective-permute-start(bf16[128,512]{1,0:T(8,128)(2,1)S(1)} %get-tuple-element.12), channel_id=1, source_target_pairs={{0,8},{1,9},{32,40},{33,41},{64,72},{65,73},{96,104},{97,105},{128... | collective-permute-start | bytes 393224 | tf_op jit(solution)/shard_map/ppermute | solution.py:26
  138.0 15.1 %collective-permute-start.4 = (bf16[128,512]{1,0:T(8,128)(2,1)}, bf16[128,512]{1,0:T(8,128)(2,1)S(1)}, u32[]{:S(2)}, u32[]{:S(2)}) collective-permute-start(bf16[128,512]{1,0:T(8,128)(2,1)} %get-tuple-element.13), channel_id=1, source_target_pairs={{0,12},{1,13},{32,44},{33,45},{64,76},{65,77},{96,108},{97,109},{1... | collective-permute-start | bytes 393224 | tf_op jit(solution)/shard_map/ppermute | solution.py:26
  139.3 13.7 %collective-permute-start.5 = (bf16[128,512]{1,0:T(8,128)(2,1)}, bf16[128,512]{1,0:T(8,128)(2,1)S(1)}, u32[]{:S(2)}, u32[]{:S(2)}) collective-permute-start(bf16[128,512]{1,0:T(8,128)(2,1)} %get-tuple-element.14), channel_id=1, source_target_pairs={{0,16},{1,17},{32,48},{33,49},{64,80},{65,81},{96,112},{97,113},{1... | collective-permute-start | bytes 393224 | tf_op jit(solution)/shard_map/ppermute | solution.py:26
  140.6 12.4 %collective-permute-start.6 = (bf16[128,512]{1,0:T(8,128)(2,1)S(1)}, bf16[128,512]{1,0:T(8,128)(2,1)S(1)}, u32[]{:S(2)}, u32[]{:S(2)}) collective-permute-start(bf16[128,512]{1,0:T(8,128)(2,1)S(1)} %get-tuple-element.15), channel_id=1, source_target_pairs={{0,20},{1,21},{32,52},{33,53},{64,84},{65,85},{96,116},{97,117},{1... | collective-permute-start | bytes 393224 | tf_op jit(solution)/shard_map/ppermute | solution.py:26
  141.9 11.1 %collective-permute-start.7 = (bf16[128,512]{1,0:T(8,128)(2,1)S(1)}, bf16[128,512]{1,0:T(8,128)(2,1)S(1)}, u32[]{:S(2)}, u32[]{:S(2)}) collective-permute-start(bf16[128,512]{1,0:T(8,128)(2,1)S(1)} %get-tuple-element.16), channel_id=1, source_target_pairs={{0,24},{1,25},{32,56},{33,57},{64,88},{65,89},{96,120},{97,121},{1... | collective-permute-start | bytes 393224 | tf_op jit(solution)/shard_map/ppermute | solution.py:26
  143.2 12.5 %collective-permute-start.8 = (bf16[128,512]{1,0:T(8,128)(2,1)S(1)}, bf16[128,512]{1,0:T(8,128)(2,1)S(1)}, u32[]{:S(2)}, u32[]{:S(2)}) collective-permute-start(bf16[128,512]{1,0:T(8,128)(2,1)S(1)} %get-tuple-element.17), channel_id=1, source_target_pairs={{0,28},{1,29},{32,60},{33,61},{64,92},{65,93},{96,124},{97,125},{1... | collective-permute-start | bytes 393224 | tf_op jit(solution)/shard_map/ppermute | solution.py:26
  156.7 4.6 %collective-permute-start.10 = (bf16[32,512]{1,0:T(8,128)(2,1)S(1)}, bf16[32,512]{1,0:T(8,128)(2,1)S(1)}, u32[]{:S(2)}, u32[]{:S(2)}) collective-permute-start(bf16[32,512]{1,0:T(8,128)(2,1)S(1)} %get-tuple-element.23), channel_id=1, source_target_pairs={{0,2},{1,3},{4,6},{5,7},{8,10},{9,11},{12,14},{13,15},{16,18},{17,... | collective-permute-start | bytes 98312 | tf_op jit(solution)/shard_map/ppermute | solution.py:34
  158.0 3.3 %collective-permute-start.11 = (bf16[32,512]{1,0:T(8,128)(2,1)S(1)}, bf16[32,512]{1,0:T(8,128)(2,1)S(1)}, u32[]{:S(2)}, u32[]{:S(2)}) collective-permute-start(bf16[32,512]{1,0:T(8,128)(2,1)S(1)} %get-tuple-element.22), channel_id=1, source_target_pairs={{0,1},{1,2},{4,5},{5,6},{8,9},{9,10},{12,13},{13,14},{16,17},{17,1... | collective-permute-start | bytes 98312 | tf_op jit(solution)/shard_map/ppermute | solution.py:34
  159.3 5.8 %collective-permute-start.9 = (bf16[32,512]{1,0:T(8,128)(2,1)S(1)}, bf16[32,512]{1,0:T(8,128)(2,1)S(1)}, u32[]{:S(2)}, u32[]{:S(2)}) collective-permute-start(bf16[32,512]{1,0:T(8,128)(2,1)S(1)} %get-tuple-element.24), channel_id=1, source_target_pairs={{0,3},{1,0},{4,7},{5,4},{8,11},{9,8},{12,15},{13,12},{16,19},{17,1... | collective-permute-start | bytes 98312 | tf_op jit(solution)/shard_map/ppermute | solution.py:34
Sparse Core Ops, SparseCore 0:
  20.1 90.3 all-gather.1

commit v5 on v4

--- a/solution.py
+++ b/solution.py
@@ -6,6 +6,7 @@
 from jax.sharding import Mesh, PartitionSpec as P
 
 NT = 16
+ROW = ("chip", "core")
 COL = ("xhi", "z")
 BF = jnp.bfloat16
 SWAP_Z = [(i, i ^ 1) for i in range(16)]
@@ -20,28 +21,27 @@
 
 def spread(updated, parts, col_at):
     share = updated.shape[0] // 32
-    part = 4 * share
     sent = []
-    for m in range(7, 0, -1):
-        block = lax.ppermute(parts[m - 1], COL, [(0, 4 * m), (1, 4 * m + 1)])
-        sent.append((col_at // 4 == m, block))
-    held = place(sent, updated[:part])
-    spot = col_at % 4
+    for m in (3, 2, 1):
+        block = lax.ppermute(parts[m - 1], COL, [(0, 8 * m), (1, 8 * m + 1)])
+        sent.append((col_at // 8 == m, block))
+    held = place(sent, updated[: 8 * share])
+    spot = col_at % 8
     got = []
-    for d in (1, 2, 3):
-        piece = lax.dynamic_slice_in_dim(held, (spot + d) % 4 * share, share, 0)
-        pairs = [(b + h, b + (h + d) % 4) for b in range(0, 32, 4) for h in (0, 1)]
+    for d in range(1, 8):
+        piece = lax.dynamic_slice_in_dim(held, (spot + d) % 8 * share, share, 0)
+        pairs = [(b + h, b + (h + d) % 8) for b in range(0, 32, 8) for h in (0, 1)]
         got.append(lax.ppermute(piece, COL, pairs))
     own = lax.dynamic_slice_in_dim(held, spot * share, share, 0)
-    left = place([(spot == d, got[d - 1]) for d in (1, 2, 3)], own)
-    right = place([((spot - 1) % 4 == d, got[d - 1]) for d in (1, 2, 3)], own)
+    left = place([(spot == d, got[d - 1]) for d in range(1, 8)], own)
+    right = place([((spot - 1) % 8 == d, got[d - 1]) for d in range(1, 8)], own)
     return jnp.concatenate([left, right], axis=1)
 
 
 def update_kernel(
     x_at_ref, left_ref, upper_ref, cols_ref, p_ref, q_ref, trailing_ref, out_ref, *rest
 ):
-    parts, (outer_ref, inner_ref, weights_ref, q_held, dense_ref, sems) = rest[:7], rest[7:]
+    parts, (outer_ref, inner_ref, weights_ref, q_held, dense_ref, sems) = rest[:3], rest[3:]
     rank_pad = p_ref.shape[2]
     depth = cols_ref.shape[4]
     copies = []
@@ -57,13 +57,20 @@
         for h in range(2):
             fetch(cols_ref.at[2 * zz + h, :, 0], outer_ref.at[zz, :, h])
     fetch(trailing_ref, dense_ref)
-    for copy in copies:
+    for copy in copies[:12]:
         copy.start()
     t = lax.broadcasted_iota(jnp.int32, (rank_pad, rank_pad), 0)
     u = lax.broadcasted_iota(jnp.int32, (rank_pad, rank_pad), 1)
     for zz in range(8):
         for copy in copies[3 * zz : 3 * zz + 3]:
             copy.wait()
+        if zz < 4:
+            for copy in copies[3 * zz + 12 : 3 * zz + 15]:
+                copy.start()
+        for copy in copies[2 * zz + 24 : 2 * zz + 26]:
+            copy.start()
+        if zz == 7:
+            copies[40].start()
         for slot in range(2):
             xhi = slot ^ x_at_ref[0]
             k = xhi * 8 + zz
@@ -84,8 +91,8 @@
     product = lax.dot_general(outer, weights_ref[...], (((0,), (0,)), ((), ())), preferred_element_type=jnp.float32)
     done = (dense_ref[...].astype(jnp.float32) - product).astype(BF)
     out_ref[...] = done
-    part = done.shape[0] // 8
-    for m in range(1, 8):
+    part = done.shape[0] // 4
+    for m in range(1, 4):
         parts[m - 1][...] = done[m * part : (m + 1) * part]
 
 
@@ -97,9 +104,9 @@
     held = pltpu.VMEM((8, 2, 2, half, depth), BF)
     return pl.pallas_call(
         update_kernel,
-        out_shape=[jax.ShapeDtypeStruct((height, width), BF)] + [jax.ShapeDtypeStruct((height // 8, width), BF)] * 7,
+        out_shape=[jax.ShapeDtypeStruct((height, width), BF)] + [jax.ShapeDtypeStruct((height // 4, width), BF)] * 3,
         in_specs=[smem, smem, smem, hbm, vmem, hbm, hbm],
-        out_specs=[vmem] * 8,
+        out_specs=[vmem] * 4,
         scratch_shapes=[held, held, pltpu.VMEM((NT * rank_pad, width), BF), pltpu.VMEM(q_rows.shape, BF), pltpu.VMEM(trailing.shape, BF), pltpu.SemaphoreType.DMA((41,))],
         compiler_params=pltpu.CompilerParams(vmem_limit_bytes=LIMIT << 20),
     )(
@@ -114,25 +121,32 @@
 
 
 def body(trailing, left_outer, left_inner, upper_outer, upper_inner, left_ranks, upper_ranks):
-    row_at = lax.axis_index("row")
+    core_at = lax.axis_index("core")
+    row_at = lax.axis_index("chip") * 2 + core_at
     x_at, z_at = lax.axis_index("xhi"), lax.axis_index("z")
     col_at = x_at * 16 + z_at
-    half = left_outer.shape[0]
+    half, depth = left_outer.shape
 
     mine = jnp.concatenate([left_outer, left_inner], axis=0)
     other = lax.ppermute(mine, "xhi", [(0, 1), (1, 0)])
+    partner = lax.ppermute(upper_outer, "z", SWAP_Z)
     cols = lax.all_gather(jnp.concatenate([mine, other], axis=0), "z", axis=0, tiled=True)
     cols = cols.reshape(NT, 2, 2, half, -1)
 
-    partner = lax.ppermute(upper_outer, "z", SWAP_Z)
     even = z_at % 2 == 0
     rows = jnp.concatenate(
         [jnp.where(even, upper_outer, partner), jnp.where(even, partner, upper_outer), upper_inner], axis=1
     )
-    rows = lax.all_to_all(jnp.broadcast_to(rows[None], (NT,) + rows.shape), "row", 0, 0)
-    rows = rows.reshape((2, 8) + rows.shape[1:])
-    depth = cols.shape[-1]
-    p_rows, q_rows = rows[..., :depth], rows[..., depth:]
+    rows = lax.all_to_all(jnp.broadcast_to(rows[None], (NT // 2,) + rows.shape), "chip", 0, 0)
+    across = lax.ppermute(rows, "core", [(0, 1), (1, 0)])
+    lower = core_at == 0
+
+    def whole(own, far):
+        both = jnp.stack([jnp.where(lower, own, far), jnp.where(lower, far, own)], axis=1)
+        return both.reshape((2, 8) + own.shape[1:])
+
+    p_rows = whole(rows[..., :depth], across[..., :depth])
+    q_rows = whole(rows[..., depth:], across[..., depth:])
 
     left = lax.dynamic_index_in_dim(left_ranks, row_at, 0, keepdims=False)
     upper = lax.dynamic_index_in_dim(upper_ranks, col_at // 2, 1, keepdims=False)
@@ -141,13 +155,13 @@
 
 
 def solution(mesh):
-    fine = Mesh(mesh.devices.reshape(16, 2, 16), ("row", "xhi", "z"))
-    grid = P("row", COL)
-    turned = P(COL, "row")
+    fine = Mesh(mesh.devices.reshape(8, 2, 2, 16), ("chip", "core", "xhi", "z"))
+    grid = P(ROW, COL)
+    turned = P(COL, ROW)
     return jax.shard_map(
         body,
         mesh=fine,
         in_specs=(grid, turned, turned, grid, grid, P(), P()),
-        out_specs=(grid, P(("row",) + COL, None)),
+        out_specs=(grid, P(ROW + COL, None)),
         check_vma=False,
     )

time: 173 us -> 167 us (0.965)
  the two profiles are of different devices: /device:TPU:26 before, /device:TPU:422 now
where the time goes in v5:
time: 167 us
  waiting for transfers between devices  80.3 us (48%)
  blocking collectives  32 us (19%)
  starting transfers between devices  16.1 us (10%)
  between operations  14.5 us (9%)
  Pallas kernels  11.2 us (7%)
  other arithmetic  11 us (7%)
    ppermute x7, waiting for transfers between devices, spread(): got.append(lax.ppermute(piece, COL, pairs))  35.2 us
    all_to_all x1, blocking collectives, body(): lax.all_to_all(jnp.broadcast_to(rows[None], (NT // 2,) + rows.shape), 'ch...  32 us
    all_gather x1, waiting for transfers between devices, body(): lax.all_gather(jnp.concatenate([mine, other], axis=0), 'z', axis=0, tiled...  30.9 us
    pallas_call x1, Pallas kernels, update(): pl.pallas_call(update_kernel, out_shape=[jax.ShapeDtypeStruct((height, wi...  11.2 us
    ppermute x1, waiting for transfers between devices, body(): other = lax.ppermute(mine, 'xhi', [(0, 1), (1, 0)])  6.72 us
    ppermute x7, starting transfers between devices, spread(): got.append(lax.ppermute(piece, COL, pairs))  5.9 us
    another operation x4, other arithmetic, whole(): jnp.stack([jnp.where(lower, own, far), jnp.where(lower, far, own)], axis=1)  4.74 us
    ppermute x1, waiting for transfers between devices, body(): partner = lax.ppermute(upper_outer, 'z', SWAP_Z)  3.78 us
  transfers between devices with their start and end apart: 14, of which 6 were waited for; matrix products, arithmetic and copies ran while one was open for 5% of the time, Pallas kernels for 0%

profile of v5, /device:TPU:422, one launch (start us, length us, event | category | flops | bytes accessed | tf_op | source)
XLA Modules:
  0.0 166.6 jit_solution(14338414755480675581)
XLA Ops:
  7.2 1.0 pad_maximum_fusion.4
  8.2 3.3 %collective-permute-start = (bf16[96,1024]{1,0:T(8,128)(2,1)S(1)}, bf16[96,1024]{1,0:T(8,128)(2,1)S(1)}, u32[]{:S(2)}, u32[]{:S(2)}) collective-permute-start(bf16[96,1024]{1,0:T(8,128)(2,1)S(1)} %pad_maximum_fusion.4), channel_id=1, source_target_pairs={{0,16},{16,0},{1,17},{17,1},{2,18},{18,2},{3,19},{19,3},{4,20},{20... | collective-permute-start | bytes 589832 | tf_op jit(solution)/shard_map/ppermute | solution.py:131
  11.5 6.7 %collective-permute-done = bf16[96,1024]{1,0:T(8,128)(2,1)S(1)} collective-permute-done((bf16[96,1024]{1,0:T(8,128)(2,1)S(1)}, bf16[96,1024]{1,0:T(8,128)(2,1)S(1)}, u32[]{:S(2)}, u32[]{:S(2)}) %collective-permute-start) | collective-permute-done | bytes 196640 | tf_op jit(solution)/shard_map/ppermute | solution.py:131
  18.2 1.7 %pad_maximum_fusion.2 = bf16[192,1024]{1,0:T(8,128)(2,1)} fusion(bf16[96,1024]{1,0:T(8,128)(2,1)S(1)} %collective-permute-done, bf16[48,1024]{1,0:T(8,128)(2,1)} %param.9, bf16[48,1024]{1,0:T(8,128)(2,1)} %param.8), kind=kLoop, calls=%fused_computation.6 | loop fusion | flops 1179648 | bytes 786432 | tf_op jit(solution)/shard_map/concatenate | solution.py:133
  20.0 2.9 %collective-permute-start.1 = (bf16[96,512]{1,0:T(8,128)(2,1)}, bf16[96,512]{1,0:T(8,128)(2,1)S(1)}, u32[]{:S(2)}, u32[]{:S(2)}) collective-permute-start(bf16[96,512]{1,0:T(8,128)(2,1)} %param.10), channel_id=1, source_target_pairs={{0,1},{1,0},{2,3},{3,2},{4,5},{5,4},{6,7},{7,6},{8,9},{9,8},{10,11... | collective-permute-start | bytes 294920 | tf_op jit(solution)/shard_map/ppermute | solution.py:132
  22.9 3.8 %collective-permute-done.1 = bf16[96,512]{1,0:T(8,128)(2,1)S(1)} collective-permute-done((bf16[96,512]{1,0:T(8,128)(2,1)}, bf16[96,512]{1,0:T(8,128)(2,1)S(1)}, u32[]{:S(2)}, u32[]{:S(2)}) %collective-permute-start.1) | collective-permute-done | bytes 98336 | tf_op jit(solution)/shard_map/ppermute | solution.py:132
  26.7 0.9 broadcast_select_fusion.1
  27.6 0.9 pad_maximum_fusion.3
  28.7 32.0 %all_to_all.5 = bf16[8,96,1536]{2,1,0:T(8,128)(2,1)S(1)} all-to-all(bf16[8,96,1536]{2,1,0:T(8,128)(2,1)S(1)} %broadcast_in_dim.2), channel_id=1, replica_groups=mesh['chip'=8,'core'=2,'xhi'=2,'z'=16] {'chip'}, dimensions={0} | all-to-all | bytes 4718592 | tf_op jit(solution)/shard_map/all_to_all | solution.py:140
  60.7 1.9 %collective-permute-start.2 = (bf16[8,96,1536]{2,1,0:T(8,128)(2,1)S(1)}, bf16[8,96,1536]{2,1,0:T(8,128)(2,1)}, u32[]{:S(2)}, u32[]{:S(2)}) collective-permute-start(bf16[8,96,1536]{2,1,0:T(8,128)(2,1)S(1)} %all_to_all.5), channel_id=1, source_target_pairs={{0,32},{32,0},{1,33},{33,1},{2,34},{34,2},{3,35},{35,3},{4,36},{36... | collective-permute-start | bytes 7077896 | tf_op jit(solution)/shard_map/ppermute | solution.py:141
  62.9 0.7 fusion.left_ref
  63.5 3.7 %collective-permute-done.2 = bf16[8,96,1536]{2,1,0:T(8,128)(2,1)} collective-permute-done((bf16[8,96,1536]{2,1,0:T(8,128)(2,1)S(1)}, bf16[8,96,1536]{2,1,0:T(8,128)(2,1)}, u32[]{:S(2)}, u32[]{:S(2)}) %collective-permute-start.2) | collective-permute-done | bytes 2359328 | tf_op jit(solution)/shard_map/ppermute | solution.py:141
  67.3 1.6 select_bitcast_fusion.1
  69.2 0.3 copy.11
  69.5 1.5 select_bitcast_fusion.3
  71.1 1.3 pad_maximum_fusion.1
  72.3 30.9 %all-gather.2.cloned.1.call-done = bf16[3072,1024]{1,0:T(8,128)(2,1)} async-done(((bf16[192,1024]{1,0:T(8,128)(2,1)}), bf16[3072,1024]{1,0:T(8,128)(2,1)}) %all-gather.2.cloned.1.call-update) | async-done | bytes 6291472 | tf_op jit(solution)/shard_map/all_gather | solution.py:133
  103.2 11.2 %shard_map.86 = (bf16[1024,512]{1,0:T(8,128)(2,1)}, bf16[256,512]{1,0:T(8,128)(2,1)}, bf16[256,512]{1,0:T(8,128)(2,1)}, bf16[256,512]{1,0:T(8,128)(2,1)S(1)}) custom-call(s32[1]{0:T(128)} %bitcast.x_at_ref, s32[16]{0:T(128)S(1)} %fusion.left_ref, s32[16]{0:T(128)S(1)} %dynamic-slice_reduce_fusion.upper_ref, bf16[16,2,2,48,1024]{4,3,2,1,0:T(8,128)(2,1)} %bitcast.17, ...), custom_call_target="tpu_custom_call" | custom-call | tf_op jit(solution)/shard_map/pallas_call | solution.py:105
  114.5 0.7 collective-permute-start.3
  115.2 0.7 collective-permute-start.4
  115.8 0.7 collective-permute-start.5
  116.7 1.0 select_select_fusion
  117.8 0.7 collective-permute-start.10
  118.5 0.7 collective-permute-start.11
  119.1 0.7 collective-permute-start.12
  119.8 0.7 collective-permute-start.6
  120.5 0.7 collective-permute-start.7
  121.2 1.3 collective-permute-start.8
  122.5 1.3 collective-permute-start.9
  123.9 33.2 %collective-permute-done.8 = bf16[32,512]{1,0:T(8,128)(2,1)S(1)} collective-permute-done((bf16[32,512]{1,0:T(8,128)(2,1)S(1)}, bf16[32,512]{1,0:T(8,128)(2,1)S(1)}, u32[]{:S(2)}, u32[]{:S(2)}) %collective-permute-start.8) | collective-permute-done | bytes 32800 | tf_op jit(solution)/shard_map/ppermute | solution.py:34
  157.1 1.9 %collective-permute-done.9 = bf16[32,512]{1,0:T(8,128)(2,1)S(1)} collective-permute-done((bf16[32,512]{1,0:T(8,128)(2,1)S(1)}, bf16[32,512]{1,0:T(8,128)(2,1)S(1)}, u32[]{:S(2)}, u32[]{:S(2)}) %collective-permute-start.9) | collective-permute-done | bytes 32800 | tf_op jit(solution)/shard_map/ppermute | solution.py:34
  159.1 0.6 pad_maximum_fusion.5
  (20 shorter events, 0.9 us)
Async XLA Ops:
  7.2 55.5 %copy-start = (s32[16,16]{1,0:T(8,128)S(1)}, s32[16,16]{1,0:T(8,128)}, u32[]{:S(2)}) copy-start(s32[16,16]{1,0:T(8,128)} %param.13) | copy-start | bytes 3076
  7.2 96.0 %all-gather.2.cloned.1.call-start = ((), (), s32[]{:S(2)}) async-start(), calls=%async_computation.1 | async-start | bytes 6684672 | tf_op jit(solution)/shard_map/all_gather | solution.py:133
  8.2 10.0 %collective-permute-start = (bf16[96,1024]{1,0:T(8,128)(2,1)S(1)}, bf16[96,1024]{1,0:T(8,128)(2,1)S(1)}, u32[]{:S(2)}, u32[]{:S(2)}) collective-permute-start(bf16[96,1024]{1,0:T(8,128)(2,1)S(1)} %pad_maximum_fusion.4), channel_id=1, source_target_pairs={{0,16},{16,0},{1,17},{17,1},{2,18},{18,2},{3,19},{19,3},{4,20},{20... | collective-permute-start | bytes 589832 | tf_op jit(solution)/shard_map/ppermute | solution.py:131
  20.0 6.7 %collective-permute-start.1 = (bf16[96,512]{1,0:T(8,128)(2,1)}, bf16[96,512]{1,0:T(8,128)(2,1)S(1)}, u32[]{:S(2)}, u32[]{:S(2)}) collective-permute-start(bf16[96,512]{1,0:T(8,128)(2,1)} %param.10), channel_id=1, source_target_pairs={{0,1},{1,0},{2,3},{3,2},{4,5},{5,4},{6,7},{7,6},{8,9},{9,8},{10,11... | collective-permute-start | bytes 294920 | tf_op jit(solution)/shard_map/ppermute | solution.py:132
  60.7 8.2 %copy-start.1 = (bf16[8,96,1536]{2,1,0:T(8,128)(2,1)}, bf16[8,96,1536]{2,1,0:T(8,128)(2,1)S(1)}, u32[]{:S(2)}) copy-start(bf16[8,96,1536]{2,1,0:T(8,128)(2,1)S(1)} %all_to_all.5) | copy-start | bytes 7077892
  60.7 6.5 %collective-permute-start.2 = (bf16[8,96,1536]{2,1,0:T(8,128)(2,1)S(1)}, bf16[8,96,1536]{2,1,0:T(8,128)(2,1)}, u32[]{:S(2)}, u32[]{:S(2)}) collective-permute-start(bf16[8,96,1536]{2,1,0:T(8,128)(2,1)S(1)} %all_to_all.5), channel_id=1, source_target_pairs={{0,32},{32,0},{1,33},{33,1},{2,34},{34,2},{3,35},{35,3},{4,36},{36... | collective-permute-start | bytes 7077896 | tf_op jit(solution)/shard_map/ppermute | solution.py:141
  114.5 2.2 %collective-permute-start.3 = (bf16[256,512]{1,0:T(8,128)(2,1)}, bf16[256,512]{1,0:T(8,128)(2,1)S(1)}, u32[]{:S(2)}, u32[]{:S(2)}) collective-permute-start(bf16[256,512]{1,0:T(8,128)(2,1)} %get-tuple-element.7), channel_id=1, source_target_pairs={{0,8},{1,9},{32,40},{33,41},{64,72},{65,73},{96,104},{97,105},{128... | collective-permute-start | bytes 786440 | tf_op jit(solution)/shard_map/ppermute | solution.py:26
  115.2 1.5 collective-permute-start.4
  115.8 0.9 collective-permute-start.5
  117.8 3.4 %collective-permute-start.10 = (bf16[32,512]{1,0:T(8,128)(2,1)S(1)}, bf16[32,512]{1,0:T(8,128)(2,1)S(1)}, u32[]{:S(2)}, u32[]{:S(2)}) collective-permute-start(bf16[32,512]{1,0:T(8,128)(2,1)S(1)} %get-tuple-element.16), channel_id=1, source_target_pairs={{0,3},{1,4},{8,11},{9,12},{16,19},{17,20},{24,27},{25,28},{32,35},... | collective-permute-start | bytes 98312 | tf_op jit(solution)/shard_map/ppermute | solution.py:34
  118.5 4.0 %collective-permute-start.11 = (bf16[32,512]{1,0:T(8,128)(2,1)S(1)}, bf16[32,512]{1,0:T(8,128)(2,1)S(1)}, u32[]{:S(2)}, u32[]{:S(2)}) collective-permute-start(bf16[32,512]{1,0:T(8,128)(2,1)S(1)} %get-tuple-element.15), channel_id=1, source_target_pairs={{0,2},{1,3},{8,10},{9,11},{16,18},{17,19},{24,26},{25,27},{32,34},... | collective-permute-start | bytes 98312 | tf_op jit(solution)/shard_map/ppermute | solution.py:34
  119.1 4.7 %collective-permute-start.12 = (bf16[32,512]{1,0:T(8,128)(2,1)S(1)}, bf16[32,512]{1,0:T(8,128)(2,1)S(1)}, u32[]{:S(2)}, u32[]{:S(2)}) collective-permute-start(bf16[32,512]{1,0:T(8,128)(2,1)S(1)} %get-tuple-element.14), channel_id=1, source_target_pairs={{0,1},{1,2},{8,9},{9,10},{16,17},{17,18},{24,25},{25,26},{32,33},{... | collective-permute-start | bytes 98312 | tf_op jit(solution)/shard_map/ppermute | solution.py:34
  119.8 4.0 %collective-permute-start.6 = (bf16[32,512]{1,0:T(8,128)(2,1)S(1)}, bf16[32,512]{1,0:T(8,128)(2,1)S(1)}, u32[]{:S(2)}, u32[]{:S(2)}) collective-permute-start(bf16[32,512]{1,0:T(8,128)(2,1)S(1)} %get-tuple-element.20), channel_id=1, source_target_pairs={{0,7},{1,0},{8,15},{9,8},{16,23},{17,16},{24,31},{25,24},{32,39},{... | collective-permute-start | bytes 98312 | tf_op jit(solution)/shard_map/ppermute | solution.py:34
  120.5 3.4 %collective-permute-start.7 = (bf16[32,512]{1,0:T(8,128)(2,1)S(1)}, bf16[32,512]{1,0:T(8,128)(2,1)S(1)}, u32[]{:S(2)}, u32[]{:S(2)}) collective-permute-start(bf16[32,512]{1,0:T(8,128)(2,1)S(1)} %get-tuple-element.19), channel_id=1, source_target_pairs={{0,6},{1,7},{8,14},{9,15},{16,22},{17,23},{24,30},{25,31},{32,38},... | collective-permute-start | bytes 98312 | tf_op jit(solution)/shard_map/ppermute | solution.py:34
  121.2 35.9 %collective-permute-start.8 = (bf16[32,512]{1,0:T(8,128)(2,1)S(1)}, bf16[32,512]{1,0:T(8,128)(2,1)S(1)}, u32[]{:S(2)}, u32[]{:S(2)}) collective-permute-start(bf16[32,512]{1,0:T(8,128)(2,1)S(1)} %get-tuple-element.18), channel_id=1, source_target_pairs={{0,5},{1,6},{8,13},{9,14},{16,21},{17,22},{24,29},{25,30},{32,37},... | collective-permute-start | bytes 98312 | tf_op jit(solution)/shard_map/ppermute | solution.py:34
  122.5 36.5 %collective-permute-start.9 = (bf16[32,512]{1,0:T(8,128)(2,1)S(1)}, bf16[32,512]{1,0:T(8,128)(2,1)S(1)}, u32[]{:S(2)}, u32[]{:S(2)}) collective-permute-start(bf16[32,512]{1,0:T(8,128)(2,1)S(1)} %get-tuple-element.17), channel_id=1, source_target_pairs={{0,4},{1,5},{8,12},{9,13},{16,20},{17,21},{24,28},{25,29},{32,36},... | collective-permute-start | bytes 98312 | tf_op jit(solution)/shard_map/ppermute | solution.py:34
Sparse Core Ops, SparseCore 0:
  20.1 83.0 all-gather.1

commit v6 on v5

--- a/solution.py
+++ b/solution.py
@@ -10,7 +10,7 @@
 COL = ("xhi", "z")
 BF = jnp.bfloat16
 SWAP_Z = [(i, i ^ 1) for i in range(16)]
-LIMIT = 28
+LIMIT = 20
 
 
 def place(branches, default):
@@ -39,7 +39,7 @@
 
 
 def update_kernel(
-    x_at_ref, left_ref, upper_ref, cols_ref, p_ref, q_ref, trailing_ref, out_ref, *rest
+    left_ref, upper_ref, cols_ref, p_ref, q_ref, trailing_ref, out_ref, *rest
 ):
     parts, (outer_ref, inner_ref, weights_ref, q_held, dense_ref, sems) = rest[:3], rest[3:]
     rank_pad = p_ref.shape[2]
@@ -57,31 +57,23 @@
         for h in range(2):
             fetch(cols_ref.at[2 * zz + h, :, 0], outer_ref.at[zz, :, h])
     fetch(trailing_ref, dense_ref)
-    for copy in copies[:12]:
+    for copy in copies:
         copy.start()
     t = lax.broadcasted_iota(jnp.int32, (rank_pad, rank_pad), 0)
     u = lax.broadcasted_iota(jnp.int32, (rank_pad, rank_pad), 1)
     for zz in range(8):
         for copy in copies[3 * zz : 3 * zz + 3]:
             copy.wait()
-        if zz < 4:
-            for copy in copies[3 * zz + 12 : 3 * zz + 15]:
-                copy.start()
-        for copy in copies[2 * zz + 24 : 2 * zz + 26]:
-            copy.start()
-        if zz == 7:
-            copies[40].start()
-        for slot in range(2):
-            xhi = slot ^ x_at_ref[0]
+        for xhi in range(2):
             k = xhi * 8 + zz
             core = lax.dot_general(
-                inner_ref[zz, slot].reshape(rank_pad, depth),
+                inner_ref[zz, xhi].reshape(rank_pad, depth),
                 p_ref[xhi, zz],
                 (((1,), (1,)), ((), ())),
                 preferred_element_type=jnp.float32,
             )
             core = jnp.where((t < left_ref[k]) & (u < upper_ref[k]), core, 0.0).astype(BF)
-            at = (2 * zz + slot) * rank_pad
+            at = (2 * zz + xhi) * rank_pad
             weights_ref[at : at + rank_pad, :] = jnp.dot(
                 core, q_held[xhi, zz], preferred_element_type=jnp.float32
             ).astype(BF)
@@ -96,7 +88,7 @@
         parts[m - 1][...] = done[m * part : (m + 1) * part]
 
 
-def update(x_at, left, upper, cols, p_rows, q_rows, trailing):
+def update(left, upper, cols, p_rows, q_rows, trailing):
     height, width = trailing.shape
     rank_pad, depth, half = p_rows.shape[2], cols.shape[4], cols.shape[3]
     vmem, smem = pl.BlockSpec(memory_space=pltpu.VMEM), pl.BlockSpec(memory_space=pltpu.SMEM)
@@ -105,12 +97,11 @@
     return pl.pallas_call(
         update_kernel,
         out_shape=[jax.ShapeDtypeStruct((height, width), BF)] + [jax.ShapeDtypeStruct((height // 4, width), BF)] * 3,
-        in_specs=[smem, smem, smem, hbm, vmem, hbm, hbm],
+        in_specs=[smem, smem, hbm, vmem, hbm, hbm],
         out_specs=[vmem] * 4,
         scratch_shapes=[held, held, pltpu.VMEM((NT * rank_pad, width), BF), pltpu.VMEM(q_rows.shape, BF), pltpu.VMEM(trailing.shape, BF), pltpu.SemaphoreType.DMA((41,))],
         compiler_params=pltpu.CompilerParams(vmem_limit_bytes=LIMIT << 20),
     )(
-        x_at,
         left,
         upper,
         pltpu.with_memory_space_constraint(cols, pltpu.HBM),
@@ -127,10 +118,10 @@
     col_at = x_at * 16 + z_at
     half, depth = left_outer.shape
 
-    mine = jnp.concatenate([left_outer, left_inner], axis=0)
-    other = lax.ppermute(mine, "xhi", [(0, 1), (1, 0)])
+    both = jnp.concatenate([left_outer, left_inner], axis=0)
+    both = lax.all_gather(both, "xhi", axis=0, tiled=True)
     partner = lax.ppermute(upper_outer, "z", SWAP_Z)
-    cols = lax.all_gather(jnp.concatenate([mine, other], axis=0), "z", axis=0, tiled=True)
+    cols = lax.all_gather(both, "z", axis=0, tiled=True)
     cols = cols.reshape(NT, 2, 2, half, -1)
 
     even = z_at % 2 == 0
@@ -150,7 +141,7 @@
 
     left = lax.dynamic_index_in_dim(left_ranks, row_at, 0, keepdims=False)
     upper = lax.dynamic_index_in_dim(upper_ranks, col_at // 2, 1, keepdims=False)
-    updated, *parts = update(x_at.reshape(1).astype(jnp.int32), left, upper, cols, p_rows, q_rows, trailing)
+    updated, *parts = update(left, upper, cols, p_rows, q_rows, trailing)
     return updated, spread(updated, parts, col_at)
 
 

time: 167 us -> 163 us (0.976)
  the two profiles are of different devices: /device:TPU:422 before, /device:TPU:390 now
where the time goes in v6:
time: 163 us; the launch traced here: 162 us
  waiting for transfers between devices  73.1 us (45%)
  blocking collectives  40.9 us (25%)
  between operations  14.5 us (9%)
  starting transfers between devices  12.8 us (8%)
  Pallas kernels  9.98 us (6%)
  other arithmetic  9.24 us (6%)
    ppermute x7, waiting for transfers between devices, spread(): got.append(lax.ppermute(piece, COL, pairs))  34.3 us
    all_to_all x1, blocking collectives, body(): lax.all_to_all(jnp.broadcast_to(rows[None], (NT // 2,) + rows.shape), 'ch...  32 us
    all_gather x1, waiting for transfers between devices, body(): cols = lax.all_gather(both, 'z', axis=0, tiled=True)  31.3 us
    pallas_call x1, Pallas kernels, update(): pl.pallas_call(update_kernel, out_shape=[jax.ShapeDtypeStruct((height, wi...  9.98 us
    all_gather x1, blocking collectives, body(): both = lax.all_gather(both, 'xhi', axis=0, tiled=True)  8.93 us
    ppermute x7, starting transfers between devices, spread(): got.append(lax.ppermute(piece, COL, pairs))  5.9 us
    another operation x4, other arithmetic, whole(): jnp.stack([jnp.where(lower, own, far), jnp.where(lower, far, own)], axis=1)  4.7 us
    ppermute x1, waiting for transfers between devices, body(): partner = lax.ppermute(upper_outer, 'z', SWAP_Z)  3.77 us
  transfers between devices with their start and end apart: 13, of which 5 were waited for; matrix products, arithmetic and copies ran while one was open for 5% of the time, Pallas kernels for 0%

profile of v6, /device:TPU:390, one launch (start us, length us, event | category | flops | bytes accessed | tf_op | source)
XLA Modules:
  0.0 162.0 jit_solution(6088680973407922919)
XLA Ops:
  7.2 1.0 pad_maximum_fusion.3
  8.2 8.9 %all_gather.6 = bf16[192,1024]{1,0:T(8,128)(2,1)} all-gather(bf16[96,1024]{1,0:T(8,128)(2,1)S(1)} %pad_maximum_fusion.3), channel_id=1, replica_groups=mesh['chip'=8,'core'=2,'xhi'=2,'z'=16] {'xhi'}, dimensions={0}, use_global_device_ids=true | all-gather | bytes 589824 | tf_op jit(solution)/shard_map/all_gather | solution.py:122
  17.1 2.9 %collective-permute-start = (bf16[96,512]{1,0:T(8,128)(2,1)}, bf16[96,512]{1,0:T(8,128)(2,1)S(1)}, u32[]{:S(2)}, u32[]{:S(2)}) collective-permute-start(bf16[96,512]{1,0:T(8,128)(2,1)} %param.10), channel_id=1, source_target_pairs={{0,1},{1,0},{2,3},{3,2},{4,5},{5,4},{6,7},{7,6},{8,9},{9,8},{10,11... | collective-permute-start | bytes 294920 | tf_op jit(solution)/shard_map/ppermute | solution.py:123
  20.1 3.8 %collective-permute-done = bf16[96,512]{1,0:T(8,128)(2,1)S(1)} collective-permute-done((bf16[96,512]{1,0:T(8,128)(2,1)}, bf16[96,512]{1,0:T(8,128)(2,1)S(1)}, u32[]{:S(2)}, u32[]{:S(2)}) %collective-permute-start) | collective-permute-done | bytes 98336 | tf_op jit(solution)/shard_map/ppermute | solution.py:123
  23.9 0.9 broadcast_select_fusion.1
  24.8 0.9 pad_maximum_fusion.2
  25.7 0.2 broadcast_in_dim.2
  25.9 32.0 %all_to_all.5 = bf16[8,96,1536]{2,1,0:T(8,128)(2,1)S(1)} all-to-all(bf16[8,96,1536]{2,1,0:T(8,128)(2,1)S(1)} %broadcast_in_dim.2), channel_id=1, replica_groups=mesh['chip'=8,'core'=2,'xhi'=2,'z'=16] {'chip'}, dimensions={0} | all-to-all | bytes 4718592 | tf_op jit(solution)/shard_map/all_to_all | solution.py:131
  57.9 1.9 %collective-permute-start.1 = (bf16[8,96,1536]{2,1,0:T(8,128)(2,1)S(1)}, bf16[8,96,1536]{2,1,0:T(8,128)(2,1)}, u32[]{:S(2)}, u32[]{:S(2)}) collective-permute-start(bf16[8,96,1536]{2,1,0:T(8,128)(2,1)S(1)} %all_to_all.5), channel_id=1, source_target_pairs={{0,32},{32,0},{1,33},{33,1},{2,34},{34,2},{3,35},{35,3},{4,36},{36... | collective-permute-start | bytes 7077896 | tf_op jit(solution)/shard_map/ppermute | solution.py:132
  60.0 0.7 fusion.left_ref
  60.7 3.7 %collective-permute-done.1 = bf16[8,96,1536]{2,1,0:T(8,128)(2,1)} collective-permute-done((bf16[8,96,1536]{2,1,0:T(8,128)(2,1)S(1)}, bf16[8,96,1536]{2,1,0:T(8,128)(2,1)}, u32[]{:S(2)}, u32[]{:S(2)}) %collective-permute-start.1) | collective-permute-done | bytes 2359328 | tf_op jit(solution)/shard_map/ppermute | solution.py:132
  64.4 1.6 select_bitcast_fusion.1
  66.1 0.3 pad_maximum_fusion
  66.4 0.3 copy.11
  66.7 1.5 select_bitcast_fusion.3
  68.2 1.3 pad_maximum_fusion.1
  69.5 31.3 %all-gather.2.cloned.1.call-done = bf16[3072,1024]{1,0:T(8,128)(2,1)} async-done(((bf16[192,1024]{1,0:T(8,128)(2,1)}), bf16[3072,1024]{1,0:T(8,128)(2,1)}) %all-gather.2.cloned.1.call-update) | async-done | bytes 6291472 | tf_op jit(solution)/shard_map/all_gather | solution.py:124
  100.8 10.0 %shard_map.86 = (bf16[1024,512]{1,0:T(8,128)(2,1)}, bf16[256,512]{1,0:T(8,128)(2,1)}, bf16[256,512]{1,0:T(8,128)(2,1)}, bf16[256,512]{1,0:T(8,128)(2,1)S(1)}) custom-call(s32[16]{0:T(128)S(1)} %fusion.left_ref, s32[16]{0:T(128)S(1)} %dynamic-slice_reduce_fusion.upper_ref, bf16[16,2,2,48,1024]{4,3,2,1,0:T(8,128)(2,1)} %bitcast.16, ...), custom_call_target="tpu_custom_call" | custom-call | tf_op jit(solution)/shard_map/pallas_call | solution.py:97
  110.7 0.7 collective-permute-start.2
  111.4 0.7 collective-permute-start.3
  112.1 0.7 collective-permute-start.4
  113.0 1.0 select_select_fusion
  114.1 0.7 collective-permute-start.10
  114.7 0.7 collective-permute-start.11
  115.4 0.7 collective-permute-start.5
  116.1 0.7 collective-permute-start.6
  116.8 0.7 collective-permute-start.7
  117.4 1.3 collective-permute-start.8
  118.7 1.3 collective-permute-start.9
  120.1 32.4 %collective-permute-done.8 = bf16[32,512]{1,0:T(8,128)(2,1)S(1)} collective-permute-done((bf16[32,512]{1,0:T(8,128)(2,1)S(1)}, bf16[32,512]{1,0:T(8,128)(2,1)S(1)}, u32[]{:S(2)}, u32[]{:S(2)}) %collective-permute-start.8) | collective-permute-done | bytes 32800 | tf_op jit(solution)/shard_map/ppermute | solution.py:34
  152.6 1.9 %collective-permute-done.9 = bf16[32,512]{1,0:T(8,128)(2,1)S(1)} collective-permute-done((bf16[32,512]{1,0:T(8,128)(2,1)S(1)}, bf16[32,512]{1,0:T(8,128)(2,1)S(1)}, u32[]{:S(2)}, u32[]{:S(2)}) %collective-permute-start.9) | collective-permute-done | bytes 32800 | tf_op jit(solution)/shard_map/ppermute | solution.py:34
  154.5 0.6 pad_maximum_fusion.4
  (18 shorter events, 0.4 us)
Async XLA Ops:
  7.2 52.7 %copy-start = (s32[16,16]{1,0:T(8,128)S(1)}, s32[16,16]{1,0:T(8,128)}, u32[]{:S(2)}) copy-start(s32[16,16]{1,0:T(8,128)} %param.13) | copy-start | bytes 3076
  7.2 93.6 %all-gather.2.cloned.1.call-start = ((), (), s32[]{:S(2)}) async-start(), calls=%async_computation.1 | async-start | bytes 6684672 | tf_op jit(solution)/shard_map/all_gather | solution.py:124
  17.1 6.7 %collective-permute-start = (bf16[96,512]{1,0:T(8,128)(2,1)}, bf16[96,512]{1,0:T(8,128)(2,1)S(1)}, u32[]{:S(2)}, u32[]{:S(2)}) collective-permute-start(bf16[96,512]{1,0:T(8,128)(2,1)} %param.10), channel_id=1, source_target_pairs={{0,1},{1,0},{2,3},{3,2},{4,5},{5,4},{6,7},{7,6},{8,9},{9,8},{10,11... | collective-permute-start | bytes 294920 | tf_op jit(solution)/shard_map/ppermute | solution.py:123
  57.9 8.2 %copy-start.1 = (bf16[8,96,1536]{2,1,0:T(8,128)(2,1)}, bf16[8,96,1536]{2,1,0:T(8,128)(2,1)S(1)}, u32[]{:S(2)}) copy-start(bf16[8,96,1536]{2,1,0:T(8,128)(2,1)S(1)} %all_to_all.5) | copy-start | bytes 7077892
  57.9 6.5 %collective-permute-start.1 = (bf16[8,96,1536]{2,1,0:T(8,128)(2,1)S(1)}, bf16[8,96,1536]{2,1,0:T(8,128)(2,1)}, u32[]{:S(2)}, u32[]{:S(2)}) collective-permute-start(bf16[8,96,1536]{2,1,0:T(8,128)(2,1)S(1)} %all_to_all.5), channel_id=1, source_target_pairs={{0,32},{32,0},{1,33},{33,1},{2,34},{34,2},{3,35},{35,3},{4,36},{36... | collective-permute-start | bytes 7077896 | tf_op jit(solution)/shard_map/ppermute | solution.py:132
  110.7 2.2 %collective-permute-start.2 = (bf16[256,512]{1,0:T(8,128)(2,1)}, bf16[256,512]{1,0:T(8,128)(2,1)S(1)}, u32[]{:S(2)}, u32[]{:S(2)}) collective-permute-start(bf16[256,512]{1,0:T(8,128)(2,1)} %get-tuple-element.7), channel_id=1, source_target_pairs={{0,8},{1,9},{32,40},{33,41},{64,72},{65,73},{96,104},{97,105},{128... | collective-permute-start | bytes 786440 | tf_op jit(solution)/shard_map/ppermute | solution.py:26
  111.4 1.5 collective-permute-start.3
  112.1 0.9 collective-permute-start.4
  114.1 3.4 %collective-permute-start.10 = (bf16[32,512]{1,0:T(8,128)(2,1)S(1)}, bf16[32,512]{1,0:T(8,128)(2,1)S(1)}, u32[]{:S(2)}, u32[]{:S(2)}) collective-permute-start(bf16[32,512]{1,0:T(8,128)(2,1)S(1)} %get-tuple-element.15), channel_id=1, source_target_pairs={{0,2},{1,3},{8,10},{9,11},{16,18},{17,19},{24,26},{25,27},{32,34},... | collective-permute-start | bytes 98312 | tf_op jit(solution)/shard_map/ppermute | solution.py:34
  114.7 4.0 %collective-permute-start.11 = (bf16[32,512]{1,0:T(8,128)(2,1)S(1)}, bf16[32,512]{1,0:T(8,128)(2,1)S(1)}, u32[]{:S(2)}, u32[]{:S(2)}) collective-permute-start(bf16[32,512]{1,0:T(8,128)(2,1)S(1)} %get-tuple-element.14), channel_id=1, source_target_pairs={{0,1},{1,2},{8,9},{9,10},{16,17},{17,18},{24,25},{25,26},{32,33},{... | collective-permute-start | bytes 98312 | tf_op jit(solution)/shard_map/ppermute | solution.py:34
  115.4 4.7 %collective-permute-start.5 = (bf16[32,512]{1,0:T(8,128)(2,1)S(1)}, bf16[32,512]{1,0:T(8,128)(2,1)S(1)}, u32[]{:S(2)}, u32[]{:S(2)}) collective-permute-start(bf16[32,512]{1,0:T(8,128)(2,1)S(1)} %get-tuple-element.20), channel_id=1, source_target_pairs={{0,7},{1,0},{8,15},{9,8},{16,23},{17,16},{24,31},{25,24},{32,39},{... | collective-permute-start | bytes 98312 | tf_op jit(solution)/shard_map/ppermute | solution.py:34
  116.1 4.0 %collective-permute-start.6 = (bf16[32,512]{1,0:T(8,128)(2,1)S(1)}, bf16[32,512]{1,0:T(8,128)(2,1)S(1)}, u32[]{:S(2)}, u32[]{:S(2)}) collective-permute-start(bf16[32,512]{1,0:T(8,128)(2,1)S(1)} %get-tuple-element.19), channel_id=1, source_target_pairs={{0,6},{1,7},{8,14},{9,15},{16,22},{17,23},{24,30},{25,31},{32,38},... | collective-permute-start | bytes 98312 | tf_op jit(solution)/shard_map/ppermute | solution.py:34
  116.8 3.4 %collective-permute-start.7 = (bf16[32,512]{1,0:T(8,128)(2,1)S(1)}, bf16[32,512]{1,0:T(8,128)(2,1)S(1)}, u32[]{:S(2)}, u32[]{:S(2)}) collective-permute-start(bf16[32,512]{1,0:T(8,128)(2,1)S(1)} %get-tuple-element.18), channel_id=1, source_target_pairs={{0,5},{1,6},{8,13},{9,14},{16,21},{17,22},{24,29},{25,30},{32,37},... | collective-permute-start | bytes 98312 | tf_op jit(solution)/shard_map/ppermute | solution.py:34
  117.4 35.1 %collective-permute-start.8 = (bf16[32,512]{1,0:T(8,128)(2,1)S(1)}, bf16[32,512]{1,0:T(8,128)(2,1)S(1)}, u32[]{:S(2)}, u32[]{:S(2)}) collective-permute-start(bf16[32,512]{1,0:T(8,128)(2,1)S(1)} %get-tuple-element.17), channel_id=1, source_target_pairs={{0,4},{1,5},{8,12},{9,13},{16,20},{17,21},{24,28},{25,29},{32,36},... | collective-permute-start | bytes 98312 | tf_op jit(solution)/shard_map/ppermute | solution.py:34
  118.7 35.7 %collective-permute-start.9 = (bf16[32,512]{1,0:T(8,128)(2,1)S(1)}, bf16[32,512]{1,0:T(8,128)(2,1)S(1)}, u32[]{:S(2)}, u32[]{:S(2)}) collective-permute-start(bf16[32,512]{1,0:T(8,128)(2,1)S(1)} %get-tuple-element.16), channel_id=1, source_target_pairs={{0,3},{1,4},{8,11},{9,12},{16,19},{17,20},{24,27},{25,28},{32,35},... | collective-permute-start | bytes 98312 | tf_op jit(solution)/shard_map/ppermute | solution.py:34
Sparse Core Ops, SparseCore 0:
  17.3 83.4 all-gather.1

commit v7 on v6

--- a/solution.py
+++ b/solution.py
@@ -11,6 +11,7 @@
 BF = jnp.bfloat16
 SWAP_Z = [(i, i ^ 1) for i in range(16)]
 LIMIT = 20
+SENT = (1, 3, 2)
 
 
 def place(branches, default):
@@ -22,8 +23,8 @@
 def spread(updated, parts, col_at):
     share = updated.shape[0] // 32
     sent = []
-    for m in (3, 2, 1):
-        block = lax.ppermute(parts[m - 1], COL, [(0, 8 * m), (1, 8 * m + 1)])
+    for block, m in zip(parts, SENT):
+        block = lax.ppermute(block, COL, [(0, 8 * m), (1, 8 * m + 1)])
         sent.append((col_at // 8 == m, block))
     held = place(sent, updated[: 8 * share])
     spot = col_at % 8
@@ -84,8 +85,8 @@
     done = (dense_ref[...].astype(jnp.float32) - product).astype(BF)
     out_ref[...] = done
     part = done.shape[0] // 4
-    for m in range(1, 4):
-        parts[m - 1][...] = done[m * part : (m + 1) * part]
+    for part_ref, m in zip(parts, SENT):
+        part_ref[...] = done[m * part : (m + 1) * part]
 
 
 def update(left, upper, cols, p_rows, q_rows, trailing):

time: 163 us -> 165 us (1.012)
  the two profiles are of different devices: /device:TPU:390 before, /device:TPU:384 now
where the time goes in v7:
time: 165 us; the launch traced here: 164 us
  waiting for transfers between devices  74.5 us (45%)
  blocking collectives  41.8 us (25%)
  between operations  14.5 us (9%)
  starting transfers between devices  12.8 us (8%)
  Pallas kernels  10.1 us (6%)
  other arithmetic  9.23 us (6%)
    ppermute x7, waiting for transfers between devices, spread(): got.append(lax.ppermute(piece, COL, pairs))  36.5 us
    all_to_all x1, blocking collectives, body(): lax.all_to_all(jnp.broadcast_to(rows[None], (NT // 2,) + rows.shape), 'ch...  32.9 us
    all_gather x1, waiting for transfers between devices, body(): cols = lax.all_gather(both, 'z', axis=0, tiled=True)  30.5 us
    pallas_call x1, Pallas kernels, update(): pl.pallas_call(update_kernel, out_shape=[jax.ShapeDtypeStruct((height, wi...  10.1 us
    all_gather x1, blocking collectives, body(): both = lax.all_gather(both, 'xhi', axis=0, tiled=True)  8.93 us
    ppermute x7, starting transfers between devices, spread(): got.append(lax.ppermute(piece, COL, pairs))  5.9 us
    another operation x4, other arithmetic, whole(): jnp.stack([jnp.where(lower, own, far), jnp.where(lower, far, own)], axis=1)  4.7 us
    ppermute x1, waiting for transfers between devices, body(): partner = lax.ppermute(upper_outer, 'z', SWAP_Z)  3.77 us
  transfers between devices with their start and end apart: 13, of which 5 were waited for; matrix products, arithmetic and copies ran while one was open for 5% of the time, Pallas kernels for 0%

profile of v7, /device:TPU:384, one launch (start us, length us, event | category | flops | bytes accessed | tf_op | source)
XLA Modules:
  0.0 164.4 jit_solution(360523105626042)
XLA Ops:
  7.2 1.0 pad_maximum_fusion.3
  8.2 8.9 %all_gather.6 = bf16[192,1024]{1,0:T(8,128)(2,1)} all-gather(bf16[96,1024]{1,0:T(8,128)(2,1)S(1)} %pad_maximum_fusion.3), channel_id=1, replica_groups=mesh['chip'=8,'core'=2,'xhi'=2,'z'=16] {'xhi'}, dimensions={0}, use_global_device_ids=true | all-gather | bytes 589824 | tf_op jit(solution)/shard_map/all_gather | solution.py:123
  17.1 2.9 %collective-permute-start = (bf16[96,512]{1,0:T(8,128)(2,1)}, bf16[96,512]{1,0:T(8,128)(2,1)S(1)}, u32[]{:S(2)}, u32[]{:S(2)}) collective-permute-start(bf16[96,512]{1,0:T(8,128)(2,1)} %param.10), channel_id=1, source_target_pairs={{0,1},{1,0},{2,3},{3,2},{4,5},{5,4},{6,7},{7,6},{8,9},{9,8},{10,11... | collective-permute-start | bytes 294920 | tf_op jit(solution)/shard_map/ppermute | solution.py:124
  20.1 3.8 %collective-permute-done = bf16[96,512]{1,0:T(8,128)(2,1)S(1)} collective-permute-done((bf16[96,512]{1,0:T(8,128)(2,1)}, bf16[96,512]{1,0:T(8,128)(2,1)S(1)}, u32[]{:S(2)}, u32[]{:S(2)}) %collective-permute-start) | collective-permute-done | bytes 98336 | tf_op jit(solution)/shard_map/ppermute | solution.py:124
  23.9 0.9 broadcast_select_fusion.1
  24.8 0.9 pad_maximum_fusion.2
  25.7 0.2 broadcast_in_dim.2
  25.9 32.9 %all_to_all.5 = bf16[8,96,1536]{2,1,0:T(8,128)(2,1)S(1)} all-to-all(bf16[8,96,1536]{2,1,0:T(8,128)(2,1)S(1)} %broadcast_in_dim.2), channel_id=1, replica_groups=mesh['chip'=8,'core'=2,'xhi'=2,'z'=16] {'chip'}, dimensions={0} | all-to-all | bytes 4718592 | tf_op jit(solution)/shard_map/all_to_all | solution.py:132
  58.8 1.9 %collective-permute-start.1 = (bf16[8,96,1536]{2,1,0:T(8,128)(2,1)S(1)}, bf16[8,96,1536]{2,1,0:T(8,128)(2,1)}, u32[]{:S(2)}, u32[]{:S(2)}) collective-permute-start(bf16[8,96,1536]{2,1,0:T(8,128)(2,1)S(1)} %all_to_all.5), channel_id=1, source_target_pairs={{0,32},{32,0},{1,33},{33,1},{2,34},{34,2},{3,35},{35,3},{4,36},{36... | collective-permute-start | bytes 7077896 | tf_op jit(solution)/shard_map/ppermute | solution.py:133
  60.9 0.7 fusion.left_ref
  61.6 3.7 %collective-permute-done.1 = bf16[8,96,1536]{2,1,0:T(8,128)(2,1)} collective-permute-done((bf16[8,96,1536]{2,1,0:T(8,128)(2,1)S(1)}, bf16[8,96,1536]{2,1,0:T(8,128)(2,1)}, u32[]{:S(2)}, u32[]{:S(2)}) %collective-permute-start.1) | collective-permute-done | bytes 2359328 | tf_op jit(solution)/shard_map/ppermute | solution.py:133
  65.3 1.6 select_bitcast_fusion.1
  67.0 0.3 pad_maximum_fusion
  67.2 0.3 copy.11
  67.6 1.5 select_bitcast_fusion.3
  69.1 1.3 pad_maximum_fusion.1
  70.4 30.5 %all-gather.2.cloned.1.call-done = bf16[3072,1024]{1,0:T(8,128)(2,1)} async-done(((bf16[192,1024]{1,0:T(8,128)(2,1)}), bf16[3072,1024]{1,0:T(8,128)(2,1)}) %all-gather.2.cloned.1.call-update) | async-done | bytes 6291472 | tf_op jit(solution)/shard_map/all_gather | solution.py:125
  100.8 10.1 %shard_map.86 = (bf16[1024,512]{1,0:T(8,128)(2,1)}, bf16[256,512]{1,0:T(8,128)(2,1)S(1)}, bf16[256,512]{1,0:T(8,128)(2,1)}, bf16[256,512]{1,0:T(8,128)(2,1)}) custom-call(s32[16]{0:T(128)S(1)} %fusion.left_ref, s32[16]{0:T(128)S(1)} %dynamic-slice_reduce_fusion.upper_ref, bf16[16,2,2,48,1024]{4,3,2,1,0:T(8,128)(2,1)} %bitcast.16, ...), custom_call_target="tpu_custom_call" | custom-call | tf_op jit(solution)/shard_map/pallas_call | solution.py:98
  111.0 0.7 collective-permute-start.2
  111.6 0.7 collective-permute-start.3
  112.3 0.7 collective-permute-start.4
  113.2 1.0 select_select_fusion
  114.3 0.7 collective-permute-start.10
  115.0 0.7 collective-permute-start.11
  115.6 0.7 collective-permute-start.5
  116.3 0.7 collective-permute-start.6
  117.0 0.7 collective-permute-start.7
  117.7 1.3 collective-permute-start.8
  119.0 1.3 collective-permute-start.9
  120.3 34.6 %collective-permute-done.8 = bf16[32,512]{1,0:T(8,128)(2,1)S(1)} collective-permute-done((bf16[32,512]{1,0:T(8,128)(2,1)S(1)}, bf16[32,512]{1,0:T(8,128)(2,1)S(1)}, u32[]{:S(2)}, u32[]{:S(2)}) %collective-permute-start.8) | collective-permute-done | bytes 32800 | tf_op jit(solution)/shard_map/ppermute | solution.py:35
  155.0 1.9 %collective-permute-done.9 = bf16[32,512]{1,0:T(8,128)(2,1)S(1)} collective-permute-done((bf16[32,512]{1,0:T(8,128)(2,1)S(1)}, bf16[32,512]{1,0:T(8,128)(2,1)S(1)}, u32[]{:S(2)}, u32[]{:S(2)}) %collective-permute-start.9) | collective-permute-done | bytes 32800 | tf_op jit(solution)/shard_map/ppermute | solution.py:35
  156.9 0.6 pad_maximum_fusion.4
  (18 shorter events, 0.4 us)
Async XLA Ops:
  7.2 53.5 %copy-start = (s32[16,16]{1,0:T(8,128)S(1)}, s32[16,16]{1,0:T(8,128)}, u32[]{:S(2)}) copy-start(s32[16,16]{1,0:T(8,128)} %param.13) | copy-start | bytes 3076
  7.2 93.6 %all-gather.2.cloned.1.call-start = ((), (), s32[]{:S(2)}) async-start(), calls=%async_computation.1 | async-start | bytes 6684672 | tf_op jit(solution)/shard_map/all_gather | solution.py:125
  17.1 6.7 %collective-permute-start = (bf16[96,512]{1,0:T(8,128)(2,1)}, bf16[96,512]{1,0:T(8,128)(2,1)S(1)}, u32[]{:S(2)}, u32[]{:S(2)}) collective-permute-start(bf16[96,512]{1,0:T(8,128)(2,1)} %param.10), channel_id=1, source_target_pairs={{0,1},{1,0},{2,3},{3,2},{4,5},{5,4},{6,7},{7,6},{8,9},{9,8},{10,11... | collective-permute-start | bytes 294920 | tf_op jit(solution)/shard_map/ppermute | solution.py:124
  58.8 8.2 %copy-start.1 = (bf16[8,96,1536]{2,1,0:T(8,128)(2,1)}, bf16[8,96,1536]{2,1,0:T(8,128)(2,1)S(1)}, u32[]{:S(2)}) copy-start(bf16[8,96,1536]{2,1,0:T(8,128)(2,1)S(1)} %all_to_all.5) | copy-start | bytes 7077892
  58.8 6.5 %collective-permute-start.1 = (bf16[8,96,1536]{2,1,0:T(8,128)(2,1)S(1)}, bf16[8,96,1536]{2,1,0:T(8,128)(2,1)}, u32[]{:S(2)}, u32[]{:S(2)}) collective-permute-start(bf16[8,96,1536]{2,1,0:T(8,128)(2,1)S(1)} %all_to_all.5), channel_id=1, source_target_pairs={{0,32},{32,0},{1,33},{33,1},{2,34},{34,2},{3,35},{35,3},{4,36},{36... | collective-permute-start | bytes 7077896 | tf_op jit(solution)/shard_map/ppermute | solution.py:133
  111.0 2.2 %collective-permute-start.2 = (bf16[256,512]{1,0:T(8,128)(2,1)}, bf16[256,512]{1,0:T(8,128)(2,1)S(1)}, u32[]{:S(2)}, u32[]{:S(2)}) collective-permute-start(bf16[256,512]{1,0:T(8,128)(2,1)} %get-tuple-element.7), channel_id=1, source_target_pairs={{0,16},{1,17},{32,48},{33,49},{64,80},{65,81},{96,112},{97,113},{1... | collective-permute-start | bytes 786440 | tf_op jit(solution)/shard_map/ppermute | solution.py:27
  111.6 1.5 collective-permute-start.3
  112.3 0.9 collective-permute-start.4
  114.3 3.4 %collective-permute-start.10 = (bf16[32,512]{1,0:T(8,128)(2,1)S(1)}, bf16[32,512]{1,0:T(8,128)(2,1)S(1)}, u32[]{:S(2)}, u32[]{:S(2)}) collective-permute-start(bf16[32,512]{1,0:T(8,128)(2,1)S(1)} %get-tuple-element.15), channel_id=1, source_target_pairs={{0,2},{1,3},{8,10},{9,11},{16,18},{17,19},{24,26},{25,27},{32,34},... | collective-permute-start | bytes 98312 | tf_op jit(solution)/shard_map/ppermute | solution.py:35
  115.0 4.0 %collective-permute-start.11 = (bf16[32,512]{1,0:T(8,128)(2,1)S(1)}, bf16[32,512]{1,0:T(8,128)(2,1)S(1)}, u32[]{:S(2)}, u32[]{:S(2)}) collective-permute-start(bf16[32,512]{1,0:T(8,128)(2,1)S(1)} %get-tuple-element.14), channel_id=1, source_target_pairs={{0,1},{1,2},{8,9},{9,10},{16,17},{17,18},{24,25},{25,26},{32,33},{... | collective-permute-start | bytes 98312 | tf_op jit(solution)/shard_map/ppermute | solution.py:35
  115.6 4.7 %collective-permute-start.5 = (bf16[32,512]{1,0:T(8,128)(2,1)S(1)}, bf16[32,512]{1,0:T(8,128)(2,1)S(1)}, u32[]{:S(2)}, u32[]{:S(2)}) collective-permute-start(bf16[32,512]{1,0:T(8,128)(2,1)S(1)} %get-tuple-element.20), channel_id=1, source_target_pairs={{0,7},{1,0},{8,15},{9,8},{16,23},{17,16},{24,31},{25,24},{32,39},{... | collective-permute-start | bytes 98312 | tf_op jit(solution)/shard_map/ppermute | solution.py:35
  116.3 4.0 %collective-permute-start.6 = (bf16[32,512]{1,0:T(8,128)(2,1)S(1)}, bf16[32,512]{1,0:T(8,128)(2,1)S(1)}, u32[]{:S(2)}, u32[]{:S(2)}) collective-permute-start(bf16[32,512]{1,0:T(8,128)(2,1)S(1)} %get-tuple-element.19), channel_id=1, source_target_pairs={{0,6},{1,7},{8,14},{9,15},{16,22},{17,23},{24,30},{25,31},{32,38},... | collective-permute-start | bytes 98312 | tf_op jit(solution)/shard_map/ppermute | solution.py:35
  117.0 3.4 %collective-permute-start.7 = (bf16[32,512]{1,0:T(8,128)(2,1)S(1)}, bf16[32,512]{1,0:T(8,128)(2,1)S(1)}, u32[]{:S(2)}, u32[]{:S(2)}) collective-permute-start(bf16[32,512]{1,0:T(8,128)(2,1)S(1)} %get-tuple-element.18), channel_id=1, source_target_pairs={{0,5},{1,6},{8,13},{9,14},{16,21},{17,22},{24,29},{25,30},{32,37},... | collective-permute-start | bytes 98312 | tf_op jit(solution)/shard_map/ppermute | solution.py:35
  117.7 37.3 %collective-permute-start.8 = (bf16[32,512]{1,0:T(8,128)(2,1)S(1)}, bf16[32,512]{1,0:T(8,128)(2,1)S(1)}, u32[]{:S(2)}, u32[]{:S(2)}) collective-permute-start(bf16[32,512]{1,0:T(8,128)(2,1)S(1)} %get-tuple-element.17), channel_id=1, source_target_pairs={{0,4},{1,5},{8,12},{9,13},{16,20},{17,21},{24,28},{25,29},{32,36},... | collective-permute-start | bytes 98312 | tf_op jit(solution)/shard_map/ppermute | solution.py:35
  119.0 37.9 %collective-permute-start.9 = (bf16[32,512]{1,0:T(8,128)(2,1)S(1)}, bf16[32,512]{1,0:T(8,128)(2,1)S(1)}, u32[]{:S(2)}, u32[]{:S(2)}) collective-permute-start(bf16[32,512]{1,0:T(8,128)(2,1)S(1)} %get-tuple-element.16), channel_id=1, source_target_pairs={{0,3},{1,4},{8,11},{9,12},{16,19},{17,20},{24,27},{25,28},{32,35},... | collective-permute-start | bytes 98312 | tf_op jit(solution)/shard_map/ppermute | solution.py:35
Sparse Core Ops, SparseCore 0:
  17.3 83.5 all-gather.1

commit v8 on v6

--- a/solution.py
+++ b/solution.py
@@ -49,35 +49,49 @@
     def fetch(source, target):
         copies.append(pltpu.make_async_copy(source, target, sems.at[len(copies)]))
 
-    for zz in range(8):
-        for h in range(2):
-            fetch(cols_ref.at[2 * zz + h, :, 1], inner_ref.at[zz, :, h])
-        fetch(q_ref.at[:, zz], q_held.at[:, zz])
-    for zz in range(8):
-        for h in range(2):
-            fetch(cols_ref.at[2 * zz + h, :, 0], outer_ref.at[zz, :, h])
+    needs = []
+    for c in range(4):
+        if c % 2 == 0:
+            at = slice(2 * c, 2 * c + 4)
+            fetch(q_ref.at[:, at], q_held.at[:, at])
+        at = slice(4 * c, 4 * c + 4)
+        fetch(cols_ref.at[at, :, 1], inner_ref.at[at])
+        needs.append(len(copies))
+    for c in range(2):
+        at = slice(8 * c, 8 * c + 8)
+        fetch(cols_ref.at[at, :, 0], outer_ref.at[at])
     fetch(trailing_ref, dense_ref)
     for copy in copies:
         copy.start()
-    t = lax.broadcasted_iota(jnp.int32, (rank_pad, rank_pad), 0)
-    u = lax.broadcasted_iota(jnp.int32, (rank_pad, rank_pad), 1)
+    half = rank_pad // 2
+    pair = (2 * rank_pad, 2 * rank_pad)
+    t, u = lax.broadcasted_iota(jnp.int32, pair, 0), lax.broadcasted_iota(jnp.int32, pair, 1)
+    u_low = u < rank_pad
+    u = jnp.where(u_low, u, u - rank_pad)
+    late = t >= rank_pad
+    t = jnp.where(late, t - rank_pad, t)
+    t_low = t < half
+    t = jnp.where(t_low, t, t - half) + jnp.where(late, half, 0)
+    same = t_low == u_low
+    waited = 0
     for zz in range(8):
-        for copy in copies[3 * zz : 3 * zz + 3]:
-            copy.wait()
-        for xhi in range(2):
-            k = xhi * 8 + zz
-            core = lax.dot_general(
-                inner_ref[zz, xhi].reshape(rank_pad, depth),
-                p_ref[xhi, zz],
-                (((1,), (1,)), ((), ())),
-                preferred_element_type=jnp.float32,
-            )
-            core = jnp.where((t < left_ref[k]) & (u < upper_ref[k]), core, 0.0).astype(BF)
-            at = (2 * zz + xhi) * rank_pad
-            weights_ref[at : at + rank_pad, :] = jnp.dot(
-                core, q_held[xhi, zz], preferred_element_type=jnp.float32
-            ).astype(BF)
-    for copy in copies[24:]:
+        while waited < needs[zz // 2]:
+            copies[waited].wait()
+            waited += 1
+        core = lax.dot_general(
+            inner_ref[2 * zz : 2 * zz + 2].reshape(2 * rank_pad, depth),
+            jnp.concatenate([p_ref[0, zz], p_ref[1, zz]], axis=0),
+            (((1,), (1,)), ((), ())),
+            preferred_element_type=jnp.float32,
+        )
+        left_live = t < jnp.where(t_low, left_ref[zz], left_ref[zz + 8])
+        upper_live = u < jnp.where(u_low, upper_ref[zz], upper_ref[zz + 8])
+        core = jnp.where(same & left_live & upper_live, core, 0.0).astype(BF)
+        at = 2 * zz * rank_pad
+        weights_ref[at : at + 2 * rank_pad, :] = jnp.dot(
+            core, jnp.concatenate([q_held[0, zz], q_held[1, zz]], axis=0), preferred_element_type=jnp.float32
+        ).astype(BF)
+    for copy in copies[waited:]:
         copy.wait()
     outer = outer_ref[...].reshape(NT * rank_pad, depth)
     product = lax.dot_general(outer, weights_ref[...], (((0,), (0,)), ((), ())), preferred_element_type=jnp.float32)
@@ -93,13 +107,13 @@
     rank_pad, depth, half = p_rows.shape[2], cols.shape[4], cols.shape[3]
     vmem, smem = pl.BlockSpec(memory_space=pltpu.VMEM), pl.BlockSpec(memory_space=pltpu.SMEM)
     hbm = pl.BlockSpec(memory_space=pltpu.HBM)
-    held = pltpu.VMEM((8, 2, 2, half, depth), BF)
+    held = pltpu.VMEM((NT, 2, half, depth), BF)
     return pl.pallas_call(
         update_kernel,
         out_shape=[jax.ShapeDtypeStruct((height, width), BF)] + [jax.ShapeDtypeStruct((height // 4, width), BF)] * 3,
         in_specs=[smem, smem, hbm, vmem, hbm, hbm],
         out_specs=[vmem] * 4,
-        scratch_shapes=[held, held, pltpu.VMEM((NT * rank_pad, width), BF), pltpu.VMEM(q_rows.shape, BF), pltpu.VMEM(trailing.shape, BF), pltpu.SemaphoreType.DMA((41,))],
+        scratch_shapes=[held, held, pltpu.VMEM((NT * rank_pad, width), BF), pltpu.VMEM(q_rows.shape, BF), pltpu.VMEM(trailing.shape, BF), pltpu.SemaphoreType.DMA((9,))],
         compiler_params=pltpu.CompilerParams(vmem_limit_bytes=LIMIT << 20),
     )(
         left,

time: 163 us -> 161 us (0.988)
  no operation moved by 1% of the time
where the time goes in v8:
time: 161 us; the launch traced here: 160 us
  waiting for transfers between devices  73.1 us (45%)
  blocking collectives  40.9 us (25%)
  between operations  14.5 us (9%)
  starting transfers between devices  12.8 us (8%)
  other arithmetic  9.24 us (6%)
  Pallas kernels  8.5 us (5%)
    ppermute x7, waiting for transfers between devices, spread(): got.append(lax.ppermute(piece, COL, pairs))  34.3 us
    all_to_all x1, blocking collectives, body(): lax.all_to_all(jnp.broadcast_to(rows[None], (NT // 2,) + rows.shape), 'ch...  32 us
    all_gather x1, waiting for transfers between devices, body(): cols = lax.all_gather(both, 'z', axis=0, tiled=True)  31.3 us
    all_gather x1, blocking collectives, body(): both = lax.all_gather(both, 'xhi', axis=0, tiled=True)  8.93 us
    pallas_call x1, Pallas kernels, update(): pl.pallas_call(update_kernel, out_shape=[jax.ShapeDtypeStruct((height, wi...  8.5 us
    ppermute x7, starting transfers between devices, spread(): got.append(lax.ppermute(piece, COL, pairs))  5.9 us
    another operation x4, other arithmetic, whole(): jnp.stack([jnp.where(lower, own, far), jnp.where(lower, far, own)], axis=1)  4.7 us
    ppermute x1, waiting for transfers between devices, body(): partner = lax.ppermute(upper_outer, 'z', SWAP_Z)  3.77 us
  transfers between devices with their start and end apart: 13, of which 5 were waited for; matrix products, arithmetic and copies ran while one was open for 5% of the time, Pallas kernels for 0%

profile of v8, /device:TPU:390, one launch (start us, length us, event | category | flops | bytes accessed | tf_op | source)
XLA Modules:
  0.0 160.5 jit_solution(17579895259000726001)
XLA Ops:
  7.2 1.0 pad_maximum_fusion.3
  8.2 8.9 %all_gather.6 = bf16[192,1024]{1,0:T(8,128)(2,1)} all-gather(bf16[96,1024]{1,0:T(8,128)(2,1)S(1)} %pad_maximum_fusion.3), channel_id=1, replica_groups=mesh['chip'=8,'core'=2,'xhi'=2,'z'=16] {'xhi'}, dimensions={0}, use_global_device_ids=true | all-gather | bytes 589824 | tf_op jit(solution)/shard_map/all_gather | solution.py:136
  17.1 2.9 %collective-permute-start = (bf16[96,512]{1,0:T(8,128)(2,1)}, bf16[96,512]{1,0:T(8,128)(2,1)S(1)}, u32[]{:S(2)}, u32[]{:S(2)}) collective-permute-start(bf16[96,512]{1,0:T(8,128)(2,1)} %param.10), channel_id=1, source_target_pairs={{0,1},{1,0},{2,3},{3,2},{4,5},{5,4},{6,7},{7,6},{8,9},{9,8},{10,11... | collective-permute-start | bytes 294920 | tf_op jit(solution)/shard_map/ppermute | solution.py:137
  20.1 3.8 %collective-permute-done = bf16[96,512]{1,0:T(8,128)(2,1)S(1)} collective-permute-done((bf16[96,512]{1,0:T(8,128)(2,1)}, bf16[96,512]{1,0:T(8,128)(2,1)S(1)}, u32[]{:S(2)}, u32[]{:S(2)}) %collective-permute-start) | collective-permute-done | bytes 98336 | tf_op jit(solution)/shard_map/ppermute | solution.py:137
  23.9 0.9 broadcast_select_fusion.1
  24.8 0.9 pad_maximum_fusion.2
  25.7 0.2 broadcast_in_dim.2
  25.9 32.0 %all_to_all.5 = bf16[8,96,1536]{2,1,0:T(8,128)(2,1)S(1)} all-to-all(bf16[8,96,1536]{2,1,0:T(8,128)(2,1)S(1)} %broadcast_in_dim.2), channel_id=1, replica_groups=mesh['chip'=8,'core'=2,'xhi'=2,'z'=16] {'chip'}, dimensions={0} | all-to-all | bytes 4718592 | tf_op jit(solution)/shard_map/all_to_all | solution.py:145
  57.9 1.9 %collective-permute-start.1 = (bf16[8,96,1536]{2,1,0:T(8,128)(2,1)S(1)}, bf16[8,96,1536]{2,1,0:T(8,128)(2,1)}, u32[]{:S(2)}, u32[]{:S(2)}) collective-permute-start(bf16[8,96,1536]{2,1,0:T(8,128)(2,1)S(1)} %all_to_all.5), channel_id=1, source_target_pairs={{0,32},{32,0},{1,33},{33,1},{2,34},{34,2},{3,35},{35,3},{4,36},{36... | collective-permute-start | bytes 7077896 | tf_op jit(solution)/shard_map/ppermute | solution.py:146
  60.0 0.7 fusion.left_ref
  60.7 3.7 %collective-permute-done.1 = bf16[8,96,1536]{2,1,0:T(8,128)(2,1)} collective-permute-done((bf16[8,96,1536]{2,1,0:T(8,128)(2,1)S(1)}, bf16[8,96,1536]{2,1,0:T(8,128)(2,1)}, u32[]{:S(2)}, u32[]{:S(2)}) %collective-permute-start.1) | collective-permute-done | bytes 2359328 | tf_op jit(solution)/shard_map/ppermute | solution.py:146
  64.4 1.6 %select_bitcast_fusion.1 = (bf16[8,1,96,1024]{3,2,0,1:T(8,128)(2,1)S(1)}, bf16[8,1,96,1024]{3,2,0,1:T(8,128)(2,1)S(1)}) fusion(pred[]{:T(512)S(6)} %eq.74, bf16[8,96,1536]{2,1,0:T(8,128)(2,1)} %collective-permute-done.1, bf16[8,96,1536]{2,1,0:T(8,128)(2,1)S(1)} %all_to_all.5), kind=kLoop, calls=%fused_computation.3 | loop fusion | flops 1572864 | bytes 6291457 | tf_op jit(solution)/shard_map/stack | solution.py:150
  66.1 0.3 pad_maximum_fusion
  66.4 0.3 copy.11
  66.7 1.5 select_bitcast_fusion.3
  68.2 1.3 pad_maximum_fusion.1
  69.5 31.3 %all-gather.2.cloned.1.call-done = bf16[3072,1024]{1,0:T(8,128)(2,1)} async-done(((bf16[192,1024]{1,0:T(8,128)(2,1)}), bf16[3072,1024]{1,0:T(8,128)(2,1)}) %all-gather.2.cloned.1.call-update) | async-done | bytes 6291472 | tf_op jit(solution)/shard_map/all_gather | solution.py:138
  100.8 8.5 %shard_map.86 = (bf16[1024,512]{1,0:T(8,128)(2,1)}, bf16[256,512]{1,0:T(8,128)(2,1)}, bf16[256,512]{1,0:T(8,128)(2,1)}, bf16[256,512]{1,0:T(8,128)(2,1)S(1)}) custom-call(s32[16]{0:T(128)S(1)} %fusion.left_ref, s32[16]{0:T(128)S(1)} %dynamic-slice_reduce_fusion.upper_ref, bf16[16,2,2,48,1024]{4,3,2,1,0:T(8,128)(2,1)} %bitcast.16, ...), custom_call_target="tpu_custom_call" | custom-call | tf_op jit(solution)/shard_map/pallas_call | solution.py:111
  109.3 0.7 collective-permute-start.2
  109.9 0.7 collective-permute-start.3
  110.6 0.7 collective-permute-start.4
  111.5 1.0 select_select_fusion
  112.6 0.7 collective-permute-start.10
  113.3 0.7 collective-permute-start.11
  113.9 0.7 collective-permute-start.5
  114.6 0.7 collective-permute-start.6
  115.3 0.7 collective-permute-start.7
  115.9 1.3 collective-permute-start.8
  117.3 1.3 collective-permute-start.9
  118.6 32.4 %collective-permute-done.8 = bf16[32,512]{1,0:T(8,128)(2,1)S(1)} collective-permute-done((bf16[32,512]{1,0:T(8,128)(2,1)S(1)}, bf16[32,512]{1,0:T(8,128)(2,1)S(1)}, u32[]{:S(2)}, u32[]{:S(2)}) %collective-permute-start.8) | collective-permute-done | bytes 32800 | tf_op jit(solution)/shard_map/ppermute | solution.py:34
  151.1 1.9 %collective-permute-done.9 = bf16[32,512]{1,0:T(8,128)(2,1)S(1)} collective-permute-done((bf16[32,512]{1,0:T(8,128)(2,1)S(1)}, bf16[32,512]{1,0:T(8,128)(2,1)S(1)}, u32[]{:S(2)}, u32[]{:S(2)}) %collective-permute-start.9) | collective-permute-done | bytes 32800 | tf_op jit(solution)/shard_map/ppermute | solution.py:34
  153.0 0.6 pad_maximum_fusion.4
  (18 shorter events, 0.4 us)
Async XLA Ops:
  7.2 52.7 %copy-start = (s32[16,16]{1,0:T(8,128)S(1)}, s32[16,16]{1,0:T(8,128)}, u32[]{:S(2)}) copy-start(s32[16,16]{1,0:T(8,128)} %param.13) | copy-start | bytes 3076
  7.2 93.6 %all-gather.2.cloned.1.call-start = ((), (), s32[]{:S(2)}) async-start(), calls=%async_computation.1 | async-start | bytes 6684672 | tf_op jit(solution)/shard_map/all_gather | solution.py:138
  17.1 6.7 %collective-permute-start = (bf16[96,512]{1,0:T(8,128)(2,1)}, bf16[96,512]{1,0:T(8,128)(2,1)S(1)}, u32[]{:S(2)}, u32[]{:S(2)}) collective-permute-start(bf16[96,512]{1,0:T(8,128)(2,1)} %param.10), channel_id=1, source_target_pairs={{0,1},{1,0},{2,3},{3,2},{4,5},{5,4},{6,7},{7,6},{8,9},{9,8},{10,11... | collective-permute-start | bytes 294920 | tf_op jit(solution)/shard_map/ppermute | solution.py:137
  57.9 8.2 %copy-start.1 = (bf16[8,96,1536]{2,1,0:T(8,128)(2,1)}, bf16[8,96,1536]{2,1,0:T(8,128)(2,1)S(1)}, u32[]{:S(2)}) copy-start(bf16[8,96,1536]{2,1,0:T(8,128)(2,1)S(1)} %all_to_all.5) | copy-start | bytes 7077892
  57.9 6.5 %collective-permute-start.1 = (bf16[8,96,1536]{2,1,0:T(8,128)(2,1)S(1)}, bf16[8,96,1536]{2,1,0:T(8,128)(2,1)}, u32[]{:S(2)}, u32[]{:S(2)}) collective-permute-start(bf16[8,96,1536]{2,1,0:T(8,128)(2,1)S(1)} %all_to_all.5), channel_id=1, source_target_pairs={{0,32},{32,0},{1,33},{33,1},{2,34},{34,2},{3,35},{35,3},{4,36},{36... | collective-permute-start | bytes 7077896 | tf_op jit(solution)/shard_map/ppermute | solution.py:146
  109.3 2.2 %collective-permute-start.2 = (bf16[256,512]{1,0:T(8,128)(2,1)}, bf16[256,512]{1,0:T(8,128)(2,1)S(1)}, u32[]{:S(2)}, u32[]{:S(2)}) collective-permute-start(bf16[256,512]{1,0:T(8,128)(2,1)} %get-tuple-element.7), channel_id=1, source_target_pairs={{0,8},{1,9},{32,40},{33,41},{64,72},{65,73},{96,104},{97,105},{128... | collective-permute-start | bytes 786440 | tf_op jit(solution)/shard_map/ppermute | solution.py:26
  109.9 1.5 collective-permute-start.3
  110.6 0.9 collective-permute-start.4
  112.6 3.4 %collective-permute-start.10 = (bf16[32,512]{1,0:T(8,128)(2,1)S(1)}, bf16[32,512]{1,0:T(8,128)(2,1)S(1)}, u32[]{:S(2)}, u32[]{:S(2)}) collective-permute-start(bf16[32,512]{1,0:T(8,128)(2,1)S(1)} %get-tuple-element.15), channel_id=1, source_target_pairs={{0,2},{1,3},{8,10},{9,11},{16,18},{17,19},{24,26},{25,27},{32,34},... | collective-permute-start | bytes 98312 | tf_op jit(solution)/shard_map/ppermute | solution.py:34
  113.3 4.0 %collective-permute-start.11 = (bf16[32,512]{1,0:T(8,128)(2,1)S(1)}, bf16[32,512]{1,0:T(8,128)(2,1)S(1)}, u32[]{:S(2)}, u32[]{:S(2)}) collective-permute-start(bf16[32,512]{1,0:T(8,128)(2,1)S(1)} %get-tuple-element.14), channel_id=1, source_target_pairs={{0,1},{1,2},{8,9},{9,10},{16,17},{17,18},{24,25},{25,26},{32,33},{... | collective-permute-start | bytes 98312 | tf_op jit(solution)/shard_map/ppermute | solution.py:34
  113.9 4.7 %collective-permute-start.5 = (bf16[32,512]{1,0:T(8,128)(2,1)S(1)}, bf16[32,512]{1,0:T(8,128)(2,1)S(1)}, u32[]{:S(2)}, u32[]{:S(2)}) collective-permute-start(bf16[32,512]{1,0:T(8,128)(2,1)S(1)} %get-tuple-element.20), channel_id=1, source_target_pairs={{0,7},{1,0},{8,15},{9,8},{16,23},{17,16},{24,31},{25,24},{32,39},{... | collective-permute-start | bytes 98312 | tf_op jit(solution)/shard_map/ppermute | solution.py:34
  114.6 4.0 %collective-permute-start.6 = (bf16[32,512]{1,0:T(8,128)(2,1)S(1)}, bf16[32,512]{1,0:T(8,128)(2,1)S(1)}, u32[]{:S(2)}, u32[]{:S(2)}) collective-permute-start(bf16[32,512]{1,0:T(8,128)(2,1)S(1)} %get-tuple-element.19), channel_id=1, source_target_pairs={{0,6},{1,7},{8,14},{9,15},{16,22},{17,23},{24,30},{25,31},{32,38},... | collective-permute-start | bytes 98312 | tf_op jit(solution)/shard_map/ppermute | solution.py:34
  115.3 3.4 %collective-permute-start.7 = (bf16[32,512]{1,0:T(8,128)(2,1)S(1)}, bf16[32,512]{1,0:T(8,128)(2,1)S(1)}, u32[]{:S(2)}, u32[]{:S(2)}) collective-permute-start(bf16[32,512]{1,0:T(8,128)(2,1)S(1)} %get-tuple-element.18), channel_id=1, source_target_pairs={{0,5},{1,6},{8,13},{9,14},{16,21},{17,22},{24,29},{25,30},{32,37},... | collective-permute-start | bytes 98312 | tf_op jit(solution)/shard_map/ppermute | solution.py:34
  115.9 35.1 %collective-permute-start.8 = (bf16[32,512]{1,0:T(8,128)(2,1)S(1)}, bf16[32,512]{1,0:T(8,128)(2,1)S(1)}, u32[]{:S(2)}, u32[]{:S(2)}) collective-permute-start(bf16[32,512]{1,0:T(8,128)(2,1)S(1)} %get-tuple-element.17), channel_id=1, source_target_pairs={{0,4},{1,5},{8,12},{9,13},{16,20},{17,21},{24,28},{25,29},{32,36},... | collective-permute-start | bytes 98312 | tf_op jit(solution)/shard_map/ppermute | solution.py:34
  117.3 35.7 %collective-permute-start.9 = (bf16[32,512]{1,0:T(8,128)(2,1)S(1)}, bf16[32,512]{1,0:T(8,128)(2,1)S(1)}, u32[]{:S(2)}, u32[]{:S(2)}) collective-permute-start(bf16[32,512]{1,0:T(8,128)(2,1)S(1)} %get-tuple-element.16), channel_id=1, source_target_pairs={{0,3},{1,4},{8,11},{9,12},{16,19},{17,20},{24,27},{25,28},{32,35},... | collective-permute-start | bytes 98312 | tf_op jit(solution)/shard_map/ppermute | solution.py:34
Sparse Core Ops, SparseCore 0:
  17.3 83.4 all-gather.1

commit v9 on v8

--- a/solution.py
+++ b/solution.py
@@ -21,20 +21,22 @@
 
 def spread(updated, parts, col_at):
     share = updated.shape[0] // 32
+    lands = (0, 6, 0, 6)
     sent = []
     for m in (3, 2, 1):
-        block = lax.ppermute(parts[m - 1], COL, [(0, 8 * m), (1, 8 * m + 1)])
+        block = lax.ppermute(parts[m - 1], COL, [(h, 8 * m + lands[m] + h) for h in (0, 1)])
         sent.append((col_at // 8 == m, block))
     held = place(sent, updated[: 8 * share])
     spot = col_at % 8
     got = []
     for d in range(1, 8):
         piece = lax.dynamic_slice_in_dim(held, (spot + d) % 8 * share, share, 0)
-        pairs = [(b + h, b + (h + d) % 8) for b in range(0, 32, 8) for h in (0, 1)]
+        pairs = [(8 * m + lands[m] + h, 8 * m + (lands[m] + h + d) % 8) for m in range(4) for h in (0, 1)]
         got.append(lax.ppermute(piece, COL, pairs))
     own = lax.dynamic_slice_in_dim(held, spot * share, share, 0)
-    left = place([(spot == d, got[d - 1]) for d in range(1, 8)], own)
-    right = place([((spot - 1) % 8 == d, got[d - 1]) for d in range(1, 8)], own)
+    apart = (spot - jnp.where(col_at // 8 % 2 == 0, lands[0], lands[1])) % 8
+    left = place([(apart == d, got[d - 1]) for d in range(1, 8)], own)
+    right = place([((apart - 1) % 8 == d, got[d - 1]) for d in range(1, 8)], own)
     return jnp.concatenate([left, right], axis=1)
 
 

time: 161 us -> 163 us (1.012)
  the two profiles are of different devices: /device:TPU:390 before, /device:TPU:1 now
where the time goes in v9:
time: 163 us; the launch traced here: 162 us
  waiting for transfers between devices  60.4 us (37%)
  blocking collectives  36.7 us (23%)
  starting transfers between devices  31.3 us (19%)
  between operations  14.6 us (9%)
  other arithmetic  9.25 us (6%)
  Pallas kernels  8.49 us (5%)
    all_gather x1, waiting for transfers between devices, body(): cols = lax.all_gather(both, 'z', axis=0, tiled=True)  35 us
    all_to_all x1, blocking collectives, body(): lax.all_to_all(jnp.broadcast_to(rows[None], (NT // 2,) + rows.shape), 'ch...  29.3 us
    ppermute x3, waiting for transfers between devices, spread(): lax.ppermute(parts[m - 1], COL, [(h, 8 * m + lands[m] + h) for h in (0, 1)])  19 us
    ppermute x7, starting transfers between devices, spread(): got.append(lax.ppermute(piece, COL, pairs))  9.67 us
    pallas_call x1, Pallas kernels, update(): pl.pallas_call(update_kernel, out_shape=[jax.ShapeDtypeStruct((height, wi...  8.49 us
    ppermute x3, starting transfers between devices, spread(): lax.ppermute(parts[m - 1], COL, [(h, 8 * m + lands[m] + h) for h in (0, 1)])  8.34 us
    ppermute x1, starting transfers between devices, body(): across = lax.ppermute(rows, 'core', [(0, 1), (1, 0)])  8.17 us
    all_gather x1, blocking collectives, body(): both = lax.all_gather(both, 'xhi', axis=0, tiled=True)  7.39 us
  transfers between devices with their start and end apart: 13, of which 6 were waited for; matrix products, arithmetic and copies ran while one was open for 5% of the time, Pallas kernels for 0%

profile of v9, /device:TPU:1, one launch (start us, length us, event | category | flops | bytes accessed | tf_op | source)
XLA Modules:
  0.0 162.1 jit_solution(6546954971935606486)
XLA Ops:
  7.2 1.0 pad_maximum_fusion.3
  8.2 7.4 %all_gather.6 = bf16[192,1024]{1,0:T(8,128)(2,1)} all-gather(bf16[96,1024]{1,0:T(8,128)(2,1)S(1)} %pad_maximum_fusion.3), channel_id=1, replica_groups=mesh['chip'=8,'core'=2,'xhi'=2,'z'=16] {'xhi'}, dimensions={0}, use_global_device_ids=true | all-gather | bytes 589824 | tf_op jit(solution)/shard_map/all_gather | solution.py:138
  15.6 5.0 %collective-permute-start = (bf16[96,512]{1,0:T(8,128)(2,1)}, bf16[96,512]{1,0:T(8,128)(2,1)S(1)}, u32[]{:S(2)}, u32[]{:S(2)}) collective-permute-start(bf16[96,512]{1,0:T(8,128)(2,1)} %param.10), channel_id=1, source_target_pairs={{0,1},{1,0},{2,3},{3,2},{4,5},{5,4},{6,7},{7,6},{8,9},{9,8},{10,11... | collective-permute-start | bytes 294920 | tf_op jit(solution)/shard_map/ppermute | solution.py:139
  20.7 2.2 %collective-permute-done = bf16[96,512]{1,0:T(8,128)(2,1)S(1)} collective-permute-done((bf16[96,512]{1,0:T(8,128)(2,1)}, bf16[96,512]{1,0:T(8,128)(2,1)S(1)}, u32[]{:S(2)}, u32[]{:S(2)}) %collective-permute-start) | collective-permute-done | bytes 98336 | tf_op jit(solution)/shard_map/ppermute | solution.py:139
  22.9 0.9 broadcast_select_fusion.1
  23.8 0.9 pad_maximum_fusion.2
  24.9 29.3 %all_to_all.5 = bf16[8,96,1536]{2,1,0:T(8,128)(2,1)S(1)} all-to-all(bf16[8,96,1536]{2,1,0:T(8,128)(2,1)S(1)} %broadcast_in_dim.2), channel_id=1, replica_groups=mesh['chip'=8,'core'=2,'xhi'=2,'z'=16] {'chip'}, dimensions={0} | all-to-all | bytes 4718592 | tf_op jit(solution)/shard_map/all_to_all | solution.py:147
  54.2 8.2 %collective-permute-start.1 = (bf16[8,96,1536]{2,1,0:T(8,128)(2,1)S(1)}, bf16[8,96,1536]{2,1,0:T(8,128)(2,1)}, u32[]{:S(2)}, u32[]{:S(2)}) collective-permute-start(bf16[8,96,1536]{2,1,0:T(8,128)(2,1)S(1)} %all_to_all.5), channel_id=1, source_target_pairs={{0,32},{32,0},{1,33},{33,1},{2,34},{34,2},{3,35},{35,3},{4,36},{36... | collective-permute-start | bytes 7077896 | tf_op jit(solution)/shard_map/ppermute | solution.py:148
  62.6 0.7 fusion.left_ref
  63.3 3.4 %collective-permute-done.1 = bf16[8,96,1536]{2,1,0:T(8,128)(2,1)} collective-permute-done((bf16[8,96,1536]{2,1,0:T(8,128)(2,1)S(1)}, bf16[8,96,1536]{2,1,0:T(8,128)(2,1)}, u32[]{:S(2)}, u32[]{:S(2)}) %collective-permute-start.1) | collective-permute-done | bytes 2359328 | tf_op jit(solution)/shard_map/ppermute | solution.py:148
  66.6 1.6 %select_bitcast_fusion.1 = (bf16[8,1,96,1024]{3,2,0,1:T(8,128)(2,1)S(1)}, bf16[8,1,96,1024]{3,2,0,1:T(8,128)(2,1)S(1)}) fusion(pred[]{:T(512)S(6)} %eq.79, bf16[8,96,1536]{2,1,0:T(8,128)(2,1)} %collective-permute-done.1, bf16[8,96,1536]{2,1,0:T(8,128)(2,1)S(1)} %all_to_all.5), kind=kLoop, calls=%fused_computation.3 | loop fusion | flops 1572864 | bytes 6291457 | tf_op jit(solution)/shard_map/stack | solution.py:152
  68.3 0.3 pad_maximum_fusion
  68.6 0.3 copy.11
  68.9 1.5 select_bitcast_fusion.3
  70.4 1.3 pad_maximum_fusion.1
  71.7 35.0 %all-gather.2.cloned.1.call-done = bf16[3072,1024]{1,0:T(8,128)(2,1)} async-done(((bf16[192,1024]{1,0:T(8,128)(2,1)}), bf16[3072,1024]{1,0:T(8,128)(2,1)}) %all-gather.2.cloned.1.call-update) | async-done | bytes 6291472 | tf_op jit(solution)/shard_map/all_gather | solution.py:140
  106.7 8.5 %shard_map.86 = (bf16[1024,512]{1,0:T(8,128)(2,1)}, bf16[256,512]{1,0:T(8,128)(2,1)}, bf16[256,512]{1,0:T(8,128)(2,1)}, bf16[256,512]{1,0:T(8,128)(2,1)S(1)}) custom-call(s32[16]{0:T(128)S(1)} %fusion.left_ref, s32[16]{0:T(128)S(1)} %dynamic-slice_reduce_fusion.upper_ref, bf16[16,2,2,48,1024]{4,3,2,1,0:T(8,128)(2,1)} %bitcast.16, ...), custom_call_target="tpu_custom_call" | custom-call | tf_op jit(solution)/shard_map/pallas_call | solution.py:113
  115.2 4.5 %collective-permute-start.2 = (bf16[256,512]{1,0:T(8,128)(2,1)}, bf16[256,512]{1,0:T(8,128)(2,1)S(1)}, u32[]{:S(2)}, u32[]{:S(2)}) collective-permute-start(bf16[256,512]{1,0:T(8,128)(2,1)} %get-tuple-element.7), channel_id=1, source_target_pairs={{0,14},{1,15},{32,46},{33,47},{64,78},{65,79},{96,110},{97,111},{1... | collective-permute-start | bytes 786440 | tf_op jit(solution)/shard_map/ppermute | solution.py:27
  119.6 1.3 collective-permute-start.3
  121.0 2.6 %collective-permute-start.4 = (bf16[256,512]{1,0:T(8,128)(2,1)S(1)}, bf16[256,512]{1,0:T(8,128)(2,1)S(1)}, u32[]{:S(2)}, u32[]{:S(2)}) collective-permute-start(bf16[256,512]{1,0:T(8,128)(2,1)S(1)} %get-tuple-element.9), channel_id=1, source_target_pairs={{0,30},{1,31},{32,62},{33,63},{64,94},{65,95},{96,126},{97,127},{1... | collective-permute-start | bytes 786440 | tf_op jit(solution)/shard_map/ppermute | solution.py:27
  123.7 13.5 %collective-permute-done.2 = bf16[256,512]{1,0:T(8,128)(2,1)S(1)} collective-permute-done((bf16[256,512]{1,0:T(8,128)(2,1)}, bf16[256,512]{1,0:T(8,128)(2,1)S(1)}, u32[]{:S(2)}, u32[]{:S(2)}) %collective-permute-start.2) | collective-permute-done | bytes 262176 | tf_op jit(solution)/shard_map/ppermute | solution.py:27
  137.2 5.5 %collective-permute-done.4 = bf16[256,512]{1,0:T(8,128)(2,1)S(1)} collective-permute-done((bf16[256,512]{1,0:T(8,128)(2,1)S(1)}, bf16[256,512]{1,0:T(8,128)(2,1)S(1)}, u32[]{:S(2)}, u32[]{:S(2)}) %collective-permute-start.4) | collective-permute-done | bytes 262176 | tf_op jit(solution)/shard_map/ppermute | solution.py:27
  142.7 1.0 select_select_fusion
  143.7 1.3 collective-permute-start.10
  145.0 1.3 collective-permute-start.11
  146.3 1.9 %collective-permute-start.5 = (bf16[32,512]{1,0:T(8,128)(2,1)S(1)}, bf16[32,512]{1,0:T(8,128)(2,1)S(1)}, u32[]{:S(2)}, u32[]{:S(2)}) collective-permute-start(bf16[32,512]{1,0:T(8,128)(2,1)S(1)} %get-tuple-element.20), channel_id=1, source_target_pairs={{0,7},{1,0},{14,13},{15,14},{16,23},{17,16},{30,29},{31,30},{32,39... | collective-permute-start | bytes 98312 | tf_op jit(solution)/shard_map/ppermute | solution.py:35
  148.3 1.3 collective-permute-start.6
  149.6 1.3 collective-permute-start.7
  150.9 1.3 collective-permute-start.8
  152.2 1.3 collective-permute-start.9
  153.6 0.9 collective-permute-done.9
  154.6 0.6 pad_maximum_fusion.4
  (18 shorter events, 0.6 us)
Async XLA Ops:
  7.2 55.2 %copy-start = (s32[16,16]{1,0:T(8,128)S(1)}, s32[16,16]{1,0:T(8,128)}, u32[]{:S(2)}) copy-start(s32[16,16]{1,0:T(8,128)} %param.13) | copy-start | bytes 3076
  7.2 99.5 %all-gather.2.cloned.1.call-start = ((), (), s32[]{:S(2)}) async-start(), calls=%async_computation.1 | async-start | bytes 6684672 | tf_op jit(solution)/shard_map/all_gather | solution.py:140
  15.6 7.3 %collective-permute-start = (bf16[96,512]{1,0:T(8,128)(2,1)}, bf16[96,512]{1,0:T(8,128)(2,1)S(1)}, u32[]{:S(2)}, u32[]{:S(2)}) collective-permute-start(bf16[96,512]{1,0:T(8,128)(2,1)} %param.10), channel_id=1, source_target_pairs={{0,1},{1,0},{2,3},{3,2},{4,5},{5,4},{6,7},{7,6},{8,9},{9,8},{10,11... | collective-permute-start | bytes 294920 | tf_op jit(solution)/shard_map/ppermute | solution.py:139
  54.2 14.1 %copy-start.1 = (bf16[8,96,1536]{2,1,0:T(8,128)(2,1)}, bf16[8,96,1536]{2,1,0:T(8,128)(2,1)S(1)}, u32[]{:S(2)}) copy-start(bf16[8,96,1536]{2,1,0:T(8,128)(2,1)S(1)} %all_to_all.5) | copy-start | bytes 7077892
  54.2 12.4 %collective-permute-start.1 = (bf16[8,96,1536]{2,1,0:T(8,128)(2,1)S(1)}, bf16[8,96,1536]{2,1,0:T(8,128)(2,1)}, u32[]{:S(2)}, u32[]{:S(2)}) collective-permute-start(bf16[8,96,1536]{2,1,0:T(8,128)(2,1)S(1)} %all_to_all.5), channel_id=1, source_target_pairs={{0,32},{32,0},{1,33},{33,1},{2,34},{34,2},{3,35},{35,3},{4,36},{36... | collective-permute-start | bytes 7077896 | tf_op jit(solution)/shard_map/ppermute | solution.py:148
  115.2 22.0 %collective-permute-start.2 = (bf16[256,512]{1,0:T(8,128)(2,1)}, bf16[256,512]{1,0:T(8,128)(2,1)S(1)}, u32[]{:S(2)}, u32[]{:S(2)}) collective-permute-start(bf16[256,512]{1,0:T(8,128)(2,1)} %get-tuple-element.7), channel_id=1, source_target_pairs={{0,14},{1,15},{32,46},{33,47},{64,78},{65,79},{96,110},{97,111},{1... | collective-permute-start | bytes 786440 | tf_op jit(solution)/shard_map/ppermute | solution.py:27
  119.6 17.5 %collective-permute-start.3 = (bf16[256,512]{1,0:T(8,128)(2,1)}, bf16[256,512]{1,0:T(8,128)(2,1)S(1)}, u32[]{:S(2)}, u32[]{:S(2)}) collective-permute-start(bf16[256,512]{1,0:T(8,128)(2,1)} %get-tuple-element.8), channel_id=1, source_target_pairs={{0,16},{1,17},{32,48},{33,49},{64,80},{65,81},{96,112},{97,113},{1... | collective-permute-start | bytes 786440 | tf_op jit(solution)/shard_map/ppermute | solution.py:27
  121.0 21.7 %collective-permute-start.4 = (bf16[256,512]{1,0:T(8,128)(2,1)S(1)}, bf16[256,512]{1,0:T(8,128)(2,1)S(1)}, u32[]{:S(2)}, u32[]{:S(2)}) collective-permute-start(bf16[256,512]{1,0:T(8,128)(2,1)S(1)} %get-tuple-element.9), channel_id=1, source_target_pairs={{0,30},{1,31},{32,62},{33,63},{64,94},{65,95},{96,126},{97,127},{1... | collective-permute-start | bytes 786440 | tf_op jit(solution)/shard_map/ppermute | solution.py:27
  143.7 7.1 %collective-permute-start.10 = (bf16[32,512]{1,0:T(8,128)(2,1)S(1)}, bf16[32,512]{1,0:T(8,128)(2,1)S(1)}, u32[]{:S(2)}, u32[]{:S(2)}) collective-permute-start(bf16[32,512]{1,0:T(8,128)(2,1)S(1)} %get-tuple-element.15), channel_id=1, source_target_pairs={{0,2},{1,3},{14,8},{15,9},{16,18},{17,19},{30,24},{31,25},{32,34},... | collective-permute-start | bytes 98312 | tf_op jit(solution)/shard_map/ppermute | solution.py:35
  145.0 7.1 %collective-permute-start.11 = (bf16[32,512]{1,0:T(8,128)(2,1)S(1)}, bf16[32,512]{1,0:T(8,128)(2,1)S(1)}, u32[]{:S(2)}, u32[]{:S(2)}) collective-permute-start(bf16[32,512]{1,0:T(8,128)(2,1)S(1)} %get-tuple-element.14), channel_id=1, source_target_pairs={{0,1},{1,2},{14,15},{15,8},{16,17},{17,18},{30,31},{31,24},{32,33}... | collective-permute-start | bytes 98312 | tf_op jit(solution)/shard_map/ppermute | solution.py:35
  146.3 7.2 %collective-permute-start.5 = (bf16[32,512]{1,0:T(8,128)(2,1)S(1)}, bf16[32,512]{1,0:T(8,128)(2,1)S(1)}, u32[]{:S(2)}, u32[]{:S(2)}) collective-permute-start(bf16[32,512]{1,0:T(8,128)(2,1)S(1)} %get-tuple-element.20), channel_id=1, source_target_pairs={{0,7},{1,0},{14,13},{15,14},{16,23},{17,16},{30,29},{31,30},{32,39... | collective-permute-start | bytes 98312 | tf_op jit(solution)/shard_map/ppermute | solution.py:35
  148.3 5.3 %collective-permute-start.6 = (bf16[32,512]{1,0:T(8,128)(2,1)S(1)}, bf16[32,512]{1,0:T(8,128)(2,1)S(1)}, u32[]{:S(2)}, u32[]{:S(2)}) collective-permute-start(bf16[32,512]{1,0:T(8,128)(2,1)S(1)} %get-tuple-element.19), channel_id=1, source_target_pairs={{0,6},{1,7},{14,12},{15,13},{16,22},{17,23},{30,28},{31,29},{32,38... | collective-permute-start | bytes 98312 | tf_op jit(solution)/shard_map/ppermute | solution.py:35
  149.6 4.0 %collective-permute-start.7 = (bf16[32,512]{1,0:T(8,128)(2,1)S(1)}, bf16[32,512]{1,0:T(8,128)(2,1)S(1)}, u32[]{:S(2)}, u32[]{:S(2)}) collective-permute-start(bf16[32,512]{1,0:T(8,128)(2,1)S(1)} %get-tuple-element.18), channel_id=1, source_target_pairs={{0,5},{1,6},{14,11},{15,12},{16,21},{17,22},{30,27},{31,28},{32,37... | collective-permute-start | bytes 98312 | tf_op jit(solution)/shard_map/ppermute | solution.py:35
  150.9 2.7 %collective-permute-start.8 = (bf16[32,512]{1,0:T(8,128)(2,1)S(1)}, bf16[32,512]{1,0:T(8,128)(2,1)S(1)}, u32[]{:S(2)}, u32[]{:S(2)}) collective-permute-start(bf16[32,512]{1,0:T(8,128)(2,1)S(1)} %get-tuple-element.17), channel_id=1, source_target_pairs={{0,4},{1,5},{14,10},{15,11},{16,20},{17,21},{30,26},{31,27},{32,36... | collective-permute-start | bytes 98312 | tf_op jit(solution)/shard_map/ppermute | solution.py:35
  152.2 2.3 %collective-permute-start.9 = (bf16[32,512]{1,0:T(8,128)(2,1)S(1)}, bf16[32,512]{1,0:T(8,128)(2,1)S(1)}, u32[]{:S(2)}, u32[]{:S(2)}) collective-permute-start(bf16[32,512]{1,0:T(8,128)(2,1)S(1)} %get-tuple-element.16), channel_id=1, source_target_pairs={{0,3},{1,4},{14,9},{15,10},{16,19},{17,20},{30,25},{31,26},{32,35}... | collective-permute-start | bytes 98312 | tf_op jit(solution)/shard_map/ppermute | solution.py:35
Sparse Core Ops, SparseCore 0:
  15.7 90.9 all-gather.1

commit v10 on v9

--- a/solution.py
+++ b/solution.py
@@ -19,22 +19,30 @@
     return default
 
 
-def spread(updated, parts, col_at):
-    share = updated.shape[0] // 32
-    lands = (0, 6, 0, 6)
+LANDS = (4, 7, 4, 7)
+
+
+def column_of(group, pos):
+    return group // 2 * 16 + (group % 2 * 8 + pos - 4) % 16
+
+
+def spread(parts, x_at, z_at):
+    share = parts[0].shape[0] // 8
+    turned = (z_at + 4) % 16
+    group, pos = x_at * 2 + turned // 8, turned % 8
+    landing = [[(LANDS[m] + h) % 8 for h in (0, 1)] for m in range(4)]
     sent = []
     for m in (3, 2, 1):
-        block = lax.ppermute(parts[m - 1], COL, [(h, 8 * m + lands[m] + h) for h in (0, 1)])
-        sent.append((col_at // 8 == m, block))
-    held = place(sent, updated[: 8 * share])
-    spot = col_at % 8
+        block = lax.ppermute(parts[m], COL, [(h, column_of(m, landing[m][h])) for h in (0, 1)])
+        sent.append((group == m, block))
+    held = place(sent, parts[0])
     got = []
     for d in range(1, 8):
-        piece = lax.dynamic_slice_in_dim(held, (spot + d) % 8 * share, share, 0)
-        pairs = [(8 * m + lands[m] + h, 8 * m + (lands[m] + h + d) % 8) for m in range(4) for h in (0, 1)]
+        piece = lax.dynamic_slice_in_dim(held, (pos + d) % 8 * share, share, 0)
+        pairs = [(column_of(m, at), column_of(m, (at + d) % 8)) for m in range(4) for at in landing[m]]
         got.append(lax.ppermute(piece, COL, pairs))
-    own = lax.dynamic_slice_in_dim(held, spot * share, share, 0)
-    apart = (spot - jnp.where(col_at // 8 % 2 == 0, lands[0], lands[1])) % 8
+    own = lax.dynamic_slice_in_dim(held, pos * share, share, 0)
+    apart = (pos - jnp.where(group % 2 == 0, LANDS[0], LANDS[1])) % 8
     left = place([(apart == d, got[d - 1]) for d in range(1, 8)], own)
     right = place([((apart - 1) % 8 == d, got[d - 1]) for d in range(1, 8)], own)
     return jnp.concatenate([left, right], axis=1)
@@ -43,7 +51,7 @@
 def update_kernel(
     left_ref, upper_ref, cols_ref, p_ref, q_ref, trailing_ref, out_ref, *rest
 ):
-    parts, (outer_ref, inner_ref, weights_ref, q_held, dense_ref, sems) = rest[:3], rest[3:]
+    parts, (outer_ref, inner_ref, weights_ref, q_held, dense_ref, sems) = rest[:4], rest[4:]
     rank_pad = p_ref.shape[2]
     depth = cols_ref.shape[4]
     copies = []
@@ -99,9 +107,11 @@
     product = lax.dot_general(outer, weights_ref[...], (((0,), (0,)), ((), ())), preferred_element_type=jnp.float32)
     done = (dense_ref[...].astype(jnp.float32) - product).astype(BF)
     out_ref[...] = done
-    part = done.shape[0] // 4
-    for m in range(1, 4):
-        parts[m - 1][...] = done[m * part : (m + 1) * part]
+    share = done.shape[0] // 32
+    for m, part_ref in enumerate(parts):
+        for pos in range(8):
+            at = column_of(m, pos) * share
+            part_ref[pos * share : (pos + 1) * share, :] = done[at : at + share]
 
 
 def update(left, upper, cols, p_rows, q_rows, trailing):
@@ -112,9 +122,9 @@
     held = pltpu.VMEM((NT, 2, half, depth), BF)
     return pl.pallas_call(
         update_kernel,
-        out_shape=[jax.ShapeDtypeStruct((height, width), BF)] + [jax.ShapeDtypeStruct((height // 4, width), BF)] * 3,
+        out_shape=[jax.ShapeDtypeStruct((height, width), BF)] + [jax.ShapeDtypeStruct((height // 4, width), BF)] * 4,
         in_specs=[smem, smem, hbm, vmem, hbm, hbm],
-        out_specs=[vmem] * 4,
+        out_specs=[vmem] * 5,
         scratch_shapes=[held, held, pltpu.VMEM((NT * rank_pad, width), BF), pltpu.VMEM(q_rows.shape, BF), pltpu.VMEM(trailing.shape, BF), pltpu.SemaphoreType.DMA((9,))],
         compiler_params=pltpu.CompilerParams(vmem_limit_bytes=LIMIT << 20),
     )(
@@ -158,7 +168,7 @@
     left = lax.dynamic_index_in_dim(left_ranks, row_at, 0, keepdims=False)
     upper = lax.dynamic_index_in_dim(upper_ranks, col_at // 2, 1, keepdims=False)
     updated, *parts = update(left, upper, cols, p_rows, q_rows, trailing)
-    return updated, spread(updated, parts, col_at)
+    return updated, spread(parts, x_at, z_at)
 
 
 def solution(mesh):

time: 163 us -> 160 us (0.982)
  the two profiles are of different devices: /device:TPU:1 before, /device:TPU:142 now
where the time goes in v10:
time: 160 us; the launch traced here: 159 us
  waiting for transfers between devices  58.8 us (37%)
  blocking collectives  40.4 us (25%)
  starting transfers between devices  27.3 us (17%)
  between operations  14.6 us (9%)
  Pallas kernels  8.61 us (5%)
  other arithmetic  8.28 us (5%)
    all_gather x1, waiting for transfers between devices, body(): cols = lax.all_gather(both, 'z', axis=0, tiled=True)  34.9 us
    all_to_all x1, blocking collectives, body(): lax.all_to_all(jnp.broadcast_to(rows[None], (NT // 2,) + rows.shape), 'ch...  31.5 us
    ppermute x7, starting transfers between devices, spread(): got.append(lax.ppermute(piece, COL, pairs))  18.9 us
    ppermute x3, waiting for transfers between devices, spread(): lax.ppermute(parts[m], COL, [(h, column_of(m, landing[m][h])) for h in (0...  15.9 us
    all_gather x1, blocking collectives, body(): both = lax.all_gather(both, 'xhi', axis=0, tiled=True)  8.93 us
    pallas_call x1, Pallas kernels, update(): pl.pallas_call(update_kernel, out_shape=[jax.ShapeDtypeStruct((height, wi...  8.61 us
    another operation x4, other arithmetic, whole(): jnp.stack([jnp.where(lower, own, far), jnp.where(lower, far, own)], axis=1)  4.73 us
    ppermute x1, starting transfers between devices, body(): partner = lax.ppermute(upper_outer, 'z', SWAP_Z)  3.83 us
  transfers between devices with their start and end apart: 13, of which 6 were waited for; matrix products, arithmetic and copies ran while one was open for 5% of the time, Pallas kernels for 0%

profile of v10, /device:TPU:142, one launch (start us, length us, event | category | flops | bytes accessed | tf_op | source)
XLA Modules:
  0.0 159.4 jit_solution(2570888702168584087)
XLA Ops:
  7.2 1.0 pad_maximum_fusion.3
  8.2 8.9 %all_gather.6 = bf16[192,1024]{1,0:T(8,128)(2,1)} all-gather(bf16[96,1024]{1,0:T(8,128)(2,1)S(1)} %pad_maximum_fusion.3), channel_id=1, replica_groups=mesh['chip'=8,'core'=2,'xhi'=2,'z'=16] {'xhi'}, dimensions={0}, use_global_device_ids=true | all-gather | bytes 589824 | tf_op jit(solution)/shard_map/all_gather | solution.py:148
  17.1 3.8 %collective-permute-start = (bf16[96,512]{1,0:T(8,128)(2,1)}, bf16[96,512]{1,0:T(8,128)(2,1)S(1)}, u32[]{:S(2)}, u32[]{:S(2)}) collective-permute-start(bf16[96,512]{1,0:T(8,128)(2,1)} %param.10), channel_id=1, source_target_pairs={{0,1},{1,0},{2,3},{3,2},{4,5},{5,4},{6,7},{7,6},{8,9},{9,8},{10,11... | collective-permute-start | bytes 294920 | tf_op jit(solution)/shard_map/ppermute | solution.py:149
  21.0 2.9 %collective-permute-done = bf16[96,512]{1,0:T(8,128)(2,1)S(1)} collective-permute-done((bf16[96,512]{1,0:T(8,128)(2,1)}, bf16[96,512]{1,0:T(8,128)(2,1)S(1)}, u32[]{:S(2)}, u32[]{:S(2)}) %collective-permute-start) | collective-permute-done | bytes 98336 | tf_op jit(solution)/shard_map/ppermute | solution.py:149
  23.9 0.9 broadcast_select_fusion.1
  24.8 0.9 pad_maximum_fusion.2
  25.7 0.2 broadcast_in_dim.2
  25.9 31.5 %all_to_all.5 = bf16[8,96,1536]{2,1,0:T(8,128)(2,1)S(1)} all-to-all(bf16[8,96,1536]{2,1,0:T(8,128)(2,1)S(1)} %broadcast_in_dim.2), channel_id=1, replica_groups=mesh['chip'=8,'core'=2,'xhi'=2,'z'=16] {'chip'}, dimensions={0} | all-to-all | bytes 4718592 | tf_op jit(solution)/shard_map/all_to_all | solution.py:157
  57.4 1.9 %collective-permute-start.1 = (bf16[8,96,1536]{2,1,0:T(8,128)(2,1)S(1)}, bf16[8,96,1536]{2,1,0:T(8,128)(2,1)}, u32[]{:S(2)}, u32[]{:S(2)}) collective-permute-start(bf16[8,96,1536]{2,1,0:T(8,128)(2,1)S(1)} %all_to_all.5), channel_id=1, source_target_pairs={{0,32},{32,0},{1,33},{33,1},{2,34},{34,2},{3,35},{35,3},{4,36},{36... | collective-permute-start | bytes 7077896 | tf_op jit(solution)/shard_map/ppermute | solution.py:158
  59.3 0.2 dynamic-slice_reduce_fusion.upper_ref
  59.5 0.7 fusion.left_ref
  60.2 3.7 %collective-permute-done.1 = bf16[8,96,1536]{2,1,0:T(8,128)(2,1)} collective-permute-done((bf16[8,96,1536]{2,1,0:T(8,128)(2,1)S(1)}, bf16[8,96,1536]{2,1,0:T(8,128)(2,1)}, u32[]{:S(2)}, u32[]{:S(2)}) %collective-permute-start.1) | collective-permute-done | bytes 2359328 | tf_op jit(solution)/shard_map/ppermute | solution.py:158
  63.9 1.6 %select_bitcast_fusion.1 = (bf16[8,1,96,1024]{3,2,0,1:T(8,128)(2,1)S(1)}, bf16[8,1,96,1024]{3,2,0,1:T(8,128)(2,1)S(1)}) fusion(pred[]{:T(512)S(6)} %eq.80, bf16[8,96,1536]{2,1,0:T(8,128)(2,1)} %collective-permute-done.1, bf16[8,96,1536]{2,1,0:T(8,128)(2,1)S(1)} %all_to_all.5), kind=kLoop, calls=%fused_computation.3 | loop fusion | flops 1572864 | bytes 6291457 | tf_op jit(solution)/shard_map/stack | solution.py:162
  65.6 0.3 pad_maximum_fusion
  65.9 0.3 copy.11
  66.2 1.5 select_bitcast_fusion.3
  67.7 1.3 pad_maximum_fusion.1
  69.0 34.9 %all-gather.2.cloned.1.call-done = bf16[3072,1024]{1,0:T(8,128)(2,1)} async-done(((bf16[192,1024]{1,0:T(8,128)(2,1)}), bf16[3072,1024]{1,0:T(8,128)(2,1)}) %all-gather.2.cloned.1.call-update) | async-done | bytes 6291472 | tf_op jit(solution)/shard_map/all_gather | solution.py:150
  103.8 8.6 %shard_map.86 = (bf16[1024,512]{1,0:T(8,128)(2,1)}, bf16[256,512]{1,0:T(8,128)(2,1)S(1)}, bf16[256,512]{1,0:T(8,128)(2,1)}, bf16[256,512]{1,0:T(8,128)(2,1)}, bf16[256,512]{1,0:T(8,128)(2,1)}) custom-call(s32[16]{0:T(128)S(1)} %fusion.left_ref, s32[16]{0:T(128)S(1)} %dynamic-slice_reduce_fusion.upper_ref, bf16[16,2,2,48,1024]{4,3,2,1,0:T(8,128)(2,1)} %bitcast.16, ...), custom_call_target="tpu_custom_call" | custom-call | tf_op jit(solution)/shard_map/pallas_call | solution.py:123
  112.5 0.7 collective-permute-start.2
  113.1 0.7 collective-permute-start.3
  113.8 1.3 collective-permute-start.4
  115.3 15.9 %collective-permute-done.4 = bf16[256,512]{1,0:T(8,128)(2,1)S(1)} collective-permute-done((bf16[256,512]{1,0:T(8,128)(2,1)}, bf16[256,512]{1,0:T(8,128)(2,1)S(1)}, u32[]{:S(2)}, u32[]{:S(2)}) %collective-permute-start.4) | collective-permute-done | bytes 262176 | tf_op jit(solution)/shard_map/ppermute | solution.py:36
  131.3 1.3 collective-permute-start.10
  132.6 1.9 %collective-permute-start.11 = (bf16[32,512]{1,0:T(8,128)(2,1)S(1)}, bf16[32,512]{1,0:T(8,128)(2,1)S(1)}, u32[]{:S(2)}, u32[]{:S(2)}) collective-permute-start(bf16[32,512]{1,0:T(8,128)(2,1)S(1)} %get-tuple-element.16), channel_id=1, source_target_pairs={{0,1},{1,2},{11,4},{4,5},{16,17},{17,18},{27,20},{20,21},{32,33},{... | collective-permute-start | bytes 98312 | tf_op jit(solution)/shard_map/ppermute | solution.py:43
  134.5 10.5 %collective-permute-start.5 = (bf16[32,512]{1,0:T(8,128)(2,1)S(1)}, bf16[32,512]{1,0:T(8,128)(2,1)S(1)}, u32[]{:S(2)}, u32[]{:S(2)}) collective-permute-start(bf16[32,512]{1,0:T(8,128)(2,1)S(1)} %get-tuple-element.22), channel_id=1, source_target_pairs={{0,15},{1,0},{11,10},{4,11},{16,31},{17,16},{27,26},{20,27},{32,47... | collective-permute-start | bytes 98312 | tf_op jit(solution)/shard_map/ppermute | solution.py:43
  145.1 1.3 collective-permute-start.6
  146.3 1.3 collective-permute-start.7
  147.7 1.3 collective-permute-start.8
  149.0 1.3 collective-permute-start.9
  150.5 1.3 collective-permute-done.9
  151.9 0.6 pad_maximum_fusion.4
  (18 shorter events, 0.4 us)
Async XLA Ops:
  7.2 52.1 %copy-start = (s32[16,16]{1,0:T(8,128)S(1)}, s32[16,16]{1,0:T(8,128)}, u32[]{:S(2)}) copy-start(s32[16,16]{1,0:T(8,128)} %param.13) | copy-start | bytes 3076
  7.2 96.7 %all-gather.2.cloned.1.call-start = ((), (), s32[]{:S(2)}) async-start(), calls=%async_computation.1 | async-start | bytes 6684672 | tf_op jit(solution)/shard_map/all_gather | solution.py:150
  17.1 6.7 %collective-permute-start = (bf16[96,512]{1,0:T(8,128)(2,1)}, bf16[96,512]{1,0:T(8,128)(2,1)S(1)}, u32[]{:S(2)}, u32[]{:S(2)}) collective-permute-start(bf16[96,512]{1,0:T(8,128)(2,1)} %param.10), channel_id=1, source_target_pairs={{0,1},{1,0},{2,3},{3,2},{4,5},{5,4},{6,7},{7,6},{8,9},{9,8},{10,11... | collective-permute-start | bytes 294920 | tf_op jit(solution)/shard_map/ppermute | solution.py:149
  57.4 8.2 %copy-start.1 = (bf16[8,96,1536]{2,1,0:T(8,128)(2,1)}, bf16[8,96,1536]{2,1,0:T(8,128)(2,1)S(1)}, u32[]{:S(2)}) copy-start(bf16[8,96,1536]{2,1,0:T(8,128)(2,1)S(1)} %all_to_all.5) | copy-start | bytes 7077892
  57.4 6.5 %collective-permute-start.1 = (bf16[8,96,1536]{2,1,0:T(8,128)(2,1)S(1)}, bf16[8,96,1536]{2,1,0:T(8,128)(2,1)}, u32[]{:S(2)}, u32[]{:S(2)}) collective-permute-start(bf16[8,96,1536]{2,1,0:T(8,128)(2,1)S(1)} %all_to_all.5), channel_id=1, source_target_pairs={{0,32},{32,0},{1,33},{33,1},{2,34},{34,2},{3,35},{35,3},{4,36},{36... | collective-permute-start | bytes 7077896 | tf_op jit(solution)/shard_map/ppermute | solution.py:158
  112.5 2.9 %collective-permute-start.2 = (bf16[256,512]{1,0:T(8,128)(2,1)}, bf16[256,512]{1,0:T(8,128)(2,1)S(1)}, u32[]{:S(2)}, u32[]{:S(2)}) collective-permute-start(bf16[256,512]{1,0:T(8,128)(2,1)} %get-tuple-element.8), channel_id=1, source_target_pairs={{0,11},{1,4},{32,43},{33,36},{64,75},{65,68},{96,107},{97,100},{12... | collective-permute-start | bytes 786440 | tf_op jit(solution)/shard_map/ppermute | solution.py:36
  113.1 2.2 %collective-permute-start.3 = (bf16[256,512]{1,0:T(8,128)(2,1)}, bf16[256,512]{1,0:T(8,128)(2,1)S(1)}, u32[]{:S(2)}, u32[]{:S(2)}) collective-permute-start(bf16[256,512]{1,0:T(8,128)(2,1)} %get-tuple-element.9), channel_id=1, source_target_pairs={{0,16},{1,17},{32,48},{33,49},{64,80},{65,81},{96,112},{97,113},{1... | collective-permute-start | bytes 786440 | tf_op jit(solution)/shard_map/ppermute | solution.py:36
  113.8 17.4 %collective-permute-start.4 = (bf16[256,512]{1,0:T(8,128)(2,1)}, bf16[256,512]{1,0:T(8,128)(2,1)S(1)}, u32[]{:S(2)}, u32[]{:S(2)}) collective-permute-start(bf16[256,512]{1,0:T(8,128)(2,1)} %get-tuple-element.10), channel_id=1, source_target_pairs={{0,27},{1,20},{32,59},{33,52},{64,91},{65,84},{96,123},{97,116},{1... | collective-permute-start | bytes 786440 | tf_op jit(solution)/shard_map/ppermute | solution.py:36
  131.3 16.4 %collective-permute-start.10 = (bf16[32,512]{1,0:T(8,128)(2,1)S(1)}, bf16[32,512]{1,0:T(8,128)(2,1)S(1)}, u32[]{:S(2)}, u32[]{:S(2)}) collective-permute-start(bf16[32,512]{1,0:T(8,128)(2,1)S(1)} %get-tuple-element.17), channel_id=1, source_target_pairs={{0,2},{1,3},{11,5},{4,6},{16,18},{17,19},{27,21},{20,22},{32,34},{... | collective-permute-start | bytes 98312 | tf_op jit(solution)/shard_map/ppermute | solution.py:43
  132.6 16.4 %collective-permute-start.11 = (bf16[32,512]{1,0:T(8,128)(2,1)S(1)}, bf16[32,512]{1,0:T(8,128)(2,1)S(1)}, u32[]{:S(2)}, u32[]{:S(2)}) collective-permute-start(bf16[32,512]{1,0:T(8,128)(2,1)S(1)} %get-tuple-element.16), channel_id=1, source_target_pairs={{0,1},{1,2},{11,4},{4,5},{16,17},{17,18},{27,20},{20,21},{32,33},{... | collective-permute-start | bytes 98312 | tf_op jit(solution)/shard_map/ppermute | solution.py:43
  134.5 15.8 %collective-permute-start.5 = (bf16[32,512]{1,0:T(8,128)(2,1)S(1)}, bf16[32,512]{1,0:T(8,128)(2,1)S(1)}, u32[]{:S(2)}, u32[]{:S(2)}) collective-permute-start(bf16[32,512]{1,0:T(8,128)(2,1)S(1)} %get-tuple-element.22), channel_id=1, source_target_pairs={{0,15},{1,0},{11,10},{4,11},{16,31},{17,16},{27,26},{20,27},{32,47... | collective-permute-start | bytes 98312 | tf_op jit(solution)/shard_map/ppermute | solution.py:43
  145.1 5.3 %collective-permute-start.6 = (bf16[32,512]{1,0:T(8,128)(2,1)S(1)}, bf16[32,512]{1,0:T(8,128)(2,1)S(1)}, u32[]{:S(2)}, u32[]{:S(2)}) collective-permute-start(bf16[32,512]{1,0:T(8,128)(2,1)S(1)} %get-tuple-element.21), channel_id=1, source_target_pairs={{0,14},{1,15},{11,9},{4,10},{16,30},{17,31},{27,25},{20,26},{32,46... | collective-permute-start | bytes 98312 | tf_op jit(solution)/shard_map/ppermute | solution.py:43
  146.3 4.0 %collective-permute-start.7 = (bf16[32,512]{1,0:T(8,128)(2,1)S(1)}, bf16[32,512]{1,0:T(8,128)(2,1)S(1)}, u32[]{:S(2)}, u32[]{:S(2)}) collective-permute-start(bf16[32,512]{1,0:T(8,128)(2,1)S(1)} %get-tuple-element.20), channel_id=1, source_target_pairs={{0,13},{1,14},{11,8},{4,9},{16,29},{17,30},{27,24},{20,25},{32,45}... | collective-permute-start | bytes 98312 | tf_op jit(solution)/shard_map/ppermute | solution.py:43
  147.7 2.9 %collective-permute-start.8 = (bf16[32,512]{1,0:T(8,128)(2,1)S(1)}, bf16[32,512]{1,0:T(8,128)(2,1)S(1)}, u32[]{:S(2)}, u32[]{:S(2)}) collective-permute-start(bf16[32,512]{1,0:T(8,128)(2,1)S(1)} %get-tuple-element.19), channel_id=1, source_target_pairs={{0,12},{1,13},{11,7},{4,8},{16,28},{17,29},{27,23},{20,24},{32,44}... | collective-permute-start | bytes 98312 | tf_op jit(solution)/shard_map/ppermute | solution.py:43
  149.0 2.9 %collective-permute-start.9 = (bf16[32,512]{1,0:T(8,128)(2,1)S(1)}, bf16[32,512]{1,0:T(8,128)(2,1)S(1)}, u32[]{:S(2)}, u32[]{:S(2)}) collective-permute-start(bf16[32,512]{1,0:T(8,128)(2,1)S(1)} %get-tuple-element.18), channel_id=1, source_target_pairs={{0,3},{1,12},{11,6},{4,7},{16,19},{17,28},{27,22},{20,23},{32,35},... | collective-permute-start | bytes 98312 | tf_op jit(solution)/shard_map/ppermute | solution.py:43
Sparse Core Ops, SparseCore 0:
  17.3 86.5 all-gather.1

commit v11 on v10

--- a/solution.py
+++ b/solution.py
@@ -20,6 +20,7 @@
 
 
 LANDS = (4, 7, 4, 7)
+STEPS = (3, 2, 7, 1, 6, 5, 4)
 
 
 def column_of(group, pos):
@@ -32,19 +33,19 @@
     group, pos = x_at * 2 + turned // 8, turned % 8
     landing = [[(LANDS[m] + h) % 8 for h in (0, 1)] for m in range(4)]
     sent = []
-    for m in (3, 2, 1):
+    for m in (2, 1, 3):
         block = lax.ppermute(parts[m], COL, [(h, column_of(m, landing[m][h])) for h in (0, 1)])
         sent.append((group == m, block))
     held = place(sent, parts[0])
-    got = []
-    for d in range(1, 8):
+    got = {}
+    for d in STEPS:
         piece = lax.dynamic_slice_in_dim(held, (pos + d) % 8 * share, share, 0)
         pairs = [(column_of(m, at), column_of(m, (at + d) % 8)) for m in range(4) for at in landing[m]]
-        got.append(lax.ppermute(piece, COL, pairs))
+        got[d] = lax.ppermute(piece, COL, pairs)
     own = lax.dynamic_slice_in_dim(held, pos * share, share, 0)
     apart = (pos - jnp.where(group % 2 == 0, LANDS[0], LANDS[1])) % 8
-    left = place([(apart == d, got[d - 1]) for d in range(1, 8)], own)
-    right = place([((apart - 1) % 8 == d, got[d - 1]) for d in range(1, 8)], own)
+    left = place([(apart == d, got[d]) for d in STEPS], own)
+    right = place([((apart - 1) % 8 == d, got[d]) for d in STEPS], own)
     return jnp.concatenate([left, right], axis=1)
 
 

time: 160 us -> 162 us (1.012)
  the two profiles are of different devices: /device:TPU:142 before, /device:TPU:360 now
where the time goes in v11:
time: 162 us
  waiting for transfers between devices  71.1 us (44%)
  blocking collectives  40.4 us (25%)
  starting transfers between devices  17.2 us (11%)
  between operations  14.6 us (9%)
  Pallas kernels  8.61 us (5%)
  other arithmetic  8.27 us (5%)
    all_to_all x1, blocking collectives, body(): lax.all_to_all(jnp.broadcast_to(rows[None], (NT // 2,) + rows.shape), 'ch...  31.5 us
    all_gather x1, waiting for transfers between devices, body(): cols = lax.all_gather(both, 'z', axis=0, tiled=True)  31.4 us
    ppermute x3, waiting for transfers between devices, spread(): lax.ppermute(parts[m], COL, [(h, column_of(m, landing[m][h])) for h in (0...  21.8 us
    ppermute x7, waiting for transfers between devices, spread(): got[d] = lax.ppermute(piece, COL, pairs)  10.4 us
    ppermute x7, starting transfers between devices, spread(): got[d] = lax.ppermute(piece, COL, pairs)  9.67 us
    all_gather x1, blocking collectives, body(): both = lax.all_gather(both, 'xhi', axis=0, tiled=True)  8.93 us
    pallas_call x1, Pallas kernels, update(): pl.pallas_call(update_kernel, out_shape=[jax.ShapeDtypeStruct((height, wi...  8.61 us
    another operation x4, other arithmetic, whole(): jnp.stack([jnp.where(lower, own, far), jnp.where(lower, far, own)], axis=1)  4.72 us
  transfers between devices with their start and end apart: 13, of which 5 were waited for; matrix products, arithmetic and copies ran while one was open for 5% of the time, Pallas kernels for 0%

profile of v11, /device:TPU:360, one launch (start us, length us, event | category | flops | bytes accessed | tf_op | source)
XLA Modules:
  0.0 161.6 jit_solution(13613825269841455751)
XLA Ops:
  7.2 1.0 pad_maximum_fusion.3
  8.2 8.9 %all_gather.6 = bf16[192,1024]{1,0:T(8,128)(2,1)} all-gather(bf16[96,1024]{1,0:T(8,128)(2,1)S(1)} %pad_maximum_fusion.3), channel_id=1, replica_groups=mesh['chip'=8,'core'=2,'xhi'=2,'z'=16] {'xhi'}, dimensions={0}, use_global_device_ids=true | all-gather | bytes 589824 | tf_op jit(solution)/shard_map/all_gather | solution.py:149
  17.1 2.9 %collective-permute-start = (bf16[96,512]{1,0:T(8,128)(2,1)}, bf16[96,512]{1,0:T(8,128)(2,1)S(1)}, u32[]{:S(2)}, u32[]{:S(2)}) collective-permute-start(bf16[96,512]{1,0:T(8,128)(2,1)} %param.10), channel_id=1, source_target_pairs={{0,1},{1,0},{2,3},{3,2},{4,5},{5,4},{6,7},{7,6},{8,9},{9,8},{10,11... | collective-permute-start | bytes 294920 | tf_op jit(solution)/shard_map/ppermute | solution.py:150
  20.1 3.8 %collective-permute-done = bf16[96,512]{1,0:T(8,128)(2,1)S(1)} collective-permute-done((bf16[96,512]{1,0:T(8,128)(2,1)}, bf16[96,512]{1,0:T(8,128)(2,1)S(1)}, u32[]{:S(2)}, u32[]{:S(2)}) %collective-permute-start) | collective-permute-done | bytes 98336 | tf_op jit(solution)/shard_map/ppermute | solution.py:150
  23.9 0.9 broadcast_select_fusion.1
  24.8 0.9 pad_maximum_fusion.2
  25.7 0.2 broadcast_in_dim.2
  25.9 31.5 %all_to_all.5 = bf16[8,96,1536]{2,1,0:T(8,128)(2,1)S(1)} all-to-all(bf16[8,96,1536]{2,1,0:T(8,128)(2,1)S(1)} %broadcast_in_dim.2), channel_id=1, replica_groups=mesh['chip'=8,'core'=2,'xhi'=2,'z'=16] {'chip'}, dimensions={0} | all-to-all | bytes 4718592 | tf_op jit(solution)/shard_map/all_to_all | solution.py:158
  57.4 1.9 %collective-permute-start.1 = (bf16[8,96,1536]{2,1,0:T(8,128)(2,1)S(1)}, bf16[8,96,1536]{2,1,0:T(8,128)(2,1)}, u32[]{:S(2)}, u32[]{:S(2)}) collective-permute-start(bf16[8,96,1536]{2,1,0:T(8,128)(2,1)S(1)} %all_to_all.5), channel_id=1, source_target_pairs={{0,32},{32,0},{1,33},{33,1},{2,34},{34,2},{3,35},{35,3},{4,36},{36... | collective-permute-start | bytes 7077896 | tf_op jit(solution)/shard_map/ppermute | solution.py:159
  59.4 0.2 dynamic-slice_reduce_fusion.upper_ref
  59.5 0.7 fusion.left_ref
  60.2 3.7 %collective-permute-done.1 = bf16[8,96,1536]{2,1,0:T(8,128)(2,1)} collective-permute-done((bf16[8,96,1536]{2,1,0:T(8,128)(2,1)S(1)}, bf16[8,96,1536]{2,1,0:T(8,128)(2,1)}, u32[]{:S(2)}, u32[]{:S(2)}) %collective-permute-start.1) | collective-permute-done | bytes 2359328 | tf_op jit(solution)/shard_map/ppermute | solution.py:159
  63.9 1.6 %select_bitcast_fusion.1 = (bf16[8,1,96,1024]{3,2,0,1:T(8,128)(2,1)S(1)}, bf16[8,1,96,1024]{3,2,0,1:T(8,128)(2,1)S(1)}) fusion(pred[]{:T(512)S(6)} %eq.80, bf16[8,96,1536]{2,1,0:T(8,128)(2,1)} %collective-permute-done.1, bf16[8,96,1536]{2,1,0:T(8,128)(2,1)S(1)} %all_to_all.5), kind=kLoop, calls=%fused_computation.3 | loop fusion | flops 1572864 | bytes 6291457 | tf_op jit(solution)/shard_map/stack | solution.py:163
  65.6 0.3 pad_maximum_fusion
  65.9 0.3 copy.11
  66.2 1.5 select_bitcast_fusion.3
  67.7 1.3 pad_maximum_fusion.1
  69.0 31.4 %all-gather.2.cloned.1.call-done = bf16[3072,1024]{1,0:T(8,128)(2,1)} async-done(((bf16[192,1024]{1,0:T(8,128)(2,1)}), bf16[3072,1024]{1,0:T(8,128)(2,1)}) %all-gather.2.cloned.1.call-update) | async-done | bytes 6291472 | tf_op jit(solution)/shard_map/all_gather | solution.py:151
  100.4 8.6 %shard_map.86 = (bf16[1024,512]{1,0:T(8,128)(2,1)}, bf16[256,512]{1,0:T(8,128)(2,1)S(1)}, bf16[256,512]{1,0:T(8,128)(2,1)}, bf16[256,512]{1,0:T(8,128)(2,1)}, bf16[256,512]{1,0:T(8,128)(2,1)}) custom-call(s32[16]{0:T(128)S(1)} %fusion.left_ref, s32[16]{0:T(128)S(1)} %dynamic-slice_reduce_fusion.upper_ref, bf16[16,2,2,48,1024]{4,3,2,1,0:T(8,128)(2,1)} %bitcast.16, ...), custom_call_target="tpu_custom_call" | custom-call | tf_op jit(solution)/shard_map/pallas_call | solution.py:124
  109.0 0.7 collective-permute-start.2
  109.7 1.3 collective-permute-start.3
  111.0 0.7 collective-permute-start.4
  111.9 21.8 %collective-permute-done.3 = bf16[256,512]{1,0:T(8,128)(2,1)S(1)} collective-permute-done((bf16[256,512]{1,0:T(8,128)(2,1)}, bf16[256,512]{1,0:T(8,128)(2,1)S(1)}, u32[]{:S(2)}, u32[]{:S(2)}) %collective-permute-start.3) | collective-permute-done | bytes 262176 | tf_op jit(solution)/shard_map/ppermute | solution.py:37
  133.8 1.3 collective-permute-start.10
  135.1 1.3 collective-permute-start.11
  136.4 1.3 collective-permute-start.5
  137.7 1.3 collective-permute-start.6
  139.0 1.3 collective-permute-start.7
  140.3 1.3 collective-permute-start.8
  141.6 1.9 %collective-permute-start.9 = (bf16[32,512]{1,0:T(8,128)(2,1)S(1)}, bf16[32,512]{1,0:T(8,128)(2,1)S(1)}, u32[]{:S(2)}, u32[]{:S(2)}) collective-permute-start(bf16[32,512]{1,0:T(8,128)(2,1)S(1)} %get-tuple-element.18), channel_id=1, source_target_pairs={{0,15},{1,0},{11,10},{4,11},{16,31},{17,16},{27,26},{20,27},{32,47... | collective-permute-start | bytes 98312 | tf_op jit(solution)/shard_map/ppermute | solution.py:44
  143.6 10.4 %collective-permute-done.9 = bf16[32,512]{1,0:T(8,128)(2,1)S(1)} collective-permute-done((bf16[32,512]{1,0:T(8,128)(2,1)S(1)}, bf16[32,512]{1,0:T(8,128)(2,1)S(1)}, u32[]{:S(2)}, u32[]{:S(2)}) %collective-permute-start.9) | collective-permute-done | bytes 32800 | tf_op jit(solution)/shard_map/ppermute | solution.py:44
  154.1 0.6 pad_maximum_fusion.4
  (18 shorter events, 0.3 us)
Async XLA Ops:
  7.2 52.2 %copy-start = (s32[16,16]{1,0:T(8,128)S(1)}, s32[16,16]{1,0:T(8,128)}, u32[]{:S(2)}) copy-start(s32[16,16]{1,0:T(8,128)} %param.13) | copy-start | bytes 3076
  7.2 93.2 %all-gather.2.cloned.1.call-start = ((), (), s32[]{:S(2)}) async-start(), calls=%async_computation.1 | async-start | bytes 6684672 | tf_op jit(solution)/shard_map/all_gather | solution.py:151
  17.1 6.7 %collective-permute-start = (bf16[96,512]{1,0:T(8,128)(2,1)}, bf16[96,512]{1,0:T(8,128)(2,1)S(1)}, u32[]{:S(2)}, u32[]{:S(2)}) collective-permute-start(bf16[96,512]{1,0:T(8,128)(2,1)} %param.10), channel_id=1, source_target_pairs={{0,1},{1,0},{2,3},{3,2},{4,5},{5,4},{6,7},{7,6},{8,9},{9,8},{10,11... | collective-permute-start | bytes 294920 | tf_op jit(solution)/shard_map/ppermute | solution.py:150
  57.4 8.2 %copy-start.1 = (bf16[8,96,1536]{2,1,0:T(8,128)(2,1)}, bf16[8,96,1536]{2,1,0:T(8,128)(2,1)S(1)}, u32[]{:S(2)}) copy-start(bf16[8,96,1536]{2,1,0:T(8,128)(2,1)S(1)} %all_to_all.5) | copy-start | bytes 7077892
  57.4 6.5 %collective-permute-start.1 = (bf16[8,96,1536]{2,1,0:T(8,128)(2,1)S(1)}, bf16[8,96,1536]{2,1,0:T(8,128)(2,1)}, u32[]{:S(2)}, u32[]{:S(2)}) collective-permute-start(bf16[8,96,1536]{2,1,0:T(8,128)(2,1)S(1)} %all_to_all.5), channel_id=1, source_target_pairs={{0,32},{32,0},{1,33},{33,1},{2,34},{34,2},{3,35},{35,3},{4,36},{36... | collective-permute-start | bytes 7077896 | tf_op jit(solution)/shard_map/ppermute | solution.py:159
  109.0 2.9 %collective-permute-start.2 = (bf16[256,512]{1,0:T(8,128)(2,1)}, bf16[256,512]{1,0:T(8,128)(2,1)S(1)}, u32[]{:S(2)}, u32[]{:S(2)}) collective-permute-start(bf16[256,512]{1,0:T(8,128)(2,1)} %get-tuple-element.8), channel_id=1, source_target_pairs={{0,27},{1,20},{32,59},{33,52},{64,91},{65,84},{96,123},{97,116},{1... | collective-permute-start | bytes 786440 | tf_op jit(solution)/shard_map/ppermute | solution.py:37
  109.7 23.9 %collective-permute-start.3 = (bf16[256,512]{1,0:T(8,128)(2,1)}, bf16[256,512]{1,0:T(8,128)(2,1)S(1)}, u32[]{:S(2)}, u32[]{:S(2)}) collective-permute-start(bf16[256,512]{1,0:T(8,128)(2,1)} %get-tuple-element.9), channel_id=1, source_target_pairs={{0,11},{1,4},{32,43},{33,36},{64,75},{65,68},{96,107},{97,100},{12... | collective-permute-start | bytes 786440 | tf_op jit(solution)/shard_map/ppermute | solution.py:37
  111.0 22.6 %collective-permute-start.4 = (bf16[256,512]{1,0:T(8,128)(2,1)}, bf16[256,512]{1,0:T(8,128)(2,1)S(1)}, u32[]{:S(2)}, u32[]{:S(2)}) collective-permute-start(bf16[256,512]{1,0:T(8,128)(2,1)} %get-tuple-element.10), channel_id=1, source_target_pairs={{0,16},{1,17},{32,48},{33,49},{64,80},{65,81},{96,112},{97,113},{1... | collective-permute-start | bytes 786440 | tf_op jit(solution)/shard_map/ppermute | solution.py:37
  133.8 6.5 %collective-permute-start.10 = (bf16[32,512]{1,0:T(8,128)(2,1)S(1)}, bf16[32,512]{1,0:T(8,128)(2,1)S(1)}, u32[]{:S(2)}, u32[]{:S(2)}) collective-permute-start(bf16[32,512]{1,0:T(8,128)(2,1)S(1)} %get-tuple-element.17), channel_id=1, source_target_pairs={{0,2},{1,3},{11,5},{4,6},{16,18},{17,19},{27,21},{20,22},{32,34},{... | collective-permute-start | bytes 98312 | tf_op jit(solution)/shard_map/ppermute | solution.py:44
  135.1 6.5 %collective-permute-start.11 = (bf16[32,512]{1,0:T(8,128)(2,1)S(1)}, bf16[32,512]{1,0:T(8,128)(2,1)S(1)}, u32[]{:S(2)}, u32[]{:S(2)}) collective-permute-start(bf16[32,512]{1,0:T(8,128)(2,1)S(1)} %get-tuple-element.16), channel_id=1, source_target_pairs={{0,3},{1,12},{11,6},{4,7},{16,19},{17,28},{27,22},{20,23},{32,35},... | collective-permute-start | bytes 98312 | tf_op jit(solution)/shard_map/ppermute | solution.py:44
  136.4 7.2 %collective-permute-start.5 = (bf16[32,512]{1,0:T(8,128)(2,1)S(1)}, bf16[32,512]{1,0:T(8,128)(2,1)S(1)}, u32[]{:S(2)}, u32[]{:S(2)}) collective-permute-start(bf16[32,512]{1,0:T(8,128)(2,1)S(1)} %get-tuple-element.22), channel_id=1, source_target_pairs={{0,12},{1,13},{11,7},{4,8},{16,28},{17,29},{27,23},{20,24},{32,44}... | collective-permute-start | bytes 98312 | tf_op jit(solution)/shard_map/ppermute | solution.py:44
  137.7 5.9 %collective-permute-start.6 = (bf16[32,512]{1,0:T(8,128)(2,1)S(1)}, bf16[32,512]{1,0:T(8,128)(2,1)S(1)}, u32[]{:S(2)}, u32[]{:S(2)}) collective-permute-start(bf16[32,512]{1,0:T(8,128)(2,1)S(1)} %get-tuple-element.21), channel_id=1, source_target_pairs={{0,13},{1,14},{11,8},{4,9},{16,29},{17,30},{27,24},{20,25},{32,45}... | collective-permute-start | bytes 98312 | tf_op jit(solution)/shard_map/ppermute | solution.py:44
  139.0 4.7 %collective-permute-start.7 = (bf16[32,512]{1,0:T(8,128)(2,1)S(1)}, bf16[32,512]{1,0:T(8,128)(2,1)S(1)}, u32[]{:S(2)}, u32[]{:S(2)}) collective-permute-start(bf16[32,512]{1,0:T(8,128)(2,1)S(1)} %get-tuple-element.20), channel_id=1, source_target_pairs={{0,14},{1,15},{11,9},{4,10},{16,30},{17,31},{27,25},{20,26},{32,46... | collective-permute-start | bytes 98312 | tf_op jit(solution)/shard_map/ppermute | solution.py:44
  140.3 3.4 %collective-permute-start.8 = (bf16[32,512]{1,0:T(8,128)(2,1)S(1)}, bf16[32,512]{1,0:T(8,128)(2,1)S(1)}, u32[]{:S(2)}, u32[]{:S(2)}) collective-permute-start(bf16[32,512]{1,0:T(8,128)(2,1)S(1)} %get-tuple-element.19), channel_id=1, source_target_pairs={{0,1},{1,2},{11,4},{4,5},{16,17},{17,18},{27,20},{20,21},{32,33},{... | collective-permute-start | bytes 98312 | tf_op jit(solution)/shard_map/ppermute | solution.py:44
  141.6 12.4 %collective-permute-start.9 = (bf16[32,512]{1,0:T(8,128)(2,1)S(1)}, bf16[32,512]{1,0:T(8,128)(2,1)S(1)}, u32[]{:S(2)}, u32[]{:S(2)}) collective-permute-start(bf16[32,512]{1,0:T(8,128)(2,1)S(1)} %get-tuple-element.18), channel_id=1, source_target_pairs={{0,15},{1,0},{11,10},{4,11},{16,31},{17,16},{27,26},{20,27},{32,47... | collective-permute-start | bytes 98312 | tf_op jit(solution)/shard_map/ppermute | solution.py:44
Sparse Core Ops, SparseCore 0:
  17.3 83.1 all-gather.1

commit v12 on v11

--- a/solution.py
+++ b/solution.py
@@ -33,7 +33,7 @@
     group, pos = x_at * 2 + turned // 8, turned % 8
     landing = [[(LANDS[m] + h) % 8 for h in (0, 1)] for m in range(4)]
     sent = []
-    for m in (2, 1, 3):
+    for m in (3, 2, 1):
         block = lax.ppermute(parts[m], COL, [(h, column_of(m, landing[m][h])) for h in (0, 1)])
         sent.append((group == m, block))
     held = place(sent, parts[0])

time: 162 us -> 161 us (level)
  the two profiles are of different devices: /device:TPU:360 before, /device:TPU:358 now
where the time goes in v12:
time: 161 us; the launch traced here: 160 us
  waiting for transfers between devices  69.1 us (43%)
  blocking collectives  40.9 us (25%)
  starting transfers between devices  17.2 us (11%)
  between operations  14.6 us (9%)
  Pallas kernels  8.61 us (5%)
  other arithmetic  8.27 us (5%)
    all_to_all x1, blocking collectives, body(): lax.all_to_all(jnp.broadcast_to(rows[None], (NT // 2,) + rows.shape), 'ch...  32 us
    all_gather x1, waiting for transfers between devices, body(): cols = lax.all_gather(both, 'z', axis=0, tiled=True)  30.9 us
    ppermute x3, waiting for transfers between devices, spread(): lax.ppermute(parts[m], COL, [(h, column_of(m, landing[m][h])) for h in (0...  20.3 us
    ppermute x7, waiting for transfers between devices, spread(): got[d] = lax.ppermute(piece, COL, pairs)  10.4 us
    ppermute x7, starting transfers between devices, spread(): got[d] = lax.ppermute(piece, COL, pairs)  9.67 us
    all_gather x1, blocking collectives, body(): both = lax.all_gather(both, 'xhi', axis=0, tiled=True)  8.93 us
    pallas_call x1, Pallas kernels, update(): pl.pallas_call(update_kernel, out_shape=[jax.ShapeDtypeStruct((height, wi...  8.61 us
    another operation x4, other arithmetic, whole(): jnp.stack([jnp.where(lower, own, far), jnp.where(lower, far, own)], axis=1)  4.72 us
  transfers between devices with their start and end apart: 13, of which 5 were waited for; matrix products, arithmetic and copies ran while one was open for 5% of the time, Pallas kernels for 0%

profile of v12, /device:TPU:358, one launch (start us, length us, event | category | flops | bytes accessed | tf_op | source)
XLA Modules:
  0.0 160.1 jit_solution(3746756501743001975)
XLA Ops:
  7.2 1.0 pad_maximum_fusion.3
  8.2 8.9 %all_gather.6 = bf16[192,1024]{1,0:T(8,128)(2,1)} all-gather(bf16[96,1024]{1,0:T(8,128)(2,1)S(1)} %pad_maximum_fusion.3), channel_id=1, replica_groups=mesh['chip'=8,'core'=2,'xhi'=2,'z'=16] {'xhi'}, dimensions={0}, use_global_device_ids=true | all-gather | bytes 589824 | tf_op jit(solution)/shard_map/all_gather | solution.py:149
  17.1 2.9 %collective-permute-start = (bf16[96,512]{1,0:T(8,128)(2,1)}, bf16[96,512]{1,0:T(8,128)(2,1)S(1)}, u32[]{:S(2)}, u32[]{:S(2)}) collective-permute-start(bf16[96,512]{1,0:T(8,128)(2,1)} %param.10), channel_id=1, source_target_pairs={{0,1},{1,0},{2,3},{3,2},{4,5},{5,4},{6,7},{7,6},{8,9},{9,8},{10,11... | collective-permute-start | bytes 294920 | tf_op jit(solution)/shard_map/ppermute | solution.py:150
  20.1 3.8 %collective-permute-done = bf16[96,512]{1,0:T(8,128)(2,1)S(1)} collective-permute-done((bf16[96,512]{1,0:T(8,128)(2,1)}, bf16[96,512]{1,0:T(8,128)(2,1)S(1)}, u32[]{:S(2)}, u32[]{:S(2)}) %collective-permute-start) | collective-permute-done | bytes 98336 | tf_op jit(solution)/shard_map/ppermute | solution.py:150
  23.9 0.9 broadcast_select_fusion.1
  24.8 0.9 pad_maximum_fusion.2
  25.7 0.2 broadcast_in_dim.2
  25.9 32.0 %all_to_all.5 = bf16[8,96,1536]{2,1,0:T(8,128)(2,1)S(1)} all-to-all(bf16[8,96,1536]{2,1,0:T(8,128)(2,1)S(1)} %broadcast_in_dim.2), channel_id=1, replica_groups=mesh['chip'=8,'core'=2,'xhi'=2,'z'=16] {'chip'}, dimensions={0} | all-to-all | bytes 4718592 | tf_op jit(solution)/shard_map/all_to_all | solution.py:158
  57.9 1.9 %collective-permute-start.1 = (bf16[8,96,1536]{2,1,0:T(8,128)(2,1)S(1)}, bf16[8,96,1536]{2,1,0:T(8,128)(2,1)}, u32[]{:S(2)}, u32[]{:S(2)}) collective-permute-start(bf16[8,96,1536]{2,1,0:T(8,128)(2,1)S(1)} %all_to_all.5), channel_id=1, source_target_pairs={{0,32},{32,0},{1,33},{33,1},{2,34},{34,2},{3,35},{35,3},{4,36},{36... | collective-permute-start | bytes 7077896 | tf_op jit(solution)/shard_map/ppermute | solution.py:159
  59.8 0.2 dynamic-slice_reduce_fusion.upper_ref
  60.0 0.7 fusion.left_ref
  60.7 3.7 %collective-permute-done.1 = bf16[8,96,1536]{2,1,0:T(8,128)(2,1)} collective-permute-done((bf16[8,96,1536]{2,1,0:T(8,128)(2,1)S(1)}, bf16[8,96,1536]{2,1,0:T(8,128)(2,1)}, u32[]{:S(2)}, u32[]{:S(2)}) %collective-permute-start.1) | collective-permute-done | bytes 2359328 | tf_op jit(solution)/shard_map/ppermute | solution.py:159
  64.4 1.6 %select_bitcast_fusion.1 = (bf16[8,1,96,1024]{3,2,0,1:T(8,128)(2,1)S(1)}, bf16[8,1,96,1024]{3,2,0,1:T(8,128)(2,1)S(1)}) fusion(pred[]{:T(512)S(6)} %eq.80, bf16[8,96,1536]{2,1,0:T(8,128)(2,1)} %collective-permute-done.1, bf16[8,96,1536]{2,1,0:T(8,128)(2,1)S(1)} %all_to_all.5), kind=kLoop, calls=%fused_computation.3 | loop fusion | flops 1572864 | bytes 6291457 | tf_op jit(solution)/shard_map/stack | solution.py:163
  66.1 0.3 pad_maximum_fusion
  66.4 0.3 copy.11
  66.7 1.5 select_bitcast_fusion.3
  68.2 1.3 pad_maximum_fusion.1
  69.5 30.9 %all-gather.2.cloned.1.call-done = bf16[3072,1024]{1,0:T(8,128)(2,1)} async-done(((bf16[192,1024]{1,0:T(8,128)(2,1)}), bf16[3072,1024]{1,0:T(8,128)(2,1)}) %all-gather.2.cloned.1.call-update) | async-done | bytes 6291472 | tf_op jit(solution)/shard_map/all_gather | solution.py:151
  100.4 8.6 %shard_map.86 = (bf16[1024,512]{1,0:T(8,128)(2,1)}, bf16[256,512]{1,0:T(8,128)(2,1)S(1)}, bf16[256,512]{1,0:T(8,128)(2,1)}, bf16[256,512]{1,0:T(8,128)(2,1)}, bf16[256,512]{1,0:T(8,128)(2,1)}) custom-call(s32[16]{0:T(128)S(1)} %fusion.left_ref, s32[16]{0:T(128)S(1)} %dynamic-slice_reduce_fusion.upper_ref, bf16[16,2,2,48,1024]{4,3,2,1,0:T(8,128)(2,1)} %bitcast.16, ...), custom_call_target="tpu_custom_call" | custom-call | tf_op jit(solution)/shard_map/pallas_call | solution.py:124
  109.0 0.7 collective-permute-start.2
  109.7 0.7 collective-permute-start.3
  110.4 1.3 collective-permute-start.4
  111.9 20.3 %collective-permute-done.4 = bf16[256,512]{1,0:T(8,128)(2,1)S(1)} collective-permute-done((bf16[256,512]{1,0:T(8,128)(2,1)}, bf16[256,512]{1,0:T(8,128)(2,1)S(1)}, u32[]{:S(2)}, u32[]{:S(2)}) %collective-permute-start.4) | collective-permute-done | bytes 262176 | tf_op jit(solution)/shard_map/ppermute | solution.py:37
  132.3 1.3 collective-permute-start.10
  133.6 1.3 collective-permute-start.11
  134.9 1.3 collective-permute-start.5
  136.2 1.3 collective-permute-start.6
  137.5 1.3 collective-permute-start.7
  138.8 1.3 collective-permute-start.8
  140.1 1.9 %collective-permute-start.9 = (bf16[32,512]{1,0:T(8,128)(2,1)S(1)}, bf16[32,512]{1,0:T(8,128)(2,1)S(1)}, u32[]{:S(2)}, u32[]{:S(2)}) collective-permute-start(bf16[32,512]{1,0:T(8,128)(2,1)S(1)} %get-tuple-element.18), channel_id=1, source_target_pairs={{0,15},{1,0},{11,10},{4,11},{16,31},{17,16},{27,26},{20,27},{32,47... | collective-permute-start | bytes 98312 | tf_op jit(solution)/shard_map/ppermute | solution.py:44
  142.1 10.4 %collective-permute-done.9 = bf16[32,512]{1,0:T(8,128)(2,1)S(1)} collective-permute-done((bf16[32,512]{1,0:T(8,128)(2,1)S(1)}, bf16[32,512]{1,0:T(8,128)(2,1)S(1)}, u32[]{:S(2)}, u32[]{:S(2)}) %collective-permute-start.9) | collective-permute-done | bytes 32800 | tf_op jit(solution)/shard_map/ppermute | solution.py:44
  152.6 0.6 pad_maximum_fusion.4
  (18 shorter events, 0.3 us)
Async XLA Ops:
  7.2 52.7 %copy-start = (s32[16,16]{1,0:T(8,128)S(1)}, s32[16,16]{1,0:T(8,128)}, u32[]{:S(2)}) copy-start(s32[16,16]{1,0:T(8,128)} %param.13) | copy-start | bytes 3076
  7.2 93.2 %all-gather.2.cloned.1.call-start = ((), (), s32[]{:S(2)}) async-start(), calls=%async_computation.1 | async-start | bytes 6684672 | tf_op jit(solution)/shard_map/all_gather | solution.py:151
  17.1 6.7 %collective-permute-start = (bf16[96,512]{1,0:T(8,128)(2,1)}, bf16[96,512]{1,0:T(8,128)(2,1)S(1)}, u32[]{:S(2)}, u32[]{:S(2)}) collective-permute-start(bf16[96,512]{1,0:T(8,128)(2,1)} %param.10), channel_id=1, source_target_pairs={{0,1},{1,0},{2,3},{3,2},{4,5},{5,4},{6,7},{7,6},{8,9},{9,8},{10,11... | collective-permute-start | bytes 294920 | tf_op jit(solution)/shard_map/ppermute | solution.py:150
  57.9 8.2 %copy-start.1 = (bf16[8,96,1536]{2,1,0:T(8,128)(2,1)}, bf16[8,96,1536]{2,1,0:T(8,128)(2,1)S(1)}, u32[]{:S(2)}) copy-start(bf16[8,96,1536]{2,1,0:T(8,128)(2,1)S(1)} %all_to_all.5) | copy-start | bytes 7077892
  57.9 6.5 %collective-permute-start.1 = (bf16[8,96,1536]{2,1,0:T(8,128)(2,1)S(1)}, bf16[8,96,1536]{2,1,0:T(8,128)(2,1)}, u32[]{:S(2)}, u32[]{:S(2)}) collective-permute-start(bf16[8,96,1536]{2,1,0:T(8,128)(2,1)S(1)} %all_to_all.5), channel_id=1, source_target_pairs={{0,32},{32,0},{1,33},{33,1},{2,34},{34,2},{3,35},{35,3},{4,36},{36... | collective-permute-start | bytes 7077896 | tf_op jit(solution)/shard_map/ppermute | solution.py:159
  109.0 2.9 %collective-permute-start.2 = (bf16[256,512]{1,0:T(8,128)(2,1)}, bf16[256,512]{1,0:T(8,128)(2,1)S(1)}, u32[]{:S(2)}, u32[]{:S(2)}) collective-permute-start(bf16[256,512]{1,0:T(8,128)(2,1)} %get-tuple-element.8), channel_id=1, source_target_pairs={{0,11},{1,4},{32,43},{33,36},{64,75},{65,68},{96,107},{97,100},{12... | collective-permute-start | bytes 786440 | tf_op jit(solution)/shard_map/ppermute | solution.py:37
  109.7 2.2 %collective-permute-start.3 = (bf16[256,512]{1,0:T(8,128)(2,1)}, bf16[256,512]{1,0:T(8,128)(2,1)S(1)}, u32[]{:S(2)}, u32[]{:S(2)}) collective-permute-start(bf16[256,512]{1,0:T(8,128)(2,1)} %get-tuple-element.9), channel_id=1, source_target_pairs={{0,16},{1,17},{32,48},{33,49},{64,80},{65,81},{96,112},{97,113},{1... | collective-permute-start | bytes 786440 | tf_op jit(solution)/shard_map/ppermute | solution.py:37
  110.4 21.8 %collective-permute-start.4 = (bf16[256,512]{1,0:T(8,128)(2,1)}, bf16[256,512]{1,0:T(8,128)(2,1)S(1)}, u32[]{:S(2)}, u32[]{:S(2)}) collective-permute-start(bf16[256,512]{1,0:T(8,128)(2,1)} %get-tuple-element.10), channel_id=1, source_target_pairs={{0,27},{1,20},{32,59},{33,52},{64,91},{65,84},{96,123},{97,116},{1... | collective-permute-start | bytes 786440 | tf_op jit(solution)/shard_map/ppermute | solution.py:37
  132.3 6.5 %collective-permute-start.10 = (bf16[32,512]{1,0:T(8,128)(2,1)S(1)}, bf16[32,512]{1,0:T(8,128)(2,1)S(1)}, u32[]{:S(2)}, u32[]{:S(2)}) collective-permute-start(bf16[32,512]{1,0:T(8,128)(2,1)S(1)} %get-tuple-element.17), channel_id=1, source_target_pairs={{0,2},{1,3},{11,5},{4,6},{16,18},{17,19},{27,21},{20,22},{32,34},{... | collective-permute-start | bytes 98312 | tf_op jit(solution)/shard_map/ppermute | solution.py:44
  133.6 6.5 %collective-permute-start.11 = (bf16[32,512]{1,0:T(8,128)(2,1)S(1)}, bf16[32,512]{1,0:T(8,128)(2,1)S(1)}, u32[]{:S(2)}, u32[]{:S(2)}) collective-permute-start(bf16[32,512]{1,0:T(8,128)(2,1)S(1)} %get-tuple-element.16), channel_id=1, source_target_pairs={{0,3},{1,12},{11,6},{4,7},{16,19},{17,28},{27,22},{20,23},{32,35},... | collective-permute-start | bytes 98312 | tf_op jit(solution)/shard_map/ppermute | solution.py:44
  134.9 7.2 %collective-permute-start.5 = (bf16[32,512]{1,0:T(8,128)(2,1)S(1)}, bf16[32,512]{1,0:T(8,128)(2,1)S(1)}, u32[]{:S(2)}, u32[]{:S(2)}) collective-permute-start(bf16[32,512]{1,0:T(8,128)(2,1)S(1)} %get-tuple-element.22), channel_id=1, source_target_pairs={{0,12},{1,13},{11,7},{4,8},{16,28},{17,29},{27,23},{20,24},{32,44}... | collective-permute-start | bytes 98312 | tf_op jit(solution)/shard_map/ppermute | solution.py:44
  136.2 5.9 %collective-permute-start.6 = (bf16[32,512]{1,0:T(8,128)(2,1)S(1)}, bf16[32,512]{1,0:T(8,128)(2,1)S(1)}, u32[]{:S(2)}, u32[]{:S(2)}) collective-permute-start(bf16[32,512]{1,0:T(8,128)(2,1)S(1)} %get-tuple-element.21), channel_id=1, source_target_pairs={{0,13},{1,14},{11,8},{4,9},{16,29},{17,30},{27,24},{20,25},{32,45}... | collective-permute-start | bytes 98312 | tf_op jit(solution)/shard_map/ppermute | solution.py:44
  137.5 4.7 %collective-permute-start.7 = (bf16[32,512]{1,0:T(8,128)(2,1)S(1)}, bf16[32,512]{1,0:T(8,128)(2,1)S(1)}, u32[]{:S(2)}, u32[]{:S(2)}) collective-permute-start(bf16[32,512]{1,0:T(8,128)(2,1)S(1)} %get-tuple-element.20), channel_id=1, source_target_pairs={{0,14},{1,15},{11,9},{4,10},{16,30},{17,31},{27,25},{20,26},{32,46... | collective-permute-start | bytes 98312 | tf_op jit(solution)/shard_map/ppermute | solution.py:44
  138.8 3.4 %collective-permute-start.8 = (bf16[32,512]{1,0:T(8,128)(2,1)S(1)}, bf16[32,512]{1,0:T(8,128)(2,1)S(1)}, u32[]{:S(2)}, u32[]{:S(2)}) collective-permute-start(bf16[32,512]{1,0:T(8,128)(2,1)S(1)} %get-tuple-element.19), channel_id=1, source_target_pairs={{0,1},{1,2},{11,4},{4,5},{16,17},{17,18},{27,20},{20,21},{32,33},{... | collective-permute-start | bytes 98312 | tf_op jit(solution)/shard_map/ppermute | solution.py:44
  140.1 12.4 %collective-permute-start.9 = (bf16[32,512]{1,0:T(8,128)(2,1)S(1)}, bf16[32,512]{1,0:T(8,128)(2,1)S(1)}, u32[]{:S(2)}, u32[]{:S(2)}) collective-permute-start(bf16[32,512]{1,0:T(8,128)(2,1)S(1)} %get-tuple-element.18), channel_id=1, source_target_pairs={{0,15},{1,0},{11,10},{4,11},{16,31},{17,16},{27,26},{20,27},{32,47... | collective-permute-start | bytes 98312 | tf_op jit(solution)/shard_map/ppermute | solution.py:44
Sparse Core Ops, SparseCore 0:
  17.3 83.1 all-gather.1

commit v13 on v12

--- a/solution.py
+++ b/solution.py
@@ -19,17 +19,17 @@
     return default
 
 
-LANDS = (4, 7, 4, 7)
+LANDS = (3, 7, 3, 7)
 STEPS = (3, 2, 7, 1, 6, 5, 4)
 
 
 def column_of(group, pos):
-    return group // 2 * 16 + (group % 2 * 8 + pos - 4) % 16
+    return group // 2 * 16 + (group % 2 * 8 + pos - 3) % 16
 
 
 def spread(parts, x_at, z_at):
     share = parts[0].shape[0] // 8
-    turned = (z_at + 4) % 16
+    turned = (z_at + 3) % 16
     group, pos = x_at * 2 + turned // 8, turned % 8
     landing = [[(LANDS[m] + h) % 8 for h in (0, 1)] for m in range(4)]
     sent = []

time: 161 us -> 164 us (1.019)
  the two profiles are of different devices: /device:TPU:358 before, /device:TPU:398 now
where the time goes in v13:
time: 164 us
  waiting for transfers between devices  68.3 us (42%)
  blocking collectives  40.2 us (25%)
  starting transfers between devices  22.4 us (14%)
  between operations  14.6 us (9%)
  Pallas kernels  8.62 us (5%)
  other arithmetic  8.29 us (5%)
    all_gather x1, waiting for transfers between devices, body(): cols = lax.all_gather(both, 'z', axis=0, tiled=True)  31.9 us
    all_to_all x1, blocking collectives, body(): lax.all_to_all(jnp.broadcast_to(rows[None], (NT // 2,) + rows.shape), 'ch...  31.3 us
    ppermute x3, waiting for transfers between devices, spread(): lax.ppermute(parts[m], COL, [(h, column_of(m, landing[m][h])) for h in (0...  17.4 us
    ppermute x7, starting transfers between devices, spread(): got[d] = lax.ppermute(piece, COL, pairs)  14.9 us
    ppermute x7, waiting for transfers between devices, spread(): got[d] = lax.ppermute(piece, COL, pairs)  11.6 us
    all_gather x1, blocking collectives, body(): both = lax.all_gather(both, 'xhi', axis=0, tiled=True)  8.93 us
    pallas_call x1, Pallas kernels, update(): pl.pallas_call(update_kernel, out_shape=[jax.ShapeDtypeStruct((height, wi...  8.62 us
    another operation x4, other arithmetic, whole(): jnp.stack([jnp.where(lower, own, far), jnp.where(lower, far, own)], axis=1)  4.74 us
  transfers between devices with their start and end apart: 13, of which 5 were waited for; matrix products, arithmetic and copies ran while one was open for 5% of the time, Pallas kernels for 0%

profile of v13, /device:TPU:398, one launch (start us, length us, event | category | flops | bytes accessed | tf_op | source)
XLA Modules:
  0.0 163.9 jit_solution(935397946854672053)
XLA Ops:
  7.2 1.0 pad_maximum_fusion.3
  8.2 8.9 %all_gather.6 = bf16[192,1024]{1,0:T(8,128)(2,1)} all-gather(bf16[96,1024]{1,0:T(8,128)(2,1)S(1)} %pad_maximum_fusion.3), channel_id=1, replica_groups=mesh['chip'=8,'core'=2,'xhi'=2,'z'=16] {'xhi'}, dimensions={0}, use_global_device_ids=true | all-gather | bytes 589824 | tf_op jit(solution)/shard_map/all_gather | solution.py:149
  17.1 2.9 %collective-permute-start = (bf16[96,512]{1,0:T(8,128)(2,1)}, bf16[96,512]{1,0:T(8,128)(2,1)S(1)}, u32[]{:S(2)}, u32[]{:S(2)}) collective-permute-start(bf16[96,512]{1,0:T(8,128)(2,1)} %param.10), channel_id=1, source_target_pairs={{0,1},{1,0},{2,3},{3,2},{4,5},{5,4},{6,7},{7,6},{8,9},{9,8},{10,11... | collective-permute-start | bytes 294920 | tf_op jit(solution)/shard_map/ppermute | solution.py:150
  20.1 3.8 %collective-permute-done = bf16[96,512]{1,0:T(8,128)(2,1)S(1)} collective-permute-done((bf16[96,512]{1,0:T(8,128)(2,1)}, bf16[96,512]{1,0:T(8,128)(2,1)S(1)}, u32[]{:S(2)}, u32[]{:S(2)}) %collective-permute-start) | collective-permute-done | bytes 98336 | tf_op jit(solution)/shard_map/ppermute | solution.py:150
  23.9 0.9 broadcast_select_fusion.1
  24.8 0.9 pad_maximum_fusion.2
  25.7 0.2 broadcast_in_dim.2
  25.9 31.3 %all_to_all.5 = bf16[8,96,1536]{2,1,0:T(8,128)(2,1)S(1)} all-to-all(bf16[8,96,1536]{2,1,0:T(8,128)(2,1)S(1)} %broadcast_in_dim.2), channel_id=1, replica_groups=mesh['chip'=8,'core'=2,'xhi'=2,'z'=16] {'chip'}, dimensions={0} | all-to-all | bytes 4718592 | tf_op jit(solution)/shard_map/all_to_all | solution.py:158
  57.2 1.9 %collective-permute-start.1 = (bf16[8,96,1536]{2,1,0:T(8,128)(2,1)S(1)}, bf16[8,96,1536]{2,1,0:T(8,128)(2,1)}, u32[]{:S(2)}, u32[]{:S(2)}) collective-permute-start(bf16[8,96,1536]{2,1,0:T(8,128)(2,1)S(1)} %all_to_all.5), channel_id=1, source_target_pairs={{0,32},{32,0},{1,33},{33,1},{2,34},{34,2},{3,35},{35,3},{4,36},{36... | collective-permute-start | bytes 7077896 | tf_op jit(solution)/shard_map/ppermute | solution.py:159
  59.1 0.2 dynamic-slice_reduce_fusion.upper_ref
  59.3 0.7 fusion.left_ref
  60.0 3.7 %collective-permute-done.1 = bf16[8,96,1536]{2,1,0:T(8,128)(2,1)} collective-permute-done((bf16[8,96,1536]{2,1,0:T(8,128)(2,1)S(1)}, bf16[8,96,1536]{2,1,0:T(8,128)(2,1)}, u32[]{:S(2)}, u32[]{:S(2)}) %collective-permute-start.1) | collective-permute-done | bytes 2359328 | tf_op jit(solution)/shard_map/ppermute | solution.py:159
  63.7 1.6 %select_bitcast_fusion.1 = (bf16[8,1,96,1024]{3,2,0,1:T(8,128)(2,1)S(1)}, bf16[8,1,96,1024]{3,2,0,1:T(8,128)(2,1)S(1)}) fusion(pred[]{:T(512)S(6)} %eq.80, bf16[8,96,1536]{2,1,0:T(8,128)(2,1)} %collective-permute-done.1, bf16[8,96,1536]{2,1,0:T(8,128)(2,1)S(1)} %all_to_all.5), kind=kLoop, calls=%fused_computation.3 | loop fusion | flops 1572864 | bytes 6291457 | tf_op jit(solution)/shard_map/stack | solution.py:163
  65.4 0.3 pad_maximum_fusion
  65.7 0.3 copy.11
  66.0 1.5 select_bitcast_fusion.3
  67.5 1.3 pad_maximum_fusion.1
  68.8 31.9 %all-gather.2.cloned.1.call-done = bf16[3072,1024]{1,0:T(8,128)(2,1)} async-done(((bf16[192,1024]{1,0:T(8,128)(2,1)}), bf16[3072,1024]{1,0:T(8,128)(2,1)}) %all-gather.2.cloned.1.call-update) | async-done | bytes 6291472 | tf_op jit(solution)/shard_map/all_gather | solution.py:151
  100.7 8.6 %shard_map.86 = (bf16[1024,512]{1,0:T(8,128)(2,1)}, bf16[256,512]{1,0:T(8,128)(2,1)S(1)}, bf16[256,512]{1,0:T(8,128)(2,1)}, bf16[256,512]{1,0:T(8,128)(2,1)}, bf16[256,512]{1,0:T(8,128)(2,1)}) custom-call(s32[16]{0:T(128)S(1)} %fusion.left_ref, s32[16]{0:T(128)S(1)} %dynamic-slice_reduce_fusion.upper_ref, bf16[16,2,2,48,1024]{4,3,2,1,0:T(8,128)(2,1)} %bitcast.16, ...), custom_call_target="tpu_custom_call" | custom-call | tf_op jit(solution)/shard_map/pallas_call | solution.py:124
  109.3 0.7 collective-permute-start.2
  110.0 0.7 collective-permute-start.3
  110.7 1.3 collective-permute-start.4
  112.2 17.4 %collective-permute-done.4 = bf16[256,512]{1,0:T(8,128)(2,1)S(1)} collective-permute-done((bf16[256,512]{1,0:T(8,128)(2,1)}, bf16[256,512]{1,0:T(8,128)(2,1)S(1)}, u32[]{:S(2)}, u32[]{:S(2)}) %collective-permute-start.4) | collective-permute-done | bytes 262176 | tf_op jit(solution)/shard_map/ppermute | solution.py:37
  129.7 1.3 collective-permute-start.10
  130.9 1.3 collective-permute-start.11
  132.2 1.3 collective-permute-start.5
  133.5 1.3 collective-permute-start.6
  134.8 1.3 collective-permute-start.7
  136.2 6.5 %collective-permute-start.8 = (bf16[32,512]{1,0:T(8,128)(2,1)S(1)}, bf16[32,512]{1,0:T(8,128)(2,1)S(1)}, u32[]{:S(2)}, u32[]{:S(2)}) collective-permute-start(bf16[32,512]{1,0:T(8,128)(2,1)S(1)} %get-tuple-element.19), channel_id=1, source_target_pairs={{0,1},{1,2},{12,5},{5,6},{16,17},{17,18},{28,21},{21,22},{32,33},{... | collective-permute-start | bytes 98312 | tf_op jit(solution)/shard_map/ppermute | solution.py:44
  142.7 1.9 %collective-permute-start.9 = (bf16[32,512]{1,0:T(8,128)(2,1)S(1)}, bf16[32,512]{1,0:T(8,128)(2,1)S(1)}, u32[]{:S(2)}, u32[]{:S(2)}) collective-permute-start(bf16[32,512]{1,0:T(8,128)(2,1)S(1)} %get-tuple-element.18), channel_id=1, source_target_pairs={{0,15},{1,0},{12,11},{5,12},{16,31},{17,16},{28,27},{21,28},{32,47... | collective-permute-start | bytes 98312 | tf_op jit(solution)/shard_map/ppermute | solution.py:44
  144.7 11.6 %collective-permute-done.9 = bf16[32,512]{1,0:T(8,128)(2,1)S(1)} collective-permute-done((bf16[32,512]{1,0:T(8,128)(2,1)S(1)}, bf16[32,512]{1,0:T(8,128)(2,1)S(1)}, u32[]{:S(2)}, u32[]{:S(2)}) %collective-permute-start.9) | collective-permute-done | bytes 32800 | tf_op jit(solution)/shard_map/ppermute | solution.py:44
  156.4 0.6 pad_maximum_fusion.4
  (18 shorter events, 0.3 us)
Async XLA Ops:
  7.2 52.0 %copy-start = (s32[16,16]{1,0:T(8,128)S(1)}, s32[16,16]{1,0:T(8,128)}, u32[]{:S(2)}) copy-start(s32[16,16]{1,0:T(8,128)} %param.13) | copy-start | bytes 3076
  7.2 93.5 %all-gather.2.cloned.1.call-start = ((), (), s32[]{:S(2)}) async-start(), calls=%async_computation.1 | async-start | bytes 6684672 | tf_op jit(solution)/shard_map/all_gather | solution.py:151
  17.1 6.7 %collective-permute-start = (bf16[96,512]{1,0:T(8,128)(2,1)}, bf16[96,512]{1,0:T(8,128)(2,1)S(1)}, u32[]{:S(2)}, u32[]{:S(2)}) collective-permute-start(bf16[96,512]{1,0:T(8,128)(2,1)} %param.10), channel_id=1, source_target_pairs={{0,1},{1,0},{2,3},{3,2},{4,5},{5,4},{6,7},{7,6},{8,9},{9,8},{10,11... | collective-permute-start | bytes 294920 | tf_op jit(solution)/shard_map/ppermute | solution.py:150
  57.2 8.2 %copy-start.1 = (bf16[8,96,1536]{2,1,0:T(8,128)(2,1)}, bf16[8,96,1536]{2,1,0:T(8,128)(2,1)S(1)}, u32[]{:S(2)}) copy-start(bf16[8,96,1536]{2,1,0:T(8,128)(2,1)S(1)} %all_to_all.5) | copy-start | bytes 7077892
  57.2 6.5 %collective-permute-start.1 = (bf16[8,96,1536]{2,1,0:T(8,128)(2,1)S(1)}, bf16[8,96,1536]{2,1,0:T(8,128)(2,1)}, u32[]{:S(2)}, u32[]{:S(2)}) collective-permute-start(bf16[8,96,1536]{2,1,0:T(8,128)(2,1)S(1)} %all_to_all.5), channel_id=1, source_target_pairs={{0,32},{32,0},{1,33},{33,1},{2,34},{34,2},{3,35},{35,3},{4,36},{36... | collective-permute-start | bytes 7077896 | tf_op jit(solution)/shard_map/ppermute | solution.py:159
  109.3 2.9 %collective-permute-start.2 = (bf16[256,512]{1,0:T(8,128)(2,1)}, bf16[256,512]{1,0:T(8,128)(2,1)S(1)}, u32[]{:S(2)}, u32[]{:S(2)}) collective-permute-start(bf16[256,512]{1,0:T(8,128)(2,1)} %get-tuple-element.8), channel_id=1, source_target_pairs={{0,12},{1,5},{32,44},{33,37},{64,76},{65,69},{96,108},{97,101},{12... | collective-permute-start | bytes 786440 | tf_op jit(solution)/shard_map/ppermute | solution.py:37
  110.0 2.2 %collective-permute-start.3 = (bf16[256,512]{1,0:T(8,128)(2,1)}, bf16[256,512]{1,0:T(8,128)(2,1)S(1)}, u32[]{:S(2)}, u32[]{:S(2)}) collective-permute-start(bf16[256,512]{1,0:T(8,128)(2,1)} %get-tuple-element.9), channel_id=1, source_target_pairs={{0,16},{1,17},{32,48},{33,49},{64,80},{65,81},{96,112},{97,113},{1... | collective-permute-start | bytes 786440 | tf_op jit(solution)/shard_map/ppermute | solution.py:37
  110.7 18.9 %collective-permute-start.4 = (bf16[256,512]{1,0:T(8,128)(2,1)}, bf16[256,512]{1,0:T(8,128)(2,1)S(1)}, u32[]{:S(2)}, u32[]{:S(2)}) collective-permute-start(bf16[256,512]{1,0:T(8,128)(2,1)} %get-tuple-element.10), channel_id=1, source_target_pairs={{0,28},{1,21},{32,60},{33,53},{64,92},{65,85},{96,124},{97,117},{1... | collective-permute-start | bytes 786440 | tf_op jit(solution)/shard_map/ppermute | solution.py:37
  129.7 6.5 %collective-permute-start.10 = (bf16[32,512]{1,0:T(8,128)(2,1)S(1)}, bf16[32,512]{1,0:T(8,128)(2,1)S(1)}, u32[]{:S(2)}, u32[]{:S(2)}) collective-permute-start(bf16[32,512]{1,0:T(8,128)(2,1)S(1)} %get-tuple-element.17), channel_id=1, source_target_pairs={{0,2},{1,3},{12,6},{5,7},{16,18},{17,19},{28,22},{21,23},{32,34},{... | collective-permute-start | bytes 98312 | tf_op jit(solution)/shard_map/ppermute | solution.py:44
  130.9 11.7 %collective-permute-start.11 = (bf16[32,512]{1,0:T(8,128)(2,1)S(1)}, bf16[32,512]{1,0:T(8,128)(2,1)S(1)}, u32[]{:S(2)}, u32[]{:S(2)}) collective-permute-start(bf16[32,512]{1,0:T(8,128)(2,1)S(1)} %get-tuple-element.16), channel_id=1, source_target_pairs={{0,3},{1,4},{12,7},{5,8},{16,19},{17,20},{28,23},{21,24},{32,35},{... | collective-permute-start | bytes 98312 | tf_op jit(solution)/shard_map/ppermute | solution.py:44
  132.2 12.4 %collective-permute-start.5 = (bf16[32,512]{1,0:T(8,128)(2,1)S(1)}, bf16[32,512]{1,0:T(8,128)(2,1)S(1)}, u32[]{:S(2)}, u32[]{:S(2)}) collective-permute-start(bf16[32,512]{1,0:T(8,128)(2,1)S(1)} %get-tuple-element.22), channel_id=1, source_target_pairs={{0,4},{1,13},{12,8},{5,9},{16,20},{17,29},{28,24},{21,25},{32,36},... | collective-permute-start | bytes 98312 | tf_op jit(solution)/shard_map/ppermute | solution.py:44
  133.5 11.1 %collective-permute-start.6 = (bf16[32,512]{1,0:T(8,128)(2,1)S(1)}, bf16[32,512]{1,0:T(8,128)(2,1)S(1)}, u32[]{:S(2)}, u32[]{:S(2)}) collective-permute-start(bf16[32,512]{1,0:T(8,128)(2,1)S(1)} %get-tuple-element.21), channel_id=1, source_target_pairs={{0,13},{1,14},{12,9},{5,10},{16,29},{17,30},{28,25},{21,26},{32,45... | collective-permute-start | bytes 98312 | tf_op jit(solution)/shard_map/ppermute | solution.py:44
  134.8 9.9 %collective-permute-start.7 = (bf16[32,512]{1,0:T(8,128)(2,1)S(1)}, bf16[32,512]{1,0:T(8,128)(2,1)S(1)}, u32[]{:S(2)}, u32[]{:S(2)}) collective-permute-start(bf16[32,512]{1,0:T(8,128)(2,1)S(1)} %get-tuple-element.20), channel_id=1, source_target_pairs={{0,14},{1,15},{12,10},{5,11},{16,30},{17,31},{28,26},{21,27},{32,4... | collective-permute-start | bytes 98312 | tf_op jit(solution)/shard_map/ppermute | solution.py:44
  136.2 8.6 %collective-permute-start.8 = (bf16[32,512]{1,0:T(8,128)(2,1)S(1)}, bf16[32,512]{1,0:T(8,128)(2,1)S(1)}, u32[]{:S(2)}, u32[]{:S(2)}) collective-permute-start(bf16[32,512]{1,0:T(8,128)(2,1)S(1)} %get-tuple-element.19), channel_id=1, source_target_pairs={{0,1},{1,2},{12,5},{5,6},{16,17},{17,18},{28,21},{21,22},{32,33},{... | collective-permute-start | bytes 98312 | tf_op jit(solution)/shard_map/ppermute | solution.py:44
  142.7 13.6 %collective-permute-start.9 = (bf16[32,512]{1,0:T(8,128)(2,1)S(1)}, bf16[32,512]{1,0:T(8,128)(2,1)S(1)}, u32[]{:S(2)}, u32[]{:S(2)}) collective-permute-start(bf16[32,512]{1,0:T(8,128)(2,1)S(1)} %get-tuple-element.18), channel_id=1, source_target_pairs={{0,15},{1,0},{12,11},{5,12},{16,31},{17,16},{28,27},{21,28},{32,47... | collective-permute-start | bytes 98312 | tf_op jit(solution)/shard_map/ppermute | solution.py:44
Sparse Core Ops, SparseCore 0:
  17.3 83.3 all-gather.1
